TPU v7x, 512 devices: a whole 4x4x16 slice. The times are simulated.
512 devices in a mesh: tm: 64 (over x_lo, z, core), head: 8 (over x_hi, y).
Axes of the slice: x: 4 (x_hi: 2, x_lo: 2; x = x_hi * 2 + x_lo), y: 4, z: 16, core: 2. Of those that a mesh axis runs over, the one named last changes fastest.
Arguments:
- frames: bfloat16 [16384, 1280], P('tm', 'head'), may hold values from -6 to 6
- segment_ids: int32 [16384], replicated, may hold values from 0 to 127, never falling along the last dimension, each value on 1 to 256 neighbouring positions
- ln_gain: float32 [1280], replicated, may hold values from 0.5 to 1.5
- ln_bias: float32 [1280], replicated, may hold values from -1.5 to 1.5
- qkv_weight: bfloat16 [3, 1280, 1024], P(None, None, 'head'), may hold values from -3 to 3
- out_weight: bfloat16 [1024, 1280], P(None, 'head'), may hold values from -0.1875 to 0.1875
- out_bias: float32 [1280], P('head'), may hold values from -2.5 to 2.5
- adapter: bfloat16 [1280, 2560], P('head'), may hold values from -0.15625 to 0.15625
- rms_gain: float32 [2560], replicated, may hold values from 0.25 to 1.75
- x_weight: bfloat16 [2560, 2560], P(None, 'head'), may hold values from -0.125 to 0.125
- bc_weight: bfloat16 [2560, 256], P(None, 'head'), may hold values from -0.125 to 0.125
- decay: float32 [4096, 40], P('tm', 'head'), may hold values from 0 to 1
- skip_gain: float32 [40], P('head'), may hold values from 0.5 to 1.5
Outputs:
- encoded: bfloat16 [16384, 1280], P('tm', 'head')
- mixed: bfloat16 [4096, 2560], P('tm', 'head')
Inputs may be any that keep to these rules, and one draw needn't show every extreme that they name: `segment_ids`: segment numbers never fall along the frames; each segment holds 1 to 256 frames and one holds exactly 256.
All inputs are finite; a program needn't handle non-finite values.
Results may differ from a plain program's by a relative error of at most 0.008.
Values may be sent and summed in bfloat16 or wider, within the bound.
No kernel may reach another device: no remote copies, remote signals or barrier semaphores. Data moves between devices by JAX's collectives and lax.ppermute only.
A program may use at most 64 MiB of HBM per device.

v0:
```python
import math

import jax
import jax.numpy as jnp
from jax import lax
from jax.sharding import PartitionSpec as P

EHEAD_DIM = 64
HDIM = 64
NSTATE = 128
WINDOW = 256


EPSILON = 1e-05
HIGHEST = lax.Precision.HIGHEST


def with_halo(block, sides, width):
    for axis, dim in sides:
        count = lax.axis_size(axis)
        forward = [(i, i + 1) for i in range(count - 1)]
        backward = [(target, source) for source, target in forward]
        low = lax.ppermute(
            lax.slice_in_dim(block, block.shape[dim] - width, None, axis=dim), axis, forward
        )
        high = lax.ppermute(lax.slice_in_dim(block, 0, width, axis=dim), axis, backward)
        block = jnp.concatenate([low, block, high], axis=dim)
    return block


def prefix(part, axis, combine, identity):
    place = lax.axis_index(axis)
    gathered = jax.tree.map(lambda a: lax.all_gather(a, axis), part)
    state = jax.tree.map(lambda a, e: jnp.zeros_like(a) + jnp.asarray(e, a.dtype), part, identity)

    def one(hop, state):
        return combine(
            state, jax.tree.map(lambda a: lax.dynamic_index_in_dim(a, hop, 0, False), gathered)
        )

    return lax.fori_loop(0, place, one, state)


def layer_norm(values, gain, offset):
    center_mean = jnp.mean(values, axis=-1, keepdims=True)
    spread = jnp.mean(jnp.square(values - center_mean), axis=-1, keepdims=True)
    return (values - center_mean) * lax.rsqrt(spread + EPSILON) * gain + offset


def block_terms(inputs, b_in, c_in, decay):
    log_decay = jnp.log(decay)
    cumulative = jnp.cumsum(log_decay, axis=0)
    length = inputs.shape[0]
    sequence_indices = jnp.arange(length, dtype=jnp.int32)
    causal = sequence_indices[:, None] >= sequence_indices[None, :]
    log_gap = cumulative[:, None, :] - cumulative[None, :, :]
    weights = jnp.exp(jnp.where(causal[:, :, None], log_gap, -1e30))
    driven = inputs * (1.0 - decay)[:, :, None]
    affinity = jnp.dot(c_in, b_in.T, preferred_element_type=jnp.float32)
    within = jnp.einsum("tsh,shp->thp", affinity[:, :, None] * weights, driven, precision=HIGHEST)
    tail_decay = jnp.exp(cumulative[-1][None, :] - cumulative)
    end_state = jnp.einsum(
        "sh,shp,sn->hpn", tail_decay, driven, b_in.astype(jnp.float32), precision=HIGHEST
    )
    return (within, jnp.exp(cumulative), jnp.exp(cumulative[-1]), end_state)


def combine_states(earlier, later):
    return (earlier[0] * later[0], later[0][:, None, None] * earlier[1] + later[1])


def per_device(
    frames,
    segment_ids,
    ln_gain,
    ln_bias,
    qkv_weight,
    out_weight,
    out_bias,
    adapter,
    rms_gain,
    x_weight,
    bc_weight,
    decay,
    skip_gain,
):
    frame_count = frames.shape[0]
    margin = WINDOW
    tm_slot = lax.axis_index("tm")
    gathered = lax.all_gather(frames, "head", axis=1, tiled=True)
    normed = layer_norm(gathered.astype(jnp.float32), ln_gain, ln_bias).astype(jnp.bfloat16)
    queries = jnp.dot(normed, qkv_weight[0], preferred_element_type=jnp.float32).astype(
        jnp.bfloat16
    )
    keys_own = jnp.dot(normed, qkv_weight[1], preferred_element_type=jnp.float32).astype(
        jnp.bfloat16
    )
    values_own = jnp.dot(normed, qkv_weight[2], preferred_element_type=jnp.float32).astype(
        jnp.bfloat16
    )
    joined = jnp.concatenate([keys_own, values_own], axis=1)
    extended = with_halo(joined, (("tm", 0),), margin)
    head_width = keys_own.shape[1]
    keys_ext = extended[:, :head_width]
    values_ext = extended[:, head_width:]
    ids_pad = jnp.pad(segment_ids, (margin, margin), constant_values=-1)
    local_ids = lax.dynamic_slice_in_dim(
        ids_pad, tm_slot * frame_count, frame_count + 2 * margin, 0
    )
    heads_dev = queries.shape[1] // EHEAD_DIM
    qblock = math.gcd(frame_count, 512)
    span_rows = qblock + 2 * margin

    def attend(block_index):
        begin = block_index * qblock
        query_rows = queries.reshape(qblock, heads_dev, EHEAD_DIM)
        key_rows = keys_ext.reshape(span_rows, heads_dev, EHEAD_DIM)
        value_rows = values_ext.reshape(span_rows, heads_dev, EHEAD_DIM)
        query_ids = lax.dynamic_slice_in_dim(local_ids, begin + margin, qblock, 0)
        scores = jnp.einsum(
            "qhe,khe->hqk", query_rows, key_rows, preferred_element_type=jnp.float32
        ) * EHEAD_DIM ** (-0.5)
        allowed = query_ids[:, None] == local_ids[None, :]
        scores = jnp.where(allowed[None], scores, -1e30)
        peak = jnp.max(scores, axis=-1, keepdims=True)
        raised = jnp.exp(scores - peak)
        probs = (raised / jnp.sum(raised, axis=-1, keepdims=True)).astype(jnp.bfloat16)
        blended = jnp.einsum("hqk,khe->qhe", probs, value_rows, preferred_element_type=jnp.float32)
        return blended.astype(jnp.bfloat16).reshape(qblock, heads_dev * EHEAD_DIM)

    attended = lax.map(attend, jnp.arange(frame_count // qblock, dtype=jnp.int32)).reshape(
        frame_count, heads_dev * EHEAD_DIM
    )
    attention = jnp.dot(
        lax.all_gather(attended, "head", axis=1, tiled=True),
        out_weight,
        preferred_element_type=jnp.float32,
    )
    encoded = (frames.astype(jnp.float32) + attention + out_bias).astype(jnp.bfloat16)
    pooled = jnp.mean(
        encoded.astype(jnp.float32).reshape(frame_count // 4, 4, encoded.shape[1]), axis=1
    ).astype(jnp.bfloat16)
    partial_sum = jnp.dot(pooled, adapter, preferred_element_type=jnp.float32)
    projected = lax.psum(partial_sum, "head")
    scaled = (
        projected
        * lax.rsqrt(jnp.mean(jnp.square(projected), axis=1, keepdims=True) + EPSILON)
        * rms_gain
    ).astype(jnp.bfloat16)
    inputs = jax.nn.silu(jnp.dot(scaled, x_weight, preferred_element_type=jnp.float32)).astype(
        jnp.bfloat16
    )
    coupler_part = jax.nn.silu(
        jnp.dot(scaled, bc_weight, preferred_element_type=jnp.float32)
    ).astype(jnp.bfloat16)
    couplers = lax.all_gather(coupler_part, "head", axis=1, tiled=True)
    token_count = inputs.shape[0]
    state_heads = inputs.shape[1] // HDIM
    inputs_wide = inputs.astype(jnp.float32).reshape(token_count, state_heads, HDIM)
    c_rows = couplers[:, NSTATE:]
    within, growth, total_decay, end_state = block_terms(
        inputs_wide, couplers[:, :NSTATE], c_rows, decay
    )
    identity = (jnp.ones_like(total_decay), jnp.zeros_like(end_state))
    incoming = prefix((total_decay, end_state), "tm", combine_states, identity)
    from_state = jnp.einsum(
        "tn,hpn->thp", c_rows.astype(jnp.float32), incoming[1], precision=HIGHEST
    )
    result_rows = within + growth[:, :, None] * from_state + skip_gain[None, :, None] * inputs_wide
    mixed = result_rows.astype(jnp.bfloat16).reshape(token_count, state_heads * HDIM)
    return (encoded, mixed)


def solution(mesh):
    placed = (
        P("tm", "head"),
        P(),
        P(),
        P(),
        P(None, None, "head"),
        P(None, "head"),
        P("head"),
        P("head", None),
        P(),
        P(None, "head"),
        P(None, "head"),
        P("tm", "head"),
        P("head"),
    )
    return jax.shard_map(
        per_device,
        mesh=mesh,
        in_specs=placed,
        out_specs=(P("tm", "head"), P("tm", "head")),
        check_vma=False,
    )
```

profile of v0, /device:TPU:483, one launch (start us, length us, event | category | flops | bytes accessed | tf_op | source)
XLA Modules:
  0.0 432.9 jit_solution(7128152274875315925)
XLA Ops:
  7.3 29.6 %all_gather.19 = bf16[256,1280]{0,1:T(8,128)(2,1)S(1)} all-gather(bf16[256,160]{0,1:T(8,128)(2,1)} %param.15), channel_id=1, replica_groups=mesh['tm'=64,'head'=8] {'head'}, dimensions={1}, use_global_device_ids=true | all-gather | bytes 737280 | tf_op jit(solution)/shard_map/all_gather | solution.py:90
  38.4 8.7 %collective-permute-start.1 = (bf16[256,256]{0,1:T(8,128)(2,1)S(1)}, bf16[256,256]{0,1:T(8,128)(2,1)S(1)}, u32[]{:S(2)}, u32[]{:S(2)}) collective-permute-start(bf16[256,256]{0,1:T(8,128)(2,1)S(1)} %pad_maximum_fusion.1), channel_id=1, source_target_pairs={{8,0},{16,8},{24,16},{32,24},{40,32},{48,40},{56,48},{64,56},{72,6... | collective-permute-start | bytes 393224 | tf_op jit(solution)/shard_map/ppermute | solution.py:26
  47.1 1.3 collective-permute-start
  49.1 1.2 collective-permute-done
  52.2 29.1 %all_gather.20 = bf16[256,1024]{0,1:T(8,128)(2,1)S(1)} all-gather(bf16[256,128]{0,1:T(8,128)(2,1)S(1)} %bitcast.65), channel_id=1, replica_groups=mesh['tm'=64,'head'=8] {'head'}, dimensions={1}, use_global_device_ids=true | all-gather | bytes 589824 | tf_op jit(solution)/shard_map/all_gather | solution.py:135
  82.1 1.1 fusion.37
  83.6 103.0 %all-reduce.3.cloned.1.call-done = f32[64,2560]{1,0:T(8,128)} async-done(((f32[64,2560]{1,0:T(8,128)}), f32[64,2560]{1,0:T(8,128)}) %all-reduce.3.cloned.1.call-update) | async-done | bytes 655376 | tf_op jit(solution)/shard_map/psum | solution.py:144
  186.6 1.3 multiply_reduce_fusion
  188.0 1.4 multiply_convert_fusion.4
  189.4 28.0 %all_gather.21 = bf16[64,256]{0,1:T(8,128)(2,1)S(1)} all-gather(bf16[64,32]{0,1:T(8,128)(2,1)S(1)} %multiply_convert_fusion.4), channel_id=1, replica_groups=mesh['tm'=64,'head'=8] {'head'}, dimensions={1}, use_global_device_ids=true | all-gather | bytes 36864 | tf_op jit(solution)/shard_map/all_gather | solution.py:156
  219.2 71.0 %all-gather.1 = f32[64,1,5]{2,1,0:T(1,128)S(1)} all-gather(f32[1,1,5]{2,1,0:T(1,128)S(1)} %get-tuple-element.86), channel_id=1, replica_groups=mesh['tm'=64,'head'=8] {'tm'}, dimensions={0}, use_global_device_ids=true | all-gather | bytes 1300 | tf_op jit(solution)/shard_map/all_gather | solution.py:33
  290.4 67.9 %all-gather.4.cloned.1.call-done = f32[320,64,128]{2,1,0:T(8,128)} async-done(((f32[5,64,128]{2,1,0:T(8,128)}), f32[320,64,128]{2,1,0:T(8,128)}) %all-gather.4.cloned.1.call-update) | async-done | bytes 10485776 | tf_op jit(solution)/shard_map/all_gather | solution.py:33
  358.3 66.4 %while.3 = (s32[]{:T(128)}, f32[5,64,128]{2,1,0:T(8,128)S(1)}, s32[]{:T(128)}, f32[64,5]{1,0:T(8,128)S(1)}, f32[64,5,64,128]{3,2,1,0:T(8,128)}, /*index=5*/s32[]{:T(128)}, s32[]{:T(128)}, s32[]{:T(128)}) while((s32[]{:T(128)}, f32[5,64,128]{2,1,0:T(8,128)S(1)}, s32[]{:T(128)}, f32[64,5]{1,0:T(8,128)S(1)}, f32[64,5,64,128]{3,2,1,0:T(8,128)}, ...), condition=%wide.region_9.10_spmd, body=%wide.region_8.9_spmd.sunk | while | flops 81925 | bytes 491715 | solution.py:41
  358.3 1.0 bitcast_add_fusion.2
  359.4 1.0 bitcast_add_fusion.2
  360.5 1.0 bitcast_add_fusion.2
  362.6 1.0 bitcast_add_fusion.2
  363.6 1.0 bitcast_add_fusion.2
  364.7 1.0 bitcast_add_fusion.2
  365.7 1.0 bitcast_add_fusion.2
  366.8 1.0 bitcast_add_fusion.2
  367.8 1.0 bitcast_add_fusion.2
  368.9 1.0 bitcast_add_fusion.2
  369.9 1.0 bitcast_add_fusion.2
  372.0 1.0 bitcast_add_fusion.2
  373.1 1.0 bitcast_add_fusion.2
  374.1 1.0 bitcast_add_fusion.2
  375.2 1.0 bitcast_add_fusion.2
  376.3 1.0 bitcast_add_fusion.2
  377.3 1.0 bitcast_add_fusion.2
  378.4 1.0 bitcast_add_fusion.2
  379.4 1.0 bitcast_add_fusion.2
  380.5 1.0 bitcast_add_fusion.2
  382.6 1.0 bitcast_add_fusion.2
  383.6 1.0 bitcast_add_fusion.2
  384.7 1.0 bitcast_add_fusion.2
  385.7 1.0 bitcast_add_fusion.2
  386.8 1.0 bitcast_add_fusion.2
  387.8 1.0 bitcast_add_fusion.2
  388.9 1.0 bitcast_add_fusion.2
  389.9 1.0 bitcast_add_fusion.2
  392.1 1.0 bitcast_add_fusion.2
  393.1 1.0 bitcast_add_fusion.2
  394.2 1.0 bitcast_add_fusion.2
  395.2 1.0 bitcast_add_fusion.2
  396.3 1.0 bitcast_add_fusion.2
  397.3 1.0 bitcast_add_fusion.2
  398.4 1.0 bitcast_add_fusion.2
  (164 shorter events, 37.4 us)
Async XLA Ops:
  7.2 210.2 %copy-start = (bf16[2560,320]{0,1:T(8,128)(2,1)S(1)}, bf16[2560,320]{0,1:T(8,128)(2,1)}, u32[]{:S(2)}) copy-start(bf16[2560,320]{0,1:T(8,128)(2,1)} %param.24) | copy-start | bytes 4915204
  7.2 30.1 %copy-start.9 = (f32[1280]{0:T(1024)S(1)}, f32[1280]{0:T(1024)}, u32[]{:S(2)}) copy-start(f32[1280]{0:T(1024)} %param.18) | copy-start | bytes 15364
  7.2 30.1 %copy-start.10 = (f32[1280]{0:T(1024)S(1)}, f32[1280]{0:T(1024)}, u32[]{:S(2)}) copy-start(f32[1280]{0:T(1024)} %param.17) | copy-start | bytes 15364
  7.2 30.5 %copy-start.14 = (bf16[3,1280,128]{2,1,0:T(8,128)(2,1)S(1)}, bf16[3,1280,128]{2,1,0:T(8,128)(2,1)}, u32[]{:S(2)}) copy-start(bf16[3,1280,128]{2,1,0:T(8,128)(2,1)} %param.19) | copy-start | bytes 2949124
  7.2 179.4 %all-reduce.3.cloned.1.call-start = ((), (), s32[]{:S(2)}) async-start(), calls=%async_computation | async-start | bytes 1310720 | tf_op jit(solution)/shard_map/psum | solution.py:144
  38.1 10.7 %copy-start.6 = (s32[16384]{0:T(1024)S(1)}, s32[16384]{0:T(1024)}, u32[]{:S(2)}) copy-start(s32[16384]{0:T(1024)} %param.16) | copy-start | bytes 196612
  38.4 10.7 %collective-permute-start.1 = (bf16[256,256]{0,1:T(8,128)(2,1)S(1)}, bf16[256,256]{0,1:T(8,128)(2,1)S(1)}, u32[]{:S(2)}, u32[]{:S(2)}) collective-permute-start(bf16[256,256]{0,1:T(8,128)(2,1)S(1)} %pad_maximum_fusion.1), channel_id=1, source_target_pairs={{8,0},{16,8},{24,16},{32,24},{40,32},{48,40},{56,48},{64,56},{72,6... | collective-permute-start | bytes 393224 | tf_op jit(solution)/shard_map/ppermute | solution.py:26
  47.1 3.2 collective-permute-start
  51.2 30.2 %copy-start.4 = (bf16[1024,160]{0,1:T(8,128)(2,1)S(1)}, bf16[1024,160]{0,1:T(8,128)(2,1)}, u32[]{:S(2)}) copy-start(bf16[1024,160]{0,1:T(8,128)(2,1)} %param.20) | copy-start | bytes 983044
  51.2 30.2 %copy-start.5 = (bf16[256,160]{0,1:T(8,128)(2,1)S(1)}, bf16[256,160]{0,1:T(8,128)(2,1)}, u32[]{:S(2)}) copy-start(bf16[256,160]{0,1:T(8,128)(2,1)} %param.15) | copy-start | bytes 245764
  51.2 30.2 %copy-start.12 = (f32[160]{0:T(256)S(1)}, f32[160]{0:T(256)}, u32[]{:S(2)}) copy-start(f32[160]{0:T(256)} %param.21) | copy-start | bytes 1924
  52.2 29.8 %copy-start.2 = (bf16[160,2560]{1,0:T(8,128)(2,1)S(1)}, bf16[160,2560]{1,0:T(8,128)(2,1)}, u32[]{:S(2)}) copy-start(bf16[160,2560]{1,0:T(8,128)(2,1)} %param.22) | copy-start | bytes 2457604
  81.7 1.6 copy-start.3
  81.8 1.5 copy-start.11
  82.1 105.9 %copy-start.7 = (bf16[2560,32]{0,1:T(8,128)(2,1)S(1)}, bf16[2560,32]{0,1:T(8,128)(2,1)}, u32[]{:S(2)}) copy-start(bf16[2560,32]{0,1:T(8,128)(2,1)} %param.25) | copy-start | bytes 491524
  82.1 105.9 %copy-start.8 = (f32[2560]{0:T(1024)S(1)}, f32[2560]{0:T(1024)}, u32[]{:S(2)}) copy-start(f32[2560]{0:T(1024)} %param.23) | copy-start | bytes 30724
  83.2 275.1 %all-gather.4.cloned.1.call-start = ((), (), s32[]{:S(2)}) async-start(), calls=%async_computation.1 | async-start | bytes 10649600 | tf_op jit(solution)/shard_map/all_gather | solution.py:33
  186.6 30.8 %copy-start.1 = (f32[64,2560]{1,0:T(8,128)S(1)}, f32[64,2560]{1,0:T(8,128)}, u32[]{:S(2)}) copy-start(f32[64,2560]{1,0:T(8,128)} %all-reduce.3.cloned.1.call-done) | copy-start | bytes 1966084
  358.3 66.6 %copy-start.13 = (f32[5]{0:T(128)S(1)}, f32[5]{0:T(128)}, u32[]{:S(2)}) copy-start(f32[5]{0:T(128)} %param.27) | copy-start | bytes 64
Sparse Core Ops, SparseCore 0:
  83.3 103.2 all-reduce.2
  219.2 139.0 all-gather.3
where the time goes:
time: 435 us; the launch traced here: 433 us
  waiting for transfers between devices  172 us (40%)
  blocking collectives  158 us (36%)
  other arithmetic  66.5 us (15%)
  between operations  14.4 us (3%)
  starting transfers between devices  10.1 us (2%)
  matrix products  7.89 us (2%)
    psum x1, waiting for transfers between devices, per_device(): projected = lax.psum(partial_sum, 'head')  103 us
    all_gather x1, blocking collectives, prefix(): gathered = jax.tree.map(lambda a: lax.all_gather(a, axis), part)  71 us
    all_gather x1, waiting for transfers between devices, prefix(): gathered = jax.tree.map(lambda a: lax.all_gather(a, axis), part)  67.9 us
    add x63, other arithmetic, combine_states(): later[0][:, None, None] * earlier[1] + later[1]  63.8 us
    all_gather x1, blocking collectives, per_device(): gathered = lax.all_gather(frames, 'head', axis=1, tiled=True)  29.6 us
    all_gather x1, blocking collectives, per_device(): lax.all_gather(attended, 'head', axis=1, tiled=True)  29.1 us
    all_gather x1, blocking collectives, per_device(): couplers = lax.all_gather(coupler_part, 'head', axis=1, tiled=True)  28 us
  transfers between devices with their start and end apart: 4, of which 3 were waited for; matrix products, arithmetic and copies ran while one was open for 0% of the time, Pallas kernels for 0%

commit v1 on v0

v1 whole, which is shorter than its diff:
```python
import math

import jax
import jax.numpy as jnp
from jax import lax
from jax.sharding import PartitionSpec as P

EHEAD_DIM = 64
HDIM = 64
NSTATE = 128
WINDOW = 256
GROUP = 8

EPSILON = 1e-05
HIGHEST = lax.Precision.HIGHEST


def gather(block, axis, groups=None, count=None):
    count = lax.axis_size(axis) if count is None else count
    copies = jnp.broadcast_to(block[None], (count,) + block.shape)
    return lax.all_to_all(copies, axis, 0, 0, tiled=True, axis_index_groups=groups)


def halo(block):
    count = lax.axis_size("tm")
    forward = [(i, i + 1) for i in range(count - 1)]
    backward = [(i + 1, i) for i in range(count - 1)]
    return lax.ppermute(block, "tm", forward), lax.ppermute(block, "tm", backward)


def block_terms(inputs, b_in, c_in, decay):
    cumulative = jnp.cumsum(jnp.log(decay), axis=0)
    length = inputs.shape[0]
    places = jnp.arange(length, dtype=jnp.int32)
    causal = places[:, None] >= places[None, :]
    log_gap = cumulative[:, None, :] - cumulative[None, :, :]
    weights = jnp.exp(jnp.where(causal[:, :, None], log_gap, -1e30))
    driven = inputs * (1.0 - decay)[:, :, None]
    affinity = jnp.dot(c_in, b_in.T, preferred_element_type=jnp.float32)
    within = jnp.einsum("tsh,shp->thp", affinity[:, :, None] * weights, driven, precision=HIGHEST)
    tail_decay = jnp.exp(cumulative[-1][None, :] - cumulative)
    end_state = jnp.einsum(
        "sh,shp,sn->hpn", tail_decay, driven, b_in.astype(jnp.float32), precision=HIGHEST
    )
    return within, jnp.exp(cumulative), jnp.exp(cumulative[-1]), end_state


def state_before(total_decay, end_state):
    count = lax.axis_size("tm")
    place = lax.axis_index("tm")
    near = [[base + k for k in range(GROUP)] for base in range(0, count, GROUP)]
    far = [[lane + GROUP * k for k in range(count // GROUP)] for lane in range(GROUP)]
    heads, width, states = end_state.shape
    rows = heads * width
    share = rows // GROUP
    lane = place % GROUP
    head_rows = jnp.broadcast_to(
        jnp.pad(total_decay, (0, 8 - heads))[None, :, None], (GROUP, 8, states)
    )
    sent = jnp.concatenate([end_state.reshape(GROUP, share, states), head_rows], axis=1)
    got = lax.all_to_all(sent, "tm", 0, 0, tiled=True, axis_index_groups=near)
    row_head = (lane * share + jnp.arange(share, dtype=jnp.int32)) // width

    def spread(decays):
        out = jnp.zeros((share, states), jnp.float32)
        for h in range(heads):
            out = jnp.where((row_head == h)[:, None], decays[h][None, :], out)
        return out

    state = jnp.zeros((share, states), jnp.float32)
    grown = jnp.ones((8, states), jnp.float32)
    entering, kept = [], []
    for k in range(GROUP):
        entering.append(state)
        kept.append(spread(grown))
        state = spread(got[k, share:]) * state + got[k, :share]
        grown = grown * got[k, share:]
    totals = gather(jnp.concatenate([state, grown], axis=0), "tm", far, count // GROUP)
    before = jnp.zeros((share, states), jnp.float32)
    for k in range(count // GROUP):
        step = spread(totals[k, share:]) * before + totals[k, :share]
        before = jnp.where(k < place // GROUP, step, before)
    back = jnp.stack([entering[k] + kept[k] * before for k in range(GROUP)])
    mine = lax.all_to_all(back, "tm", 0, 0, tiled=True, axis_index_groups=near)
    return mine.reshape(heads, width, states)


def per_device(
    frames,
    segment_ids,
    ln_gain,
    ln_bias,
    qkv_weight,
    out_weight,
    out_bias,
    adapter,
    rms_gain,
    x_weight,
    bc_weight,
    decay,
    skip_gain,
):
    frame_count, share = frames.shape
    margin = WINDOW
    tm_slot = lax.axis_index("tm")
    head_count = lax.axis_size("head")
    gathered = gather(frames, "head").astype(jnp.float32)
    width = head_count * share
    center = jnp.sum(gathered, axis=(0, 2), keepdims=True) / width
    spread = jnp.sum(jnp.square(gathered - center), axis=(0, 2), keepdims=True) / width
    normed = (
        (gathered - center) * lax.rsqrt(spread + EPSILON) * ln_gain.reshape(head_count, 1, share)
        + ln_bias.reshape(head_count, 1, share)
    ).astype(jnp.bfloat16)

    def project(weight):
        parts = weight.reshape(head_count, share, weight.shape[1])
        return jnp.einsum(
            "jfc,jcn->fn", normed, parts, preferred_element_type=jnp.float32
        ).astype(jnp.bfloat16)

    keys_own = project(qkv_weight[1])
    values_own = project(qkv_weight[2])
    joined = jnp.concatenate([keys_own, values_own], axis=1)
    low, high = halo(joined)
    queries = project(qkv_weight[0])
    extended = jnp.concatenate([low, joined, high], axis=0)
    head_width = keys_own.shape[1]
    ids_pad = jnp.pad(segment_ids, (margin, margin), constant_values=-1)
    local_ids = lax.dynamic_slice_in_dim(
        ids_pad, tm_slot * frame_count, frame_count + 2 * margin, 0
    )
    heads_dev = head_width // EHEAD_DIM
    allowed = local_ids[margin : margin + frame_count, None] == local_ids[None, :]
    blended = []
    for h in range(heads_dev):
        cols = slice(h * EHEAD_DIM, (h + 1) * EHEAD_DIM)
        key_rows = extended[:, :head_width][:, cols]
        value_rows = extended[:, head_width:][:, cols]
        scores = jnp.einsum(
            "qe,ke->qk", queries[:, cols], key_rows, preferred_element_type=jnp.float32
        ) * EHEAD_DIM ** (-0.5)
        scores = jnp.where(allowed, scores, -1e30)
        raised = jnp.exp(scores - jnp.max(scores, axis=-1, keepdims=True))
        probs = (raised / jnp.sum(raised, axis=-1, keepdims=True)).astype(jnp.bfloat16)
        blended.append(jnp.dot(probs, value_rows, preferred_element_type=jnp.float32))
    attended = jnp.concatenate(blended, axis=1).astype(jnp.bfloat16)
    attention = jnp.einsum(
        "jfc,jcn->fn",
        gather(attended, "head"),
        out_weight.reshape(head_count, head_width, share),
        preferred_element_type=jnp.float32,
    )
    encoded = (frames.astype(jnp.float32) + attention + out_bias).astype(jnp.bfloat16)
    pooled = jnp.mean(
        encoded.astype(jnp.float32).reshape(frame_count // 4, 4, share), axis=1
    ).astype(jnp.bfloat16)
    partial = jnp.dot(pooled, adapter, preferred_element_type=jnp.float32)
    token_count, model = partial.shape
    chunks = partial.astype(jnp.bfloat16).reshape(head_count, token_count // head_count, model)
    parts = lax.all_to_all(chunks, "head", 0, 0, tiled=True)
    projected = jnp.sum(parts.astype(jnp.float32), axis=0)
    own = (
        projected
        * lax.rsqrt(jnp.mean(jnp.square(projected), axis=1, keepdims=True) + EPSILON)
        * rms_gain
    ).astype(jnp.bfloat16)
    scaled = gather(own, "head").reshape(token_count, model)
    coupler_part = jax.nn.silu(
        jnp.dot(scaled, bc_weight, preferred_element_type=jnp.float32)
    ).astype(jnp.bfloat16)
    couplers = gather(coupler_part, "head")
    couplers = jnp.concatenate([couplers[k] for k in range(head_count)], axis=1)
    inputs = jax.nn.silu(jnp.dot(scaled, x_weight, preferred_element_type=jnp.float32)).astype(
        jnp.bfloat16
    )
    state_heads = inputs.shape[1] // HDIM
    inputs_wide = inputs.astype(jnp.float32).reshape(token_count, state_heads, HDIM)
    c_rows = couplers[:, NSTATE:]
    within, growth, total_decay, end_state = block_terms(
        inputs_wide, couplers[:, :NSTATE], c_rows, decay
    )
    incoming = state_before(total_decay, end_state)
    from_state = jnp.einsum(
        "tn,hpn->thp", c_rows.astype(jnp.float32), incoming, precision=HIGHEST
    )
    result_rows = within + growth[:, :, None] * from_state + skip_gain[None, :, None] * inputs_wide
    mixed = result_rows.astype(jnp.bfloat16).reshape(token_count, state_heads * HDIM)
    return (encoded, mixed)


def solution(mesh):
    placed = (
        P("tm", "head"),
        P(),
        P(),
        P(),
        P(None, None, "head"),
        P(None, "head"),
        P("head"),
        P("head", None),
        P(),
        P(None, "head"),
        P(None, "head"),
        P("tm", "head"),
        P("head"),
    )
    return jax.shard_map(
        per_device,
        mesh=mesh,
        in_specs=placed,
        out_specs=(P("tm", "head"), P("tm", "head")),
        check_vma=False,
    )
```

time: 435 us -> 156 us (0.36)
  the two profiles are of different devices: /device:TPU:483 before, /device:TPU:1 now
where the time goes in v1:
time: 156 us; the launch traced here: 155 us
  waiting for transfers between devices  67.4 us (43%)
  starting transfers between devices  61.7 us (40%)
  local copies, waits for them, and re-layouts  9.01 us (6%)
  other arithmetic  8.62 us (6%)
  matrix products  6.74 us (4%)
    all_to_all x5, waiting for transfers between devices, gather(): lax.all_to_all(copies, axis, 0, 0, tiled=True, axis_index_groups=groups)  46.2 us
    all_to_all x5, starting transfers between devices, gather(): lax.all_to_all(copies, axis, 0, 0, tiled=True, axis_index_groups=groups)  30.6 us
    all_to_all x1, starting transfers between devices, state_before(): got = lax.all_to_all(sent, 'tm', 0, 0, tiled=True, axis_index_groups=near)  10.3 us
    all_to_all x1, waiting for transfers between devices, per_device(): parts = lax.all_to_all(chunks, 'head', 0, 0, tiled=True)  8.35 us
    all_to_all x1, starting transfers between devices, state_before(): mine = lax.all_to_all(back, 'tm', 0, 0, tiled=True, axis_index_groups=near)  8.21 us
    all_to_all x1, waiting for transfers between devices, state_before(): got = lax.all_to_all(sent, 'tm', 0, 0, tiled=True, axis_index_groups=near)  6.48 us
    ppermute x1, starting transfers between devices, halo(): lax.ppermute(block, 'tm', backward)  5.95 us
    all_to_all x1, waiting for transfers between devices, state_before(): mine = lax.all_to_all(back, 'tm', 0, 0, tiled=True, axis_index_groups=near)  5.25 us
  transfers between devices with their start and end apart: 10, of which 9 were waited for; matrix products, arithmetic and copies ran while one was open for 3% of the time, Pallas kernels for 0%

profile of v1, /device:TPU:1, one launch (start us, length us, event | category | flops | bytes accessed | tf_op | source)
XLA Modules:
  0.0 154.7 jit_solution(17832635931860921800)
XLA Ops:
  0.7 1.9 %broadcast_in_dim.1455 = bf16[8,256,160]{1,2,0:T(8,128)(2,1)} broadcast(bf16[256,160]{0,1:T(8,128)(2,1)} %param.13), dimensions={1,2} | broadcast | bytes 737280 | tf_op jit(solution)/shard_map/broadcast_in_dim | solution.py:20
  2.6 7.5 %all-to-all-start = ((bf16[8,256,160]{1,2,0:T(8,128)(2,1)}), bf16[8,256,160]{1,2,0:T(8,128)(2,1)S(1)}, u32[]{:S(2)}, u32[]{:S(2)}) async-start(bf16[8,256,160]{1,2,0:T(8,128)(2,1)} %broadcast_in_dim.1455), calls=%async_computation | async-start | bytes 1310720 | tf_op jit(solution)/shard_map/all_to_all | solution.py:21
  10.3 1.0 fusion.82
  11.4 8.1 %all-to-all-done = bf16[8,256,160]{1,2,0:T(8,128)(2,1)S(1)} async-done(((bf16[8,256,160]{1,2,0:T(8,128)(2,1)}), bf16[8,256,160]{1,2,0:T(8,128)(2,1)S(1)}, u32[]{:S(2)}, u32[]{:S(2)}) %all-to-all-start) | async-done | bytes 655392 | tf_op jit(solution)/shard_map/all_to_all | solution.py:21
  19.9 0.7 fusion.17
  20.9 0.7 fusion.16
  21.6 6.0 %collective-permute-start.1 = (bf16[256,256]{0,1:T(8,128)(2,1)S(1)}, bf16[256,256]{0,1:T(8,128)(2,1)S(1)}, u32[]{:S(2)}, u32[]{:S(2)}) collective-permute-start(bf16[256,256]{0,1:T(8,128)(2,1)S(1)} %pad_maximum_fusion.2), channel_id=1, source_target_pairs={{8,0},{16,8},{24,16},{32,24},{40,32},{48,40},{56,48},{64,56},{72,6... | collective-permute-start | bytes 393224 | tf_op jit(solution)/shard_map/ppermute | solution.py:28
  27.5 3.1 %collective-permute-start = (bf16[256,256]{0,1:T(8,128)(2,1)S(1)}, bf16[256,256]{0,1:T(8,128)(2,1)S(1)}, u32[]{:S(2)}, u32[]{:S(2)}) collective-permute-start(bf16[256,256]{0,1:T(8,128)(2,1)S(1)} %pad_maximum_fusion.2), channel_id=1, source_target_pairs={{0,8},{8,16},{16,24},{24,32},{32,40},{40,48},{48,56},{56,64},{64,7... | collective-permute-start | bytes 393224 | tf_op jit(solution)/shard_map/ppermute | solution.py:28
  30.6 0.7 fusion.15
  31.4 1.2 collective-permute-done
  32.6 0.4 fusion.85
  33.0 0.4 fusion.86
  33.3 0.3 fusion.19
  33.6 0.4 convolution_convert_fusion.1
  34.0 0.3 fusion.18
  34.3 0.4 convolution_convert_fusion.2
  34.9 0.9 broadcast_in_dim.1457
  35.7 3.5 %all-to-all-start.1 = ((bf16[8,256,128]{2,1,0:T(8,128)(2,1)}), bf16[8,256,128]{2,1,0:T(8,128)(2,1)S(1)}, u32[]{:S(2)}, u32[]{:S(2)}) async-start(bf16[8,256,128]{2,1,0:T(8,128)(2,1)} %broadcast_in_dim.1457), calls=%async_computation.1 | async-start | bytes 1048576 | tf_op jit(solution)/shard_map/all_to_all | solution.py:21
  39.5 10.6 %all-to-all-done.1 = bf16[8,256,128]{2,1,0:T(8,128)(2,1)S(1)} async-done(((bf16[8,256,128]{2,1,0:T(8,128)(2,1)}), bf16[8,256,128]{2,1,0:T(8,128)(2,1)S(1)}, u32[]{:S(2)}, u32[]{:S(2)}) %all-to-all-start.1) | async-done | bytes 524320 | tf_op jit(solution)/shard_map/all_to_all | solution.py:21
  50.1 0.3 fusion.13
  50.8 1.0 fusion
  51.8 3.6 %all-to-all-start.2 = ((bf16[8,8,2560]{2,1,0:T(8,128)(2,1)}), bf16[8,8,2560]{2,1,0:T(8,128)(2,1)S(1)}, u32[]{:S(2)}, u32[]{:S(2)}) async-start(bf16[8,8,2560]{2,1,0:T(8,128)(2,1)} %fusion), calls=%async_computation.2 | async-start | bytes 655360 | tf_op jit(solution)/shard_map/all_to_all | solution.py:161
  55.5 8.3 %all-to-all-done.2 = bf16[8,8,2560]{2,1,0:T(8,128)(2,1)S(1)} async-done(((bf16[8,8,2560]{2,1,0:T(8,128)(2,1)}), bf16[8,8,2560]{2,1,0:T(8,128)(2,1)S(1)}, u32[]{:S(2)}, u32[]{:S(2)}) %all-to-all-start.2) | async-done | bytes 327712 | tf_op jit(solution)/shard_map/all_to_all | solution.py:161
  64.1 0.8 broadcast_in_dim.1458
  64.9 3.9 %all-to-all-start.3 = ((bf16[8,8,2560]{2,1,0:T(8,128)(2,1)}), bf16[8,8,2560]{2,1,0:T(8,128)(2,1)S(1)}, u32[]{:S(2)}, u32[]{:S(2)}) async-start(bf16[8,8,2560]{2,1,0:T(8,128)(2,1)} %broadcast_in_dim.1458), calls=%async_computation.3 | async-start | bytes 655360 | tf_op jit(solution)/shard_map/all_to_all | solution.py:21
  68.9 7.8 %all-to-all-done.3 = bf16[8,8,2560]{2,1,0:T(8,128)(2,1)S(1)} async-done(((bf16[8,8,2560]{2,1,0:T(8,128)(2,1)}), bf16[8,8,2560]{2,1,0:T(8,128)(2,1)S(1)}, u32[]{:S(2)}, u32[]{:S(2)}) %all-to-all-start.3) | async-done | bytes 327712 | tf_op jit(solution)/shard_map/all_to_all | solution.py:21
  76.9 0.7 reshape.10530
  77.6 3.9 %all-to-all-start.4 = ((bf16[8,2,1024]{2,1,0:T(2,128)(2,1)}), bf16[8,2,1024]{2,1,0:T(2,128)(2,1)S(1)}, u32[]{:S(2)}, u32[]{:S(2)}) async-start(bf16[8,2,1024]{2,1,0:T(2,128)(2,1)} %reshape.10530), calls=%async_computation.4 | async-start | bytes 65536 | tf_op jit(solution)/shard_map/all_to_all | solution.py:21
  81.5 0.6 fusion.40
  82.2 5.9 %all-to-all-done.4 = bf16[8,2,1024]{2,1,0:T(2,128)(2,1)S(1)} async-done(((bf16[8,2,1024]{2,1,0:T(2,128)(2,1)}), bf16[8,2,1024]{2,1,0:T(2,128)(2,1)S(1)}, u32[]{:S(2)}, u32[]{:S(2)}) %all-to-all-start.4) | async-done | bytes 32800 | tf_op jit(solution)/shard_map/all_to_all | solution.py:21
  88.9 0.8 pad_maximum_fusion.1
  89.7 10.3 %all-to-all-start.5 = ((f32[8,48,128]{2,1,0:T(8,128)}), f32[8,48,128]{2,1,0:T(8,128)S(1)}, u32[]{:S(2)}, u32[]{:S(2)}) async-start(f32[8,48,128]{2,1,0:T(8,128)} %pad_maximum_fusion.1), calls=%async_computation.5 | async-start | bytes 393216 | tf_op jit(solution)/shard_map/all_to_all | solution.py:61
  100.1 6.5 %all-to-all-done.5 = f32[8,48,128]{2,1,0:T(8,128)S(1)} async-done(((f32[8,48,128]{2,1,0:T(8,128)}), f32[8,48,128]{2,1,0:T(8,128)S(1)}, u32[]{:S(2)}, u32[]{:S(2)}) %all-to-all-start.5) | async-done | bytes 196640 | tf_op jit(solution)/shard_map/all_to_all | solution.py:61
  106.8 0.7 broadcast_in_dim.1555
  107.5 11.9 %all-to-all-start.6 = ((f32[8,48,128]{2,1,0:T(8,128)}), f32[8,48,128]{2,1,0:T(8,128)S(1)}, u32[]{:S(2)}, u32[]{:S(2)}) async-start(f32[8,48,128]{2,1,0:T(8,128)} %broadcast_in_dim.1555), calls=%async_computation.6 | async-start | bytes 393216 | tf_op jit(solution)/shard_map/all_to_all | solution.py:21
  119.4 13.8 %all-to-all-done.6 = f32[8,48,128]{2,1,0:T(8,128)S(1)} async-done(((f32[8,48,128]{2,1,0:T(8,128)}), f32[8,48,128]{2,1,0:T(8,128)S(1)}, u32[]{:S(2)}, u32[]{:S(2)}) %all-to-all-start.6) | async-done | bytes 196640 | tf_op jit(solution)/shard_map/all_to_all | solution.py:21
  133.3 0.8 multiply_dynamic-update-slice_fusion
  134.1 0.7 add_dynamic-update-slice_fusion.6
  134.8 0.7 add_dynamic-update-slice_fusion.5
  135.5 0.7 add_dynamic-update-slice_fusion.4
  136.2 0.7 add_dynamic-update-slice_fusion.3
  136.9 0.7 add_dynamic-update-slice_fusion.2
  137.6 0.7 add_dynamic-update-slice_fusion.1
  138.3 0.7 add_dynamic-update-slice_fusion
  139.0 8.2 %all-to-all-start.7 = ((f32[8,40,128]{2,1,0:T(8,128)}), f32[8,40,128]{2,1,0:T(8,128)S(1)}, u32[]{:S(2)}, u32[]{:S(2)}) async-start(f32[8,40,128]{2,1,0:T(8,128)} %add_dynamic-update-slice_fusion), calls=%async_computation.7 | async-start | bytes 327680 | tf_op jit(solution)/shard_map/all_to_all | solution.py:84
  148.0 5.2 %all-to-all-done.7 = f32[8,40,128]{2,1,0:T(8,128)S(1)} async-done(((f32[8,40,128]{2,1,0:T(8,128)}), f32[8,40,128]{2,1,0:T(8,128)S(1)}, u32[]{:S(2)}, u32[]{:S(2)}) %all-to-all-start.7) | async-done | bytes 163872 | tf_op jit(solution)/shard_map/all_to_all | solution.py:84
  153.5 0.5 fusion.14
  154.0 0.7 copy.74
  (99 shorter events, 4.6 us)
Async XLA Ops:
  0.6 80.8 %copy-start = (bf16[2560,320]{0,1:T(8,128)(2,1)S(1)}, bf16[2560,320]{0,1:T(8,128)(2,1)}, u32[]{:S(2)}) copy-start(bf16[2560,320]{0,1:T(8,128)(2,1)} %param.22) | copy-start | bytes 4915204
  0.6 9.4 %copy-start.9 = (s32[16384]{0:T(1024)S(1)}, s32[16384]{0:T(1024)}, u32[]{:S(2)}) copy-start(s32[16384]{0:T(1024)} %param.14) | copy-start | bytes 196612
  0.7 9.5 %copy-start.11 = (f32[1280]{0:T(1024)S(1)}, f32[1280]{0:T(1024)}, u32[]{:S(2)}) copy-start(f32[1280]{0:T(1024)} %param.15) | copy-start | bytes 15364
  0.7 9.6 %copy-start.12 = (f32[1280]{0:T(1024)S(1)}, f32[1280]{0:T(1024)}, u32[]{:S(2)}) copy-start(f32[1280]{0:T(1024)} %param.16) | copy-start | bytes 15364
  0.7 9.7 %copy-start.1 = (bf16[3,1280,128]{2,1,0:T(8,128)(2,1)S(1)}, bf16[3,1280,128]{2,1,0:T(8,128)(2,1)}, u32[]{:S(2)}) copy-start(bf16[3,1280,128]{2,1,0:T(8,128)(2,1)} %param.17) | copy-start | bytes 2949124
  2.6 16.8 %all-to-all-start = ((bf16[8,256,160]{1,2,0:T(8,128)(2,1)}), bf16[8,256,160]{1,2,0:T(8,128)(2,1)S(1)}, u32[]{:S(2)}, u32[]{:S(2)}) async-start(bf16[8,256,160]{1,2,0:T(8,128)(2,1)} %broadcast_in_dim.1455), calls=%async_computation | async-start | bytes 1310720 | tf_op jit(solution)/shard_map/all_to_all | solution.py:21
  11.4 8.5 %copy-start.5 = (bf16[1,1280,128]{2,1,0:T(8,128)(2,1)S(1)}, bf16[1,1280,128]{2,1,0:T(8,128)(2,1)}, u32[]{:S(2)}) copy-start(bf16[1,1280,128]{2,1,0:T(8,128)(2,1)} %get-tuple-element.24) | copy-start | bytes 983044
  19.9 1.0 copy-start.4
  20.6 10.0 %copy-start.3 = (bf16[1,1280,128]{2,1,0:T(8,128)(2,1)S(1)}, bf16[1,1280,128]{2,1,0:T(8,128)(2,1)}, u32[]{:S(2)}) copy-start(bf16[1,1280,128]{2,1,0:T(8,128)(2,1)} %get-tuple-element.23) | copy-start | bytes 983044
  21.6 9.8 %collective-permute-start.1 = (bf16[256,256]{0,1:T(8,128)(2,1)S(1)}, bf16[256,256]{0,1:T(8,128)(2,1)S(1)}, u32[]{:S(2)}, u32[]{:S(2)}) collective-permute-start(bf16[256,256]{0,1:T(8,128)(2,1)S(1)} %pad_maximum_fusion.2), channel_id=1, source_target_pairs={{8,0},{16,8},{24,16},{32,24},{40,32},{48,40},{56,48},{64,56},{72,6... | collective-permute-start | bytes 393224 | tf_op jit(solution)/shard_map/ppermute | solution.py:28
  27.5 5.0 %collective-permute-start = (bf16[256,256]{0,1:T(8,128)(2,1)S(1)}, bf16[256,256]{0,1:T(8,128)(2,1)S(1)}, u32[]{:S(2)}, u32[]{:S(2)}) collective-permute-start(bf16[256,256]{0,1:T(8,128)(2,1)S(1)} %pad_maximum_fusion.2), channel_id=1, source_target_pairs={{0,8},{8,16},{16,24},{24,32},{32,40},{40,48},{48,56},{56,64},{64,7... | collective-permute-start | bytes 393224 | tf_op jit(solution)/shard_map/ppermute | solution.py:28
  34.7 4.6 %copy-start.13 = (f32[64,5]{0,1:T(8,128)S(1)}, f32[64,5]{0,1:T(8,128)}, u32[]{:S(2)}) copy-start(f32[64,5]{0,1:T(8,128)} %param.24) | copy-start | bytes 3844
  34.7 15.4 %copy-start.8 = (bf16[256,160]{0,1:T(8,128)(2,1)S(1)}, bf16[256,160]{0,1:T(8,128)(2,1)}, u32[]{:S(2)}) copy-start(bf16[256,160]{0,1:T(8,128)(2,1)} %param.13) | copy-start | bytes 245764
  34.7 15.4 %copy-start.15 = (bf16[1024,160]{0,1:T(8,128)(2,1)S(1)}, bf16[1024,160]{0,1:T(8,128)(2,1)}, u32[]{:S(2)}) copy-start(bf16[1024,160]{0,1:T(8,128)(2,1)} %param.18) | copy-start | bytes 983044
  34.7 15.4 %copy-start.16 = (f32[160]{0:T(256)S(1)}, f32[160]{0:T(256)}, u32[]{:S(2)}) copy-start(f32[160]{0:T(256)} %param.19) | copy-start | bytes 1924
  35.7 14.3 %all-to-all-start.1 = ((bf16[8,256,128]{2,1,0:T(8,128)(2,1)}), bf16[8,256,128]{2,1,0:T(8,128)(2,1)S(1)}, u32[]{:S(2)}, u32[]{:S(2)}) async-start(bf16[8,256,128]{2,1,0:T(8,128)(2,1)} %broadcast_in_dim.1457), calls=%async_computation.1 | async-start | bytes 1048576 | tf_op jit(solution)/shard_map/all_to_all | solution.py:21
  39.3 11.6 %copy-start.2 = (bf16[160,2560]{1,0:T(8,128)(2,1)S(1)}, bf16[160,2560]{1,0:T(8,128)(2,1)}, u32[]{:S(2)}) copy-start(bf16[160,2560]{1,0:T(8,128)(2,1)} %param.20) | copy-start | bytes 2457604
  50.4 1.4 copy-start.7
  50.8 13.2 %copy-start.10 = (f32[2560]{0:T(1024)S(1)}, f32[2560]{0:T(1024)}, u32[]{:S(2)}) copy-start(f32[2560]{0:T(1024)} %param.21) | copy-start | bytes 30724
  51.8 24.8 %copy-start.6 = (bf16[2560,32]{0,1:T(8,128)(2,1)S(1)}, bf16[2560,32]{0,1:T(8,128)(2,1)}, u32[]{:S(2)}) copy-start(bf16[2560,32]{0,1:T(8,128)(2,1)} %param.23) | copy-start | bytes 491524
  51.8 12.0 %all-to-all-start.2 = ((bf16[8,8,2560]{2,1,0:T(8,128)(2,1)}), bf16[8,8,2560]{2,1,0:T(8,128)(2,1)S(1)}, u32[]{:S(2)}, u32[]{:S(2)}) async-start(bf16[8,8,2560]{2,1,0:T(8,128)(2,1)} %fusion), calls=%async_computation.2 | async-start | bytes 655360 | tf_op jit(solution)/shard_map/all_to_all | solution.py:161
  64.9 11.7 %all-to-all-start.3 = ((bf16[8,8,2560]{2,1,0:T(8,128)(2,1)}), bf16[8,8,2560]{2,1,0:T(8,128)(2,1)S(1)}, u32[]{:S(2)}, u32[]{:S(2)}) async-start(bf16[8,8,2560]{2,1,0:T(8,128)(2,1)} %broadcast_in_dim.1458), calls=%async_computation.3 | async-start | bytes 655360 | tf_op jit(solution)/shard_map/all_to_all | solution.py:21
  77.6 10.5 %all-to-all-start.4 = ((bf16[8,2,1024]{2,1,0:T(2,128)(2,1)}), bf16[8,2,1024]{2,1,0:T(2,128)(2,1)S(1)}, u32[]{:S(2)}, u32[]{:S(2)}) async-start(bf16[8,2,1024]{2,1,0:T(2,128)(2,1)} %reshape.10530), calls=%async_computation.4 | async-start | bytes 65536 | tf_op jit(solution)/shard_map/all_to_all | solution.py:21
  89.7 16.8 %all-to-all-start.5 = ((f32[8,48,128]{2,1,0:T(8,128)}), f32[8,48,128]{2,1,0:T(8,128)S(1)}, u32[]{:S(2)}, u32[]{:S(2)}) async-start(f32[8,48,128]{2,1,0:T(8,128)} %pad_maximum_fusion.1), calls=%async_computation.5 | async-start | bytes 393216 | tf_op jit(solution)/shard_map/all_to_all | solution.py:61
  107.4 46.0 %copy-start.14 = (f32[5]{0:T(128)S(1)}, f32[5]{0:T(128)}, u32[]{:S(2)}) copy-start(f32[5]{0:T(128)} %param.25) | copy-start | bytes 64
  107.5 25.8 %all-to-all-start.6 = ((f32[8,48,128]{2,1,0:T(8,128)}), f32[8,48,128]{2,1,0:T(8,128)S(1)}, u32[]{:S(2)}, u32[]{:S(2)}) async-start(f32[8,48,128]{2,1,0:T(8,128)} %broadcast_in_dim.1555), calls=%async_computation.6 | async-start | bytes 393216 | tf_op jit(solution)/shard_map/all_to_all | solution.py:21
  139.0 14.3 %all-to-all-start.7 = ((f32[8,40,128]{2,1,0:T(8,128)}), f32[8,40,128]{2,1,0:T(8,128)S(1)}, u32[]{:S(2)}, u32[]{:S(2)}) async-start(f32[8,40,128]{2,1,0:T(8,128)} %add_dynamic-update-slice_fusion), calls=%async_computation.7 | async-start | bytes 327680 | tf_op jit(solution)/shard_map/all_to_all | solution.py:84

commit v2 on v0

v2 whole, which is shorter than its diff:
```python
import functools

import jax
import jax.numpy as jnp
from jax import lax
from jax.experimental import pallas as pl
from jax.experimental.pallas import tpu as pltpu
from jax.sharding import PartitionSpec as P

EHEAD_DIM = 64
HDIM = 64
NSTATE = 128
WINDOW = 256
GROUP = 8
POOL = 4

EPSILON = 1e-05
SMALLEST = 1e-37
HIGHEST = lax.Precision.HIGHEST
BF16 = jnp.bfloat16
F32 = jnp.float32


def shape(dims, kind):
    return jax.ShapeDtypeStruct(dims, kind)


def silu(v):
    return v / (1.0 + jnp.exp(-v))


def dot(a, b, dims=((1,), (0,)), precision=None):
    return lax.dot_general(
        a, b, (dims, ((), ())), preferred_element_type=F32, precision=precision
    )


def swap(copies, axis, groups=None):
    return lax.all_to_all(copies, axis, 0, 0, tiled=True, axis_index_groups=groups)


def copy_kernel(x_ref, out_ref):
    value = x_ref[...]
    for j in range(out_ref.shape[0]):
        out_ref[j] = value


def qkv_kernel(x_ref, gain_ref, bias_ref, weight_ref, q_ref, kv_ref):
    count, _, share = x_ref.shape
    features = count * share
    total = 0.0
    for j in range(count):
        total = total + jnp.sum(x_ref[j].astype(F32), axis=-1, keepdims=True)
    center = total / features
    square = 0.0
    for j in range(count):
        square = square + jnp.sum(
            jnp.square(x_ref[j].astype(F32) - center), axis=-1, keepdims=True
        )
    factor = lax.rsqrt(square / features + EPSILON)
    width = weight_ref.shape[2]
    total = 0.0
    for j in range(count):
        normed = ((x_ref[j].astype(F32) - center) * factor * gain_ref[j] + bias_ref[j]).astype(BF16)
        rows = slice(j * share, (j + 1) * share)
        weight = jnp.concatenate([weight_ref[k, rows, :] for k in range(3)], axis=1)
        total = total + dot(normed, weight)
    rounded = total.astype(BF16)
    q_ref[...] = rounded[:, :width] * BF16(EHEAD_DIM**-0.5)
    kv_ref[...] = rounded[:, width:]


def attend_kernel(q_ref, own_ref, low_ref, high_ref, row_ref, col_ref, out_ref):
    rows = q_ref.shape[0]
    width = q_ref.shape[1]
    pieces = (low_ref, own_ref, high_ref)
    allowed = [
        row_ref[...] == col_ref[:, k * rows : (k + 1) * rows] for k in range(len(pieces))
    ]
    blended = []
    for h in range(width // EHEAD_DIM):
        cols = slice(h * EHEAD_DIM, (h + 1) * EHEAD_DIM)
        vals = slice(width + h * EHEAD_DIM, width + (h + 1) * EHEAD_DIM)
        query = q_ref[:, cols]
        scores = [
            jnp.where(ok, dot(query, piece[:, cols], ((1,), (1,))), -1e30)
            for ok, piece in zip(allowed, pieces)
        ]
        peak = functools.reduce(
            jnp.maximum, [jnp.max(s, axis=-1, keepdims=True) for s in scores]
        )
        raised = [jnp.exp(s - peak) for s in scores]
        total = sum(jnp.sum(r, axis=-1, keepdims=True) for r in raised)
        mixed = sum(dot(r.astype(BF16), piece[:, vals]) for r, piece in zip(raised, pieces))
        blended.append(mixed / total)
    value = jnp.concatenate(blended, axis=1).astype(BF16)
    for j in range(out_ref.shape[0]):
        out_ref[j] = value


def encode_kernel(att_ref, weight_ref, frames_ref, bias_ref, adapter_ref, encoded_ref, part_ref):
    count, rows, width = att_ref.shape
    total = 0.0
    for j in range(0, count, 2):
        both = jnp.concatenate([att_ref[j], att_ref[j + 1]], axis=1)
        total = total + dot(both, weight_ref[j * width : (j + 2) * width, :])
    encoded = (frames_ref[...].astype(F32) + total + bias_ref[...]).astype(BF16)
    encoded_ref[...] = encoded
    tokens = rows // POOL
    token = lax.broadcasted_iota(jnp.int32, (tokens, rows), 0)
    frame = lax.broadcasted_iota(jnp.int32, (tokens, rows), 1)
    inside = (frame >= token * POOL) & (frame < (token + 1) * POOL)
    averaging = jnp.where(inside, 1.0 / POOL, 0.0).astype(BF16)
    pooled = dot(averaging, encoded).astype(BF16)
    part = dot(pooled, adapter_ref[...])
    part_ref[...] = part.reshape(part_ref.shape).astype(BF16)


def scale_kernel(part_ref, gain_ref, out_ref):
    projected = jnp.sum(part_ref[...].astype(F32), axis=0)
    spread = jnp.mean(jnp.square(projected), axis=-1, keepdims=True)
    value = (projected * lax.rsqrt(spread + EPSILON) * gain_ref[...]).astype(BF16)
    for j in range(out_ref.shape[0]):
        out_ref[j] = value


def split_rows(rows):
    first = rows.astype(BF16).astype(F32)
    second = (rows - first).astype(BF16).astype(F32)
    third = rows - first - second
    lanes = lax.broadcasted_iota(jnp.int32, rows.shape, 1)
    return jnp.where(lanes < 32, first, jnp.where(lanes < 64, second, third))


def joined_rows(parts):
    return parts[:, 0:1] + parts[:, 32:33] + parts[:, 64:65]


def state_kernel(
    scaled_ref, weight_ref, coupler_ref, decay_ref, skip_ref, base_ref, grow_ref, c_ref, out_ref
):
    scaled = scaled_ref[...]
    inputs = silu(dot(scaled, weight_ref[...])).astype(BF16).astype(F32)
    couplers = jnp.concatenate([coupler_ref[k] for k in range(coupler_ref.shape[0])], axis=1)
    b_in = couplers[:, :NSTATE]
    c_in = couplers[:, NSTATE:]
    c_ref[...] = c_in
    decay = decay_ref[...]
    tokens, heads = decay.shape
    log_decay = jnp.log(jnp.maximum(decay, SMALLEST))
    late = lax.broadcasted_iota(jnp.int32, (tokens, tokens), 0)
    early = lax.broadcasted_iota(jnp.int32, (tokens, tokens), 1)
    causal = late >= early
    below = jnp.where(causal, 1.0, 0.0)
    cumulative = dot(below, log_decay, precision=HIGHEST)
    across = dot(log_decay, below, ((0,), (1,)), precision=HIGHEST)
    grow_ref[...] = jnp.exp(cumulative)
    affinity = dot(c_in, b_in, ((1,), (1,)))
    b_wide = b_in.astype(F32)
    states, totals = [], []
    for h in range(heads):
        cols = slice(h * HDIM, (h + 1) * HDIM)
        column = cumulative[:, h : h + 1]
        gap = jnp.where(causal, column - across[h : h + 1, :], -1e30)
        own = inputs[:, cols]
        driven = own * (1.0 - decay[:, h : h + 1])
        within = dot(affinity * jnp.exp(gap), driven, precision=HIGHEST)
        base_ref[:, cols] = within + skip_ref[h] * own
        last = cumulative[tokens - 1 : tokens, h : h + 1]
        tail = jnp.exp(last - column)
        states.append(dot(driven * tail, b_wide, ((0,), (0,)), precision=HIGHEST))
        totals.append(jnp.broadcast_to(jnp.exp(last), (1, NSTATE)))
    totals.append(jnp.zeros((8 - heads, NSTATE), F32))
    ends = split_rows(jnp.concatenate(totals, axis=0))
    state = jnp.concatenate(states, axis=0)
    share = state.shape[0] // GROUP
    for j in range(GROUP):
        piece = jnp.concatenate([state[j * share : (j + 1) * share], ends], axis=0)
        out_ref[j] = piece.astype(BF16)


def spread_decay(decays, row_head, heads):
    out = jnp.zeros(row_head.shape, F32)
    for h in range(heads):
        out = jnp.where(row_head == h, decays[h : h + 1, :], out)
    return out


def row_heads(lane, share):
    rows = lane * share + lax.broadcasted_iota(jnp.int32, (share, NSTATE), 0)
    return lax.shift_right_logical(rows, HDIM.bit_length() - 1)


def near_kernel(place_ref, got_ref, out_ref, *, heads):
    share = got_ref.shape[1] - 8
    lane = lax.rem(place_ref[0], GROUP)
    row_head = row_heads(lane, share)
    state = jnp.zeros((share, NSTATE), F32)
    grown = jnp.ones((8, 1), F32)
    for k in range(GROUP):
        piece = got_ref[k].astype(F32)
        ends = joined_rows(piece[share:])
        state = spread_decay(ends, row_head, heads) * state + piece[:share]
        grown = grown * ends
    value = jnp.concatenate(
        [state, split_rows(jnp.broadcast_to(grown, (8, NSTATE)))], axis=0
    ).astype(BF16)
    for j in range(out_ref.shape[0]):
        out_ref[j] = value


def far_kernel(place_ref, got_ref, total_ref, out_ref, *, heads):
    share = got_ref.shape[1] - 8
    lane = lax.rem(place_ref[0], GROUP)
    group = lax.div(place_ref[0], GROUP)
    row_head = row_heads(lane, share)
    before = jnp.zeros((share, NSTATE), F32)
    for k in range(total_ref.shape[0]):
        piece = total_ref[k].astype(F32)
        step = spread_decay(joined_rows(piece[share:]), row_head, heads) * before + piece[:share]
        before = jnp.where(k < group, step, before)
    state = before
    for k in range(GROUP):
        out_ref[k] = state.astype(BF16)
        piece = got_ref[k].astype(F32)
        state = spread_decay(joined_rows(piece[share:]), row_head, heads) * state + piece[:share]


def final_kernel(state_ref, c_ref, base_ref, grow_ref, out_ref):
    rows = state_ref.shape[0] * state_ref.shape[1]
    state = state_ref[...].astype(F32).reshape(rows, NSTATE).astype(BF16)
    carried = dot(c_ref[...], state, ((1,), (1,)))
    for h in range(rows // HDIM):
        cols = slice(h * HDIM, (h + 1) * HDIM)
        value = base_ref[:, cols] + grow_ref[:, h : h + 1] * carried[:, cols]
        out_ref[:, cols] = value.astype(BF16)


SMEM = pl.BlockSpec(memory_space=pltpu.SMEM)
VMEM = pl.BlockSpec(memory_space=pltpu.VMEM)


def per_device(
    frames,
    segment_ids,
    ln_gain,
    ln_bias,
    qkv_weight,
    out_weight,
    out_bias,
    adapter,
    rms_gain,
    x_weight,
    bc_weight,
    decay,
    skip_gain,
):
    frame_count, share = frames.shape
    count = lax.axis_size("tm")
    place = lax.axis_index("tm")
    hosts = lax.axis_size("head")
    head_width = qkv_weight.shape[2]
    model = adapter.shape[1]
    tokens, heads = decay.shape
    per = tokens // hosts

    copies = pl.pallas_call(copy_kernel, out_shape=shape((hosts, frame_count, share), BF16))(frames)
    gathered = swap(copies, "head")
    queries, own = pl.pallas_call(
        qkv_kernel,
        out_shape=(
            shape((frame_count, head_width), BF16),
            shape((frame_count, 2 * head_width), BF16),
        ),
    )(gathered, ln_gain.reshape(hosts, 1, share), ln_bias.reshape(hosts, 1, share), qkv_weight)
    low = lax.ppermute(own, "tm", [(i, i + 1) for i in range(count - 1)])
    high = lax.ppermute(own, "tm", [(i + 1, i) for i in range(count - 1)])
    ids = jnp.pad(segment_ids, (WINDOW, WINDOW), constant_values=-1)
    ids = lax.dynamic_slice_in_dim(ids, place * frame_count, frame_count + 2 * WINDOW, 0)
    attended = pl.pallas_call(
        attend_kernel, out_shape=shape((hosts, frame_count, head_width), BF16)
    )(queries, own, low, high, ids[WINDOW : WINDOW + frame_count, None], ids[None, :])
    encoded, parts = pl.pallas_call(
        encode_kernel,
        out_shape=(shape((frame_count, share), BF16), shape((hosts, per, model), BF16)),
    )(swap(attended, "head"), out_weight, frames, out_bias[None, :], adapter)
    scaled = pl.pallas_call(scale_kernel, out_shape=shape((hosts, per, model), BF16))(
        swap(parts, "head"), rms_gain[None, :]
    )
    scaled = swap(scaled, "head").reshape(tokens, model)
    coupler_part = jax.nn.silu(jnp.dot(scaled, bc_weight, preferred_element_type=F32)).astype(BF16)
    couplers = swap(jnp.broadcast_to(coupler_part[None], (hosts,) + coupler_part.shape), "head")

    rows = heads * HDIM // GROUP
    state_shape = shape((GROUP, rows + 8, NSTATE), BF16)
    base, grow, c_rows, ends = pl.pallas_call(
        state_kernel,
        out_shape=(
            shape((tokens, heads * HDIM), F32),
            shape((tokens, heads), F32),
            shape((tokens, NSTATE), BF16),
            state_shape,
        ),
        in_specs=[VMEM, VMEM, VMEM, VMEM, SMEM],
    )(scaled, x_weight, couplers, decay, skip_gain)
    near = [[first + k for k in range(GROUP)] for first in range(0, count, GROUP)]
    far = [[lane + GROUP * k for k in range(count // GROUP)] for lane in range(GROUP)]
    where = place[None].astype(jnp.int32)
    got = swap(ends, "tm", near)
    totals = pl.pallas_call(
        functools.partial(near_kernel, heads=heads),
        out_shape=shape((count // GROUP, rows + 8, NSTATE), BF16),
        in_specs=[SMEM, VMEM],
    )(where, got)
    entering = pl.pallas_call(
        functools.partial(far_kernel, heads=heads),
        out_shape=shape((GROUP, rows, NSTATE), BF16),
        in_specs=[SMEM, VMEM, VMEM],
    )(where, got, swap(totals, "tm", far))
    mixed = pl.pallas_call(final_kernel, out_shape=shape((tokens, heads * HDIM), BF16))(
        swap(entering, "tm", near), c_rows, base, grow
    )
    return (encoded, mixed)


def solution(mesh):
    placed = (
        P("tm", "head"),
        P(),
        P(),
        P(),
        P(None, None, "head"),
        P(None, "head"),
        P("head"),
        P("head", None),
        P(),
        P(None, "head"),
        P(None, "head"),
        P("tm", "head"),
        P("head"),
    )
    return jax.shard_map(
        per_device,
        mesh=mesh,
        in_specs=placed,
        out_specs=(P("tm", "head"), P("tm", "head")),
        check_vma=False,
    )
```

time: 435 us -> 162 us (0.37)
  the two profiles are of different devices: /device:TPU:483 before, /device:TPU:1 now
where the time goes in v2:
time: 162 us; the launch traced here: 161 us
  blocking collectives  53.8 us (33%)
  waiting for transfers between devices  33.3 us (21%)
  starting transfers between devices  32.7 us (20%)
  Pallas kernels  22.5 us (14%)
  local copies, waits for them, and re-layouts  18 us (11%)
    all_to_all x3, blocking collectives, swap(): lax.all_to_all(copies, axis, 0, 0, tiled=True, axis_index_groups=groups)  53.8 us
    all_to_all x5, waiting for transfers between devices, swap(): lax.all_to_all(copies, axis, 0, 0, tiled=True, axis_index_groups=groups)  32.6 us
    all_to_all x5, starting transfers between devices, swap(): lax.all_to_all(copies, axis, 0, 0, tiled=True, axis_index_groups=groups)  23.7 us
    unnamed x38, local copies, waits for them, and re-layouts  10.3 us
    ppermute x1, starting transfers between devices, per_device(): high = lax.ppermute(own, 'tm', [(i + 1, i) for i in range(count - 1)])  5.94 us
    pallas_call x1, Pallas kernels, per_device(): pl.pallas_call(qkv_kernel, out_shape=(shape((frame_count, head_width), BF...  3.61 us
    pallas_call x1, Pallas kernels, per_device(): pl.pallas_call(state_kernel, out_shape=(shape((tokens, heads * HDIM), F32...  3.36 us
    pallas_call x1, Pallas kernels, per_device(): pl.pallas_call(attend_kernel, out_shape=shape((hosts, frame_count, head_w...  3.27 us
  transfers between devices with their start and end apart: 7, of which 6 were waited for; matrix products, arithmetic and copies ran while one was open for 5% of the time, Pallas kernels for 0%

profile of v2, /device:TPU:1, one launch (start us, length us, event | category | flops | bytes accessed | tf_op | source)
XLA Modules:
  0.0 161.3 jit_solution(10854476366396418086)
XLA Ops:
  0.6 0.0 copy-start
  0.6 1.7 %copy.30.x_ref.frames_ref = bf16[256,160]{1,0:T(8,128)(2,1)} copy(bf16[256,160]{0,1:T(8,128)(2,1)} %param.13) | data formatting | bytes 163840 | tf_op args[0]
  2.3 2.0 %shard_map.140 = bf16[8,256,160]{2,1,0:T(8,128)(2,1)} custom-call(bf16[256,160]{1,0:T(8,128)(2,1)} %copy.30.x_ref.frames_ref), custom_call_target="tpu_custom_call" | custom-call | tf_op jit(solution)/shard_map/pallas_call | solution.py:267
  4.3 2.2 %copy.31 = bf16[8,256,160]{1,2,0:T(8,128)(2,1)} copy(bf16[8,256,160]{2,1,0:T(8,128)(2,1)} %shard_map.140) | data formatting | bytes 1310720 | tf_op jit(solution)/shard_map/pallas_call | solution.py:267
  6.5 7.5 %all-to-all-start = ((bf16[8,256,160]{1,2,0:T(8,128)(2,1)}), bf16[8,256,160]{1,2,0:T(8,128)(2,1)S(1)}, u32[]{:S(2)}, u32[]{:S(2)}) async-start(bf16[8,256,160]{1,2,0:T(8,128)(2,1)} %copy.31), calls=%async_computation | async-start | bytes 1310720 | tf_op jit(solution)/shard_map/all_to_all | solution.py:39
  14.0 0.7 reshape.14.gain_ref
  14.7 0.7 reshape.15.bias_ref
  15.3 8.0 %all-to-all-done = bf16[8,256,160]{1,2,0:T(8,128)(2,1)S(1)} async-done(((bf16[8,256,160]{1,2,0:T(8,128)(2,1)}), bf16[8,256,160]{1,2,0:T(8,128)(2,1)S(1)}, u32[]{:S(2)}, u32[]{:S(2)}) %all-to-all-start) | async-done | bytes 655392 | tf_op jit(solution)/shard_map/all_to_all | solution.py:39
  23.3 1.3 copy.32.x_ref
  24.6 3.6 %shard_map.141 = (bf16[256,128]{1,0:T(8,128)(2,1)}, bf16[256,256]{1,0:T(8,128)(2,1)}) custom-call(bf16[8,256,160]{2,1,0:T(8,128)(2,1)} %copy.32.x_ref, f32[8,1,160]{2,1,0:T(1,128)} %reshape.14.gain_ref, f32[8,1,160]{2,1,0:T(1,128)} %reshape.15.bias_ref, bf16[3,1280,128]{2,1,0:T(8,128)(2,1)} %weight_ref.3), custom_call_target="tpu_custom_call" | custom-call | tf_op jit(solution)/shard_map/pallas_call | solution.py:269
  28.2 5.9 %collective-permute-start.1 = (bf16[256,256]{1,0:T(8,128)(2,1)}, bf16[256,256]{1,0:T(8,128)(2,1)S(1)}, u32[]{:S(2)}, u32[]{:S(2)}) collective-permute-start(bf16[256,256]{1,0:T(8,128)(2,1)} %get-tuple-element.11.own_ref), channel_id=1, source_target_pairs={{8,0},{16,8},{24,16},{32,24},{40,32},{48,40},{56,48},{64,56},{72,6... | collective-permute-start | bytes 393224 | tf_op jit(solution)/shard_map/ppermute | solution.py:277
  34.2 3.1 %collective-permute-start = (bf16[256,256]{1,0:T(8,128)(2,1)}, bf16[256,256]{1,0:T(8,128)(2,1)S(1)}, u32[]{:S(2)}, u32[]{:S(2)}) collective-permute-start(bf16[256,256]{1,0:T(8,128)(2,1)} %get-tuple-element.11.own_ref), channel_id=1, source_target_pairs={{0,8},{8,16},{16,24},{24,32},{32,40},{40,48},{48,56},{56,64},{64,7... | collective-permute-start | bytes 393224 | tf_op jit(solution)/shard_map/ppermute | solution.py:276
  37.3 0.1 pad_dynamic-slice_fusion
  37.4 0.6 broadcast_in_dim.22.col_ref
  38.0 0.8 copy.33.row_ref
  38.8 0.8 collective-permute-done.low_ref
  39.5 0.7 copy-done.8
  40.2 3.3 %shard_map.142 = bf16[8,256,128]{2,1,0:T(8,128)(2,1)} custom-call(bf16[256,128]{1,0:T(8,128)(2,1)} %get-tuple-element.10.q_ref, bf16[256,256]{1,0:T(8,128)(2,1)} %get-tuple-element.11.own_ref, bf16[256,256]{1,0:T(8,128)(2,1)} %copy-done.8, bf16[256,256]{1,0:T(8,128)(2,1)} %copy-done.7, s32[256,1]{1,0:T(8,128)} %copy.33.row_ref, ...), custom_call_target="tpu_custom_call" | custom-call | tf_op jit(solution)/shard_map/pallas_call | solution.py:280
  43.5 3.5 %all-to-all-start.1 = ((bf16[8,256,128]{2,1,0:T(8,128)(2,1)}), bf16[8,256,128]{2,1,0:T(8,128)(2,1)S(1)}, u32[]{:S(2)}, u32[]{:S(2)}) async-start(bf16[8,256,128]{2,1,0:T(8,128)(2,1)} %shard_map.142), calls=%async_computation.1 | async-start | bytes 1048576 | tf_op jit(solution)/shard_map/all_to_all | solution.py:39
  47.0 0.0 copy-start.11
  47.0 1.0 copy.34.weight_ref
  48.0 9.3 %all-to-all-done.1.att_ref = bf16[8,256,128]{2,1,0:T(8,128)(2,1)S(1)} async-done(((bf16[8,256,128]{2,1,0:T(8,128)(2,1)}), bf16[8,256,128]{2,1,0:T(8,128)(2,1)S(1)}, u32[]{:S(2)}, u32[]{:S(2)}) %all-to-all-start.1) | async-done | bytes 524320 | tf_op jit(solution)/shard_map/all_to_all | solution.py:39
  57.3 0.8 copy-done.2
  58.2 3.2 %shard_map.143 = (bf16[256,160]{1,0:T(8,128)(2,1)}, bf16[8,8,2560]{2,1,0:T(8,128)(2,1)}) custom-call(bf16[8,256,128]{2,1,0:T(8,128)(2,1)} %copy-done.2, bf16[1024,160]{1,0:T(8,128)(2,1)} %copy.34.weight_ref, bf16[256,160]{1,0:T(8,128)(2,1)} %copy.30.x_ref.frames_ref, f32[1,160]{1,0:T(1,128)} %bitcast.15, bf16[160,2560]{1,0:T(8,128)(2,1)} %adapter_ref.1), custom_call_target="tpu_custom_call" | custom-call | tf_op jit(solution)/shard_map/pallas_call | solution.py:283
  61.3 3.4 %all-to-all-start.2 = ((bf16[8,8,2560]{2,1,0:T(8,128)(2,1)}), bf16[8,8,2560]{2,1,0:T(8,128)(2,1)S(1)}, u32[]{:S(2)}, u32[]{:S(2)}) async-start(bf16[8,8,2560]{2,1,0:T(8,128)(2,1)} %get-tuple-element.13), calls=%async_computation.2 | async-start | bytes 655360 | tf_op jit(solution)/shard_map/all_to_all | solution.py:39
  64.8 0.6 broadcast_in_dim.25.gain_ref
  65.4 7.4 %all-to-all-done.2.part_ref = bf16[8,8,2560]{2,1,0:T(8,128)(2,1)S(1)} async-done(((bf16[8,8,2560]{2,1,0:T(8,128)(2,1)}), bf16[8,8,2560]{2,1,0:T(8,128)(2,1)S(1)}, u32[]{:S(2)}, u32[]{:S(2)}) %all-to-all-start.2) | async-done | bytes 327712 | tf_op jit(solution)/shard_map/all_to_all | solution.py:39
  72.8 0.7 copy-done.4
  73.5 1.9 %shard_map.144 = bf16[8,8,2560]{2,1,0:T(8,128)(2,1)} custom-call(bf16[8,8,2560]{2,1,0:T(8,128)(2,1)} %copy-done.4, f32[1,2560]{1,0:T(1,128)} %broadcast_in_dim.25.gain_ref), custom_call_target="tpu_custom_call" | custom-call | tf_op jit(solution)/shard_map/pallas_call | solution.py:287
  75.3 12.5 %all_to_all.40 = bf16[8,8,2560]{2,1,0:T(8,128)(2,1)S(1)} all-to-all(bf16[8,8,2560]{2,1,0:T(8,128)(2,1)} %shard_map.144), channel_id=1, replica_groups=mesh['tm'=64,'head'=8] {'head'}, dimensions={0} | all-to-all | bytes 655360 | tf_op jit(solution)/shard_map/all_to_all | solution.py:39
  87.8 0.2 multiply_convert_fusion
  88.1 0.7 reshape.17
  88.8 3.4 %all-to-all-start.4 = ((bf16[8,2,1024]{2,1,0:T(2,128)(2,1)}), bf16[8,2,1024]{2,1,0:T(2,128)(2,1)S(1)}, u32[]{:S(2)}, u32[]{:S(2)}) async-start(bf16[8,2,1024]{2,1,0:T(2,128)(2,1)} %reshape.17), calls=%async_computation.4 | async-start | bytes 65536 | tf_op jit(solution)/shard_map/all_to_all | solution.py:39
  92.2 0.7 copy.38.decay_ref
  92.9 2.4 %copy.36.weight_ref = bf16[2560,320]{1,0:T(8,128)(2,1)} copy(bf16[2560,320]{0,1:T(8,128)(2,1)S(1)} %copy-done.3) | data formatting | bytes 3276800 | tf_op args[9]
  95.3 3.5 %all-to-all-done.4 = bf16[8,2,1024]{2,1,0:T(2,128)(2,1)S(1)} async-done(((bf16[8,2,1024]{2,1,0:T(2,128)(2,1)}), bf16[8,2,1024]{2,1,0:T(2,128)(2,1)S(1)}, u32[]{:S(2)}, u32[]{:S(2)}) %all-to-all-start.4) | async-done | bytes 32800 | tf_op jit(solution)/shard_map/all_to_all | solution.py:39
  98.8 0.1 reshape.18
  98.9 0.8 copy.37.coupler_ref
  99.7 3.4 %shard_map.145 = (f32[64,320]{1,0:T(8,128)}, f32[64,5]{1,0:T(8,128)}, bf16[64,128]{1,0:T(8,128)(2,1)}, bf16[8,48,128]{2,1,0:T(8,128)(2,1)}) custom-call(bf16[64,2560]{1,0:T(8,128)(2,1)} %bitcast.12, bf16[2560,320]{1,0:T(8,128)(2,1)} %copy.36.weight_ref, bf16[8,64,32]{2,1,0:T(8,128)(2,1)} %copy.37.coupler_ref, f32[64,5]{1,0:T(8,128)} %copy.38.decay_ref, ...), custom_call_target="tpu_custom_call" | custom-call | tf_op jit(solution)/shard_map/pallas_call | solution.py:296
  103.0 16.7 %all_to_all.41.got_ref = bf16[8,48,128]{2,1,0:T(8,128)(2,1)} all-to-all(bf16[8,48,128]{2,1,0:T(8,128)(2,1)} %get-tuple-element.14), channel_id=1, replica_groups={{0,8,16,24,32,40,48,56},{64,72,80,88,96,104,112,120},{128,136,144,152,1..., dimensions={0} | all-to-all | bytes 196608 | tf_op jit(solution)/shard_map/all_to_all | solution.py:39
  119.7 1.7 %shard_map.146 = bf16[8,48,128]{2,1,0:T(8,128)(2,1)} custom-call(s32[1]{0:T(128)} %bitcast.2.place_ref, bf16[8,48,128]{2,1,0:T(8,128)(2,1)} %all_to_all.41.got_ref), custom_call_target="tpu_custom_call" | custom-call | tf_op jit(solution)/shard_map/pallas_call | solution.py:310
  121.4 24.6 %all_to_all.42.total_ref = bf16[8,48,128]{2,1,0:T(8,128)(2,1)} all-to-all(bf16[8,48,128]{2,1,0:T(8,128)(2,1)} %shard_map.146), channel_id=1, replica_groups={{0,64,128,192,256,320,384,448},{8,72,136,200,264,328,392,456},{16,80,14..., dimensions={0} | all-to-all | bytes 196608 | tf_op jit(solution)/shard_map/all_to_all | solution.py:39
  146.0 1.8 %shard_map.147 = bf16[8,40,128]{2,1,0:T(8,128)(2,1)} custom-call(s32[1]{0:T(128)} %bitcast.2.place_ref, bf16[8,48,128]{2,1,0:T(8,128)(2,1)} %all_to_all.41.got_ref, bf16[8,48,128]{2,1,0:T(8,128)(2,1)} %all_to_all.42.total_ref), custom_call_target="tpu_custom_call" | custom-call | tf_op jit(solution)/shard_map/pallas_call | solution.py:315
  147.8 6.0 %all-to-all-start.7 = ((bf16[8,40,128]{2,1,0:T(8,128)(2,1)}), bf16[8,40,128]{2,1,0:T(8,128)(2,1)S(1)}, u32[]{:S(2)}, u32[]{:S(2)}) async-start(bf16[8,40,128]{2,1,0:T(8,128)(2,1)} %shard_map.147), calls=%async_computation.7 | async-start | bytes 163840 | tf_op jit(solution)/shard_map/all_to_all | solution.py:39
  153.8 0.7 copy.39
  154.5 4.4 %all-to-all-done.7.state_ref = bf16[8,40,128]{2,1,0:T(8,128)(2,1)S(1)} async-done(((bf16[8,40,128]{2,1,0:T(8,128)(2,1)}), bf16[8,40,128]{2,1,0:T(8,128)(2,1)S(1)}, u32[]{:S(2)}, u32[]{:S(2)}) %all-to-all-start.7) | async-done | bytes 81952 | tf_op jit(solution)/shard_map/all_to_all | solution.py:39
  159.0 0.6 copy-done.6
  159.6 1.7 %shard_map.148 = bf16[64,320]{1,0:T(8,128)(2,1)} custom-call(bf16[8,40,128]{2,1,0:T(8,128)(2,1)} %copy-done.6, bf16[64,128]{1,0:T(8,128)(2,1)} %get-tuple-element.15.c_ref, f32[64,320]{1,0:T(8,128)} %get-tuple-element.16.base_ref, f32[64,5]{1,0:T(8,128)} %get-tuple-element.17.grow_ref), custom_call_target="tpu_custom_call" | custom-call | tf_op jit(solution)/shard_map/pallas_call | solution.py:320
  (27 shorter events, 0.1 us)
Async XLA Ops:
  0.6 87.2 %copy-start = (bf16[2560,32]{0,1:T(8,128)(2,1)S(1)}, bf16[2560,32]{0,1:T(8,128)(2,1)}, u32[]{:S(2)}) copy-start(bf16[2560,32]{0,1:T(8,128)(2,1)} %param.23) | copy-start | bytes 491524
  2.3 11.6 %copy-start.12 = (f32[1280]{0:T(1024)S(1)}, f32[1280]{0:T(1024)}, u32[]{:S(2)}) copy-start(f32[1280]{0:T(1024)} %param.15) | copy-start | bytes 15364
  2.3 12.3 %copy-start.13 = (f32[1280]{0:T(1024)S(1)}, f32[1280]{0:T(1024)}, u32[]{:S(2)}) copy-start(f32[1280]{0:T(1024)} %param.16) | copy-start | bytes 15364
  6.5 16.8 %all-to-all-start = ((bf16[8,256,160]{1,2,0:T(8,128)(2,1)}), bf16[8,256,160]{1,2,0:T(8,128)(2,1)S(1)}, u32[]{:S(2)}, u32[]{:S(2)}) async-start(bf16[8,256,160]{1,2,0:T(8,128)(2,1)} %copy.31), calls=%async_computation | async-start | bytes 1310720 | tf_op jit(solution)/shard_map/all_to_all | solution.py:39
  14.0 23.3 %copy-start.10 = (s32[16384]{0:T(1024)S(1)}, s32[16384]{0:T(1024)}, u32[]{:S(2)}) copy-start(s32[16384]{0:T(1024)} %param.14) | copy-start | bytes 196612
  24.6 22.3 %copy-start.5 = (bf16[1024,160]{0,1:T(8,128)(2,1)S(1)}, bf16[1024,160]{0,1:T(8,128)(2,1)}, u32[]{:S(2)}) copy-start(bf16[1024,160]{0,1:T(8,128)(2,1)} %param.18) | copy-start | bytes 983044
  28.2 10.5 %collective-permute-start.1 = (bf16[256,256]{1,0:T(8,128)(2,1)}, bf16[256,256]{1,0:T(8,128)(2,1)S(1)}, u32[]{:S(2)}, u32[]{:S(2)}) collective-permute-start(bf16[256,256]{1,0:T(8,128)(2,1)} %get-tuple-element.11.own_ref), channel_id=1, source_target_pairs={{8,0},{16,8},{24,16},{32,24},{40,32},{48,40},{56,48},{64,56},{72,6... | collective-permute-start | bytes 393224 | tf_op jit(solution)/shard_map/ppermute | solution.py:277
  34.2 5.3 %collective-permute-start = (bf16[256,256]{1,0:T(8,128)(2,1)}, bf16[256,256]{1,0:T(8,128)(2,1)S(1)}, u32[]{:S(2)}, u32[]{:S(2)}) collective-permute-start(bf16[256,256]{1,0:T(8,128)(2,1)} %get-tuple-element.11.own_ref), channel_id=1, source_target_pairs={{0,8},{8,16},{16,24},{24,32},{32,40},{40,48},{48,56},{56,64},{64,7... | collective-permute-start | bytes 393224 | tf_op jit(solution)/shard_map/ppermute | solution.py:276
  38.8 0.8 copy-start.7
  39.5 0.7 copy-start.8
  43.5 13.9 %all-to-all-start.1 = ((bf16[8,256,128]{2,1,0:T(8,128)(2,1)}), bf16[8,256,128]{2,1,0:T(8,128)(2,1)S(1)}, u32[]{:S(2)}, u32[]{:S(2)}) async-start(bf16[8,256,128]{2,1,0:T(8,128)(2,1)} %shard_map.142), calls=%async_computation.1 | async-start | bytes 1048576 | tf_op jit(solution)/shard_map/all_to_all | solution.py:39
  47.0 17.8 %copy-start.11 = (f32[2560]{0:T(1024)S(1)}, f32[2560]{0:T(1024)}, u32[]{:S(2)}) copy-start(f32[2560]{0:T(1024)} %param.21) | copy-start | bytes 30724
  57.3 0.8 copy-start.2
  58.2 34.0 %copy-start.14 = (f32[64,5]{0,1:T(8,128)S(1)}, f32[64,5]{0,1:T(8,128)}, u32[]{:S(2)}) copy-start(f32[64,5]{0,1:T(8,128)} %param.24) | copy-start | bytes 3844
  58.2 34.7 %copy-start.3 = (bf16[2560,320]{0,1:T(8,128)(2,1)S(1)}, bf16[2560,320]{0,1:T(8,128)(2,1)}, u32[]{:S(2)}) copy-start(bf16[2560,320]{0,1:T(8,128)(2,1)} %param.22) | copy-start | bytes 4915204
  61.3 11.4 %all-to-all-start.2 = ((bf16[8,8,2560]{2,1,0:T(8,128)(2,1)}), bf16[8,8,2560]{2,1,0:T(8,128)(2,1)S(1)}, u32[]{:S(2)}, u32[]{:S(2)}) async-start(bf16[8,8,2560]{2,1,0:T(8,128)(2,1)} %get-tuple-element.13), calls=%async_computation.2 | async-start | bytes 655360 | tf_op jit(solution)/shard_map/all_to_all | solution.py:39
  72.8 0.7 copy-start.4
  87.8 7.5 %copy-start.1 = (bf16[8,8,2560]{2,1,0:T(8,128)(2,1)}, bf16[8,8,2560]{2,1,0:T(8,128)(2,1)S(1)}, u32[]{:S(2)}) copy-start(bf16[8,8,2560]{2,1,0:T(8,128)(2,1)S(1)} %all_to_all.40) | copy-start | bytes 983044
  88.8 10.0 %all-to-all-start.4 = ((bf16[8,2,1024]{2,1,0:T(2,128)(2,1)}), bf16[8,2,1024]{2,1,0:T(2,128)(2,1)S(1)}, u32[]{:S(2)}, u32[]{:S(2)}) async-start(bf16[8,2,1024]{2,1,0:T(2,128)(2,1)} %reshape.17), calls=%async_computation.4 | async-start | bytes 65536 | tf_op jit(solution)/shard_map/all_to_all | solution.py:39
  95.3 58.5 %copy-start.9 = (bf16[256,160]{1,0:T(8,128)(2,1)S(1)}, bf16[256,160]{1,0:T(8,128)(2,1)}, u32[]{:S(2)}) copy-start(bf16[256,160]{1,0:T(8,128)(2,1)} %get-tuple-element.22) | copy-start | bytes 245764
  147.8 11.1 %all-to-all-start.7 = ((bf16[8,40,128]{2,1,0:T(8,128)(2,1)}), bf16[8,40,128]{2,1,0:T(8,128)(2,1)S(1)}, u32[]{:S(2)}, u32[]{:S(2)}) async-start(bf16[8,40,128]{2,1,0:T(8,128)(2,1)} %shard_map.147), calls=%async_computation.7 | async-start | bytes 163840 | tf_op jit(solution)/shard_map/all_to_all | solution.py:39
  159.0 0.6 copy-start.6

commit v3 on v2

v3 whole, which is shorter than its diff:
```python
import functools

import jax
import jax.numpy as jnp
from jax import lax
from jax.experimental import pallas as pl
from jax.experimental.pallas import tpu as pltpu
from jax.sharding import PartitionSpec as P

EHEAD_DIM = 64
HDIM = 64
NSTATE = 128
WINDOW = 256
GROUP = 8
POOL = 4

EPSILON = 1e-05
SMALLEST = 1e-37
HIGHEST = lax.Precision.HIGHEST
BF16 = jnp.bfloat16
F32 = jnp.float32


def shape(dims, kind):
    return jax.ShapeDtypeStruct(dims, kind)


def silu(v):
    return v / (1.0 + jnp.exp(-v))


def dot(a, b, dims=((1,), (0,)), precision=None):
    return lax.dot_general(
        a, b, (dims, ((), ())), preferred_element_type=F32, precision=precision
    )


def swap(copies, axis, groups=None):
    return lax.all_to_all(copies, axis, 0, 0, tiled=True, axis_index_groups=groups)


def copy_kernel(x_ref, out_ref):
    value = x_ref[...]
    for j in range(out_ref.shape[0]):
        out_ref[j] = value


def qkv_kernel(x_ref, gain_ref, bias_ref, weight_ref, q_ref, kv_ref):
    count, share, frames = x_ref.shape
    features = count * share
    wide = x_ref[...].astype(F32).reshape(features, frames)
    center = jnp.sum(wide, axis=0, keepdims=True) / features
    wide = wide - center
    spread = jnp.sum(jnp.square(wide), axis=0, keepdims=True) / features
    normed = (wide * lax.rsqrt(spread + EPSILON) * gain_ref[...] + bias_ref[...]).astype(BF16)
    width = q_ref.shape[0]
    rounded = dot(weight_ref[...], normed).astype(BF16)
    q_ref[...] = rounded[:width] * BF16(EHEAD_DIM**-0.5)
    kv_ref[...] = rounded[width:]


def attend_kernel(place_ref, q_ref, own_ref, low_ref, high_ref, ids_ref, out_ref):
    width, frames = q_ref.shape
    blocks = ids_ref.shape[0]
    place = place_ref[0]
    pieces = (low_ref, own_ref, high_ref)
    mine = ids_ref[pl.ds(place, 1), :]
    allowed = []
    for k in range(3):
        at = place + (k - 1)
        ids = ids_ref[pl.ds(jnp.clip(at, 0, blocks - 1), 1), :]
        ids = jnp.where((at >= 0) & (at < blocks), ids, -1.0)
        column = jnp.broadcast_to(ids, (8, frames)).T[:, 0:1]
        allowed.append(column == mine)
    blended = []
    for h in range(width // EHEAD_DIM):
        keys = slice(h * EHEAD_DIM, (h + 1) * EHEAD_DIM)
        vals = slice(width + h * EHEAD_DIM, width + (h + 1) * EHEAD_DIM)
        query = q_ref[keys, :]
        scores = [
            jnp.where(ok, dot(piece[keys, :], query, ((0,), (0,))), -1e30)
            for ok, piece in zip(allowed, pieces)
        ]
        peak = functools.reduce(
            jnp.maximum, [jnp.max(s, axis=0, keepdims=True) for s in scores]
        )
        raised = [jnp.exp(s - peak) for s in scores]
        total = sum(jnp.sum(r, axis=0, keepdims=True) for r in raised)
        mixed = sum(dot(piece[vals, :], r.astype(BF16)) for r, piece in zip(raised, pieces))
        blended.append(mixed / total)
    value = jnp.concatenate(blended, axis=0).astype(BF16)
    for j in range(out_ref.shape[0]):
        out_ref[j] = value


def encode_kernel(att_ref, weight_ref, frames_ref, bias_ref, adapter_ref, encoded_ref, part_ref):
    count, width, rows = att_ref.shape
    total = dot(weight_ref[...], att_ref[...].reshape(count * width, rows))
    encoded = (frames_ref[...].astype(F32) + total + bias_ref[...]).astype(BF16)
    encoded_ref[...] = encoded
    tokens = rows // POOL
    token = lax.broadcasted_iota(jnp.int32, (tokens, rows), 0)
    frame = lax.broadcasted_iota(jnp.int32, (tokens, rows), 1)
    inside = (frame >= token * POOL) & (frame < (token + 1) * POOL)
    averaging = jnp.where(inside, 1.0 / POOL, 0.0).astype(BF16)
    pooled = dot(averaging, encoded, ((1,), (1,))).astype(BF16)
    part = dot(pooled, adapter_ref[...])
    part_ref[...] = part.reshape(part_ref.shape).astype(BF16)


def scale_kernel(part_ref, gain_ref, out_ref):
    projected = jnp.sum(part_ref[...].astype(F32), axis=0)
    spread = jnp.mean(jnp.square(projected), axis=-1, keepdims=True)
    value = (projected * lax.rsqrt(spread + EPSILON) * gain_ref[...]).astype(BF16)
    for j in range(out_ref.shape[0]):
        out_ref[j] = value


def split_rows(rows):
    first = rows.astype(BF16).astype(F32)
    second = (rows - first).astype(BF16).astype(F32)
    third = rows - first - second
    lanes = lax.broadcasted_iota(jnp.int32, rows.shape, 1)
    return jnp.where(lanes < 32, first, jnp.where(lanes < 64, second, third))


def joined_rows(parts):
    return parts[:, 0:1] + parts[:, 32:33] + parts[:, 64:65]


def twice(wide, narrow, dims=((1,), (0,))):
    first = wide.astype(BF16)
    second = (wide - first.astype(F32)).astype(BF16)
    return dot(first, narrow, dims) + dot(second, narrow, dims)


def state_kernel(
    skip_ref, scaled_ref, weight_ref, coupler_ref, decay_ref, base_ref, grow_ref, c_ref, out_ref
):
    scaled = scaled_ref[...]
    inputs = silu(dot(weight_ref[...], scaled, ((1,), (1,)))).astype(BF16)
    couplers = jnp.concatenate([coupler_ref[k] for k in range(coupler_ref.shape[0])], axis=1)
    b_in = couplers[:, :NSTATE]
    c_in = couplers[:, NSTATE:]
    c_ref[...] = c_in
    decay = decay_ref[...]
    heads, tokens = decay.shape
    log_decay = jnp.log(jnp.maximum(decay, SMALLEST))
    late = lax.broadcasted_iota(jnp.int32, (tokens, tokens), 0)
    early = lax.broadcasted_iota(jnp.int32, (tokens, tokens), 1)
    causal = late >= early
    below = jnp.where(causal, 1.0, 0.0)
    cumulative = dot(below, log_decay, ((1,), (1,)), precision=HIGHEST)
    across = dot(log_decay, below, ((1,), (1,)), precision=HIGHEST)
    grow_ref[...] = jnp.exp(cumulative)
    affinity = dot(c_in, b_in, ((1,), (1,)))
    given = 1.0 - decay
    last = across[:, tokens - 1 : tokens]
    tail = jnp.exp(last - across) * given
    states = []
    for h in range(heads):
        cols = slice(h * HDIM, (h + 1) * HDIM)
        gap = jnp.where(causal, cumulative[:, h : h + 1] - across[h : h + 1, :], -1e30)
        weights = affinity * jnp.exp(gap) * given[h : h + 1, :]
        weights = jnp.where(late == early, weights + skip_ref[h], weights)
        base_ref[:, cols] = twice(weights, inputs[cols, :], ((1,), (1,)))
        driven = inputs[cols, :].astype(F32) * tail[h : h + 1, :]
        states.append(twice(driven, b_in))
    ends = jnp.concatenate([jnp.exp(last), jnp.zeros((8 - heads, 1), F32)], axis=0)
    ends = split_rows(jnp.broadcast_to(ends, (8, NSTATE)))
    state = jnp.concatenate(states, axis=0)
    share = state.shape[0] // GROUP
    for j in range(GROUP):
        piece = jnp.concatenate([state[j * share : (j + 1) * share], ends], axis=0)
        out_ref[j] = piece.astype(BF16)


def spread_decay(decays, row_head, heads):
    out = jnp.zeros(row_head.shape, F32)
    for h in range(heads):
        out = jnp.where(row_head == h, decays[h : h + 1, :], out)
    return out


def row_heads(lane, share):
    rows = lane * share + lax.broadcasted_iota(jnp.int32, (share, NSTATE), 0)
    return lax.shift_right_logical(rows, HDIM.bit_length() - 1)


def near_kernel(place_ref, got_ref, out_ref, *, heads):
    share = got_ref.shape[1] - 8
    lane = lax.rem(place_ref[0], GROUP)
    row_head = row_heads(lane, share)
    state = jnp.zeros((share, NSTATE), F32)
    grown = jnp.ones((8, 1), F32)
    for k in range(GROUP):
        piece = got_ref[k].astype(F32)
        ends = joined_rows(piece[share:])
        state = spread_decay(ends, row_head, heads) * state + piece[:share]
        grown = grown * ends
    value = jnp.concatenate(
        [state, split_rows(jnp.broadcast_to(grown, (8, NSTATE)))], axis=0
    ).astype(BF16)
    for j in range(out_ref.shape[0]):
        out_ref[j] = value


def far_kernel(place_ref, got_ref, total_ref, out_ref, *, heads):
    share = got_ref.shape[1] - 8
    lane = lax.rem(place_ref[0], GROUP)
    group = lax.div(place_ref[0], GROUP)
    row_head = row_heads(lane, share)
    before = jnp.zeros((share, NSTATE), F32)
    for k in range(total_ref.shape[0]):
        piece = total_ref[k].astype(F32)
        step = spread_decay(joined_rows(piece[share:]), row_head, heads) * before + piece[:share]
        before = jnp.where(k < group, step, before)
    state = before
    for k in range(GROUP):
        out_ref[k] = state.astype(BF16)
        piece = got_ref[k].astype(F32)
        state = spread_decay(joined_rows(piece[share:]), row_head, heads) * state + piece[:share]


def final_kernel(state_ref, c_ref, base_ref, grow_ref, out_ref):
    rows = state_ref.shape[0] * state_ref.shape[1]
    state = state_ref[...].astype(F32).reshape(rows, NSTATE).astype(BF16)
    carried = dot(c_ref[...], state, ((1,), (1,)))
    for h in range(rows // HDIM):
        cols = slice(h * HDIM, (h + 1) * HDIM)
        value = base_ref[:, cols] + grow_ref[:, h : h + 1] * carried[:, cols]
        out_ref[:, cols] = value.astype(BF16)


def call(kernel, outs, *operands, scalars=0):
    placed = [
        x if k < scalars else pltpu.with_memory_space_constraint(x, pltpu.VMEM)
        for k, x in enumerate(operands)
    ]
    spaces = [pltpu.SMEM if k < scalars else pltpu.VMEM for k in range(len(operands))]
    many = isinstance(outs[0][0], tuple)
    made = pl.pallas_call(
        kernel,
        out_shape=tuple(pltpu.VMEM(dims, kind) for dims, kind in (outs if many else (outs,))),
        in_specs=[pl.BlockSpec(memory_space=space) for space in spaces],
        out_specs=tuple(pl.BlockSpec(memory_space=pltpu.VMEM) for _ in (outs if many else (outs,))),
        compiler_params=pltpu.CompilerParams(vmem_limit_bytes=24 << 20),
    )(*placed)
    return made if many else made[0]


def per_device(
    frames,
    segment_ids,
    ln_gain,
    ln_bias,
    qkv_weight,
    out_weight,
    out_bias,
    adapter,
    rms_gain,
    x_weight,
    bc_weight,
    decay,
    skip_gain,
):
    frame_count, share = frames.shape
    count = lax.axis_size("tm")
    place = lax.axis_index("tm")
    hosts = lax.axis_size("head")
    features = hosts * share
    head_width = qkv_weight.shape[2]
    model = adapter.shape[1]
    tokens, heads = decay.shape
    per = tokens // hosts
    where = place[None].astype(jnp.int32)

    across = frames.T
    copies = call(copy_kernel, ((hosts, share, frame_count), BF16), across)
    gathered = swap(copies, "head")
    queries, own = call(
        qkv_kernel,
        (((head_width, frame_count), BF16), ((2 * head_width, frame_count), BF16)),
        gathered,
        ln_gain[:, None],
        ln_bias[:, None],
        jnp.transpose(qkv_weight, (0, 2, 1)).reshape(3 * head_width, features),
    )
    low = lax.ppermute(own, "tm", [(i, i + 1) for i in range(count - 1)])
    high = lax.ppermute(own, "tm", [(i + 1, i) for i in range(count - 1)])
    attended = call(
        attend_kernel,
        ((hosts, head_width, frame_count), BF16),
        where,
        queries,
        own,
        low,
        high,
        segment_ids.astype(F32).reshape(count, frame_count),
        scalars=1,
    )
    encoded, parts = call(
        encode_kernel,
        (((share, frame_count), BF16), ((hosts, per, model), BF16)),
        swap(attended, "head"),
        out_weight.T,
        across,
        out_bias[:, None],
        adapter,
    )
    scaled = call(
        scale_kernel, ((hosts, per, model), BF16), swap(parts, "head"), rms_gain[None, :]
    )
    scaled = swap(scaled, "head").reshape(tokens, model)
    coupler_part = jax.nn.silu(jnp.dot(scaled, bc_weight, preferred_element_type=F32)).astype(BF16)
    couplers = swap(jnp.broadcast_to(coupler_part[None], (hosts,) + coupler_part.shape), "head")

    rows = heads * HDIM // GROUP
    base, grow, c_rows, ends = call(
        state_kernel,
        (
            ((tokens, heads * HDIM), F32),
            ((tokens, heads), F32),
            ((tokens, NSTATE), BF16),
            ((GROUP, rows + 8, NSTATE), BF16),
        ),
        skip_gain,
        scaled,
        x_weight.T,
        couplers,
        decay.T,
        scalars=1,
    )
    near = [[first + k for k in range(GROUP)] for first in range(0, count, GROUP)]
    far = [[lane + GROUP * k for k in range(count // GROUP)] for lane in range(GROUP)]
    got = swap(ends, "tm", near)
    totals = call(
        functools.partial(near_kernel, heads=heads),
        ((count // GROUP, rows + 8, NSTATE), BF16),
        where,
        got,
        scalars=1,
    )
    entering = call(
        functools.partial(far_kernel, heads=heads),
        ((GROUP, rows, NSTATE), BF16),
        where,
        got,
        swap(totals, "tm", far),
        scalars=1,
    )
    mixed = call(
        final_kernel, ((tokens, heads * HDIM), BF16), swap(entering, "tm", near), c_rows, base, grow
    )
    return (encoded.T, mixed)


def solution(mesh):
    placed = (
        P("tm", "head"),
        P(),
        P(),
        P(),
        P(None, None, "head"),
        P(None, "head"),
        P("head"),
        P("head", None),
        P(),
        P(None, "head"),
        P(None, "head"),
        P("tm", "head"),
        P("head"),
    )
    return jax.shard_map(
        per_device,
        mesh=mesh,
        in_specs=placed,
        out_specs=(P("tm", "head"), P("tm", "head")),
        check_vma=False,
    )
```

time: 162 us -> 140 us (0.86)
  local copies, waits for them, and re-layouts: 18 us -> 3.79 us
  Pallas kernels: 22.5 us -> 8.33 us
  blocking collectives: 53.8 us -> 60.7 us
  starting transfers between devices: 32.7 us -> 29.9 us
  waiting for transfers between devices: 33.3 us -> 35 us
    pallas_call x9, Pallas kernels: 22.5 us -> 8.33 us  [call(): pl.pallas_call(kernel, out_shape=tuple((pltpu.VMEM(dims, kind) for dims,...]
    unnamed x38 -> x33, local copies, waits for them, and re-layouts: 10.3 us -> 2.47 us
    all_to_all x3 -> x4, blocking collectives: 53.8 us -> 60.7 us  [swap(): lax.all_to_all(copies, axis, 0, 0, tiled=True, axis_index_groups=groups)]
    ppermute x1, waiting for transfers between devices: 0.01 us -> 4.29 us  [per_device(): high = lax.ppermute(own, 'tm', [(i + 1, i) for i in range(count - 1)])]
    ppermute x1, starting transfers between devices: 3.1 us -> 7.27 us  [per_device(): low = lax.ppermute(own, 'tm', [(i, i + 1) for i in range(count - 1)])]
    ppermute x1, starting transfers between devices: 5.94 us -> 1.92 us  [per_device(): high = lax.ppermute(own, 'tm', [(i + 1, i) for i in range(count - 1)])]
    all_to_all x5 -> x4, starting transfers between devices: 23.7 us -> 20.7 us  [swap(): lax.all_to_all(copies, axis, 0, 0, tiled=True, axis_index_groups=groups)]
    pallas_call x1 -> x0, local copies, waits for them, and re-layouts: 2.18 us -> none  [per_device(): pl.pallas_call(copy_kernel, out_shape=shape((hosts, frame_count, share),...]
  transfers between devices with their start and end apart: 7 -> 6, of which waited for: 6 -> 5; matrix products, arithmetic and copies ran while one was open for 5% -> 1% of each run, Pallas kernels for 0% -> 0%
where the time goes in v3:
time: 140 us; the launch traced here: 139 us
  blocking collectives  60.7 us (43%)
  waiting for transfers between devices  35 us (25%)
  starting transfers between devices  29.9 us (21%)
  Pallas kernels  8.33 us (6%)
  local copies, waits for them, and re-layouts  3.79 us (3%)
    all_to_all x4, blocking collectives, swap(): lax.all_to_all(copies, axis, 0, 0, tiled=True, axis_index_groups=groups)  60.7 us
    all_to_all x4, waiting for transfers between devices, swap(): lax.all_to_all(copies, axis, 0, 0, tiled=True, axis_index_groups=groups)  30.7 us
    all_to_all x4, starting transfers between devices, swap(): lax.all_to_all(copies, axis, 0, 0, tiled=True, axis_index_groups=groups)  20.7 us
    pallas_call x9, Pallas kernels, call(): pl.pallas_call(kernel, out_shape=tuple((pltpu.VMEM(dims, kind) for dims,...  8.33 us
    ppermute x1, starting transfers between devices, per_device(): low = lax.ppermute(own, 'tm', [(i, i + 1) for i in range(count - 1)])  7.27 us
    ppermute x1, waiting for transfers between devices, per_device(): high = lax.ppermute(own, 'tm', [(i + 1, i) for i in range(count - 1)])  4.29 us
  transfers between devices with their start and end apart: 6, of which 5 were waited for; matrix products, arithmetic and copies ran while one was open for 1% of the time, Pallas kernels for 0%

profile of v3, /device:TPU:1, one launch (start us, length us, event | category | flops | bytes accessed | tf_op | source)
XLA Modules:
  0.0 138.9 jit_solution(5909108003598945694)
XLA Ops:
  0.6 0.0 copy-start
  0.6 0.0 copy-start.4
  0.7 0.9 copy-done.4
  1.6 0.9 shard_map.140
  2.5 7.6 %all-to-all-start = ((bf16[8,160,256]{2,1,0:T(8,128)(2,1)}), bf16[8,160,256]{2,1,0:T(8,128)(2,1)S(1)}, u32[]{:S(2)}, u32[]{:S(2)}) async-start(bf16[8,160,256]{2,1,0:T(8,128)(2,1)} %shard_map.140), calls=%async_computation | async-start | bytes 1310720 | tf_op jit(solution)/shard_map/all_to_all | solution.py:39
  10.1 0.0 copy-done.8
  10.1 0.6 copy.22
  10.7 0.0 copy-done.11
  10.7 0.2 broadcast_in_dim.27.gain_ref
  10.9 0.0 copy-done.12
  11.0 0.2 broadcast_in_dim.28.bias_ref
  11.2 0.0 copy-start.9
  11.2 8.2 %all-to-all-done.x_ref = bf16[8,160,256]{2,1,0:T(8,128)(2,1)S(1)} async-done(((bf16[8,160,256]{2,1,0:T(8,128)(2,1)}), bf16[8,160,256]{2,1,0:T(8,128)(2,1)S(1)}, u32[]{:S(2)}, u32[]{:S(2)}) %all-to-all-start) | async-done | bytes 655392 | tf_op jit(solution)/shard_map/all_to_all | solution.py:39
  19.4 1.0 shard_map.141
  20.4 0.0 copy-start.13
  20.5 0.0 copy-start.2
  20.5 0.0 copy-start.3
  20.5 0.0 copy-start.5
  20.5 7.3 %collective-permute-start = (bf16[256,256]{1,0:T(8,128)(2,1)S(1)}, bf16[256,256]{1,0:T(8,128)(2,1)S(1)}, u32[]{:S(2)}, u32[]{:S(2)}) collective-permute-start(bf16[256,256]{1,0:T(8,128)(2,1)S(1)} %get-tuple-element.11.own_ref), channel_id=1, source_target_pairs={{0,8},{8,16},{16,24},{24,32},{32,40},{40,48},{48,56},{56,64},{64,7... | collective-permute-start | bytes 393224 | tf_op jit(solution)/shard_map/ppermute | solution.py:289
  27.8 1.9 %collective-permute-start.1 = (bf16[256,256]{1,0:T(8,128)(2,1)S(1)}, bf16[256,256]{1,0:T(8,128)(2,1)S(1)}, u32[]{:S(2)}, u32[]{:S(2)}) collective-permute-start(bf16[256,256]{1,0:T(8,128)(2,1)S(1)} %get-tuple-element.11.own_ref), channel_id=1, source_target_pairs={{8,0},{16,8},{24,16},{32,24},{40,32},{48,40},{56,48},{64,56},{72,6... | collective-permute-start | bytes 393224 | tf_op jit(solution)/shard_map/ppermute | solution.py:290
  29.7 0.0 collective-permute-done.low_ref
  29.8 4.3 %collective-permute-done.1.high_ref = bf16[256,256]{1,0:T(8,128)(2,1)S(1)} collective-permute-done((bf16[256,256]{1,0:T(8,128)(2,1)S(1)}, bf16[256,256]{1,0:T(8,128)(2,1)S(1)}, u32[]{:S(2)}, u32[]{:S(2)}) %collective-permute-start.1) | collective-permute-done | bytes 131104 | tf_op jit(solution)/shard_map/ppermute | solution.py:290
  34.0 1.9 %shard_map.142 = bf16[8,128,256]{2,1,0:T(8,128)(2,1)} custom-call(s32[1]{0:T(128)} %bitcast.place_ref, bf16[128,256]{1,0:T(8,128)(2,1)S(1)} %get-tuple-element.10.q_ref, bf16[256,256]{1,0:T(8,128)(2,1)S(1)} %get-tuple-element.11.own_ref, bf16[256,256]{1,0:T(8,128)(2,1)S(1)} %collective-permute-done.low_ref, ...), custom_call_target="tpu_custom_call" | custom-call | tf_op jit(solution)/shard_map/pallas_call | solution.py:242
  36.0 3.6 %all-to-all-start.1 = ((bf16[8,128,256]{2,1,0:T(8,128)(2,1)}), bf16[8,128,256]{2,1,0:T(8,128)(2,1)S(1)}, u32[]{:S(2)}, u32[]{:S(2)}) async-start(bf16[8,128,256]{2,1,0:T(8,128)(2,1)} %shard_map.142), calls=%async_computation.1 | async-start | bytes 1048576 | tf_op jit(solution)/shard_map/all_to_all | solution.py:39
  39.6 0.0 copy-done.13
  39.6 0.1 copy.25.bias_ref
  39.7 8.9 %all-to-all-done.1.att_ref = bf16[8,128,256]{2,1,0:T(8,128)(2,1)S(1)} async-done(((bf16[8,128,256]{2,1,0:T(8,128)(2,1)}), bf16[8,128,256]{2,1,0:T(8,128)(2,1)S(1)}, u32[]{:S(2)}, u32[]{:S(2)}) %all-to-all-start.1) | async-done | bytes 524320 | tf_op jit(solution)/shard_map/all_to_all | solution.py:39
  48.6 0.0 copy-done.5
  48.6 1.5 %shard_map.143 = (bf16[160,256]{1,0:T(8,128)(2,1)S(1)}, bf16[8,8,2560]{2,1,0:T(8,128)(2,1)}) custom-call(bf16[8,128,256]{2,1,0:T(8,128)(2,1)S(1)} %all-to-all-done.1.att_ref, bf16[160,1024]{1,0:T(8,128)(2,1)S(1)} %bitcast.22, bf16[160,256]{1,0:T(8,128)(2,1)S(1)} %bitcast.24, f32[160,1]{1,0:T(8,128)S(1)} %copy.25.bias_ref, bf16[160,2560]{1,0:T(8,128)(2,1)S(1)} %copy-done.2), custom_call_target="tpu_custom_call" | custom-call | tf_op jit(solution)/shard_map/pallas_call | solution.py:242
  50.1 3.6 %all-to-all-start.2 = ((bf16[8,8,2560]{2,1,0:T(8,128)(2,1)}), bf16[8,8,2560]{2,1,0:T(8,128)(2,1)S(1)}, u32[]{:S(2)}, u32[]{:S(2)}) async-start(bf16[8,8,2560]{2,1,0:T(8,128)(2,1)} %get-tuple-element.13), calls=%async_computation.2 | async-start | bytes 655360 | tf_op jit(solution)/shard_map/all_to_all | solution.py:39
  53.7 9.0 %all-to-all-done.2.part_ref = bf16[8,8,2560]{2,1,0:T(8,128)(2,1)S(1)} async-done(((bf16[8,8,2560]{2,1,0:T(8,128)(2,1)}), bf16[8,8,2560]{2,1,0:T(8,128)(2,1)S(1)}, u32[]{:S(2)}, u32[]{:S(2)}) %all-to-all-start.2) | async-done | bytes 327712 | tf_op jit(solution)/shard_map/all_to_all | solution.py:39
  62.7 0.2 shard_map.144
  62.9 12.0 %all_to_all.40 = bf16[8,8,2560]{2,1,0:T(8,128)(2,1)S(1)} all-to-all(bf16[8,8,2560]{2,1,0:T(8,128)(2,1)S(1)} %shard_map.144), channel_id=1, replica_groups=mesh['tm'=64,'head'=8] {'head'}, dimensions={0} | all-to-all | bytes 655360 | tf_op jit(solution)/shard_map/all_to_all | solution.py:39
  74.9 0.2 multiply_convert_fusion
  75.1 0.1 reshape.17
  75.2 9.5 %all_to_all.41 = bf16[8,2,1024]{2,1,0:T(2,128)(2,1)S(1)} all-to-all(bf16[8,2,1024]{2,1,0:T(2,128)(2,1)S(1)} %reshape.17), channel_id=1, replica_groups=mesh['tm'=64,'head'=8] {'head'}, dimensions={0} | all-to-all | bytes 65536 | tf_op jit(solution)/shard_map/all_to_all | solution.py:39
  84.7 0.1 reshape.18
  84.8 0.1 copy.26.coupler_ref
  85.0 1.6 %shard_map.145 = (f32[64,320]{1,0:T(8,128)S(1)}, f32[64,5]{1,0:T(8,128)S(1)}, bf16[64,128]{1,0:T(8,128)(2,1)S(1)}, bf16[8,48,128]{2,1,0:T(8,128)(2,1)S(1)}) custom-call(f32[5]{0:T(128)S(1)} %copy-done.7, bf16[64,2560]{1,0:T(8,128)(2,1)S(1)} %bitcast.20, bf16[320,2560]{1,0:T(8,128)(2,1)S(1)} %bitcast.21, bf16[8,64,32]{2,1,0:T(8,128)(2,1)S(1)} %copy.26.coupler_ref, ...), custom_call_target="tpu_custom_call" | custom-call | tf_op jit(solution)/shard_map/pallas_call | solution.py:242
  86.6 13.2 %all_to_all.42.got_ref = bf16[8,48,128]{2,1,0:T(8,128)(2,1)S(1)} all-to-all(bf16[8,48,128]{2,1,0:T(8,128)(2,1)S(1)} %get-tuple-element.14), channel_id=1, replica_groups={{0,8,16,24,32,40,48,56},{64,72,80,88,96,104,112,120},{128,136,144,152,1..., dimensions={0} | all-to-all | bytes 196608 | tf_op jit(solution)/shard_map/all_to_all | solution.py:39
  99.8 0.2 shard_map.146
  100.0 26.1 %all_to_all.43.total_ref = bf16[8,48,128]{2,1,0:T(8,128)(2,1)S(1)} all-to-all(bf16[8,48,128]{2,1,0:T(8,128)(2,1)S(1)} %shard_map.146), channel_id=1, replica_groups={{0,64,128,192,256,320,384,448},{8,72,136,200,264,328,392,456},{16,80,14..., dimensions={0} | all-to-all | bytes 196608 | tf_op jit(solution)/shard_map/all_to_all | solution.py:39
  126.1 0.9 shard_map.147
  126.9 6.0 %all-to-all-start.7 = ((bf16[8,40,128]{2,1,0:T(8,128)(2,1)}), bf16[8,40,128]{2,1,0:T(8,128)(2,1)S(1)}, u32[]{:S(2)}, u32[]{:S(2)}) async-start(bf16[8,40,128]{2,1,0:T(8,128)(2,1)} %shard_map.147), calls=%async_computation.7 | async-start | bytes 163840 | tf_op jit(solution)/shard_map/all_to_all | solution.py:39
  132.9 0.6 copy.27
  133.5 4.5 %all-to-all-done.7.state_ref = bf16[8,40,128]{2,1,0:T(8,128)(2,1)S(1)} async-done(((bf16[8,40,128]{2,1,0:T(8,128)(2,1)}), bf16[8,40,128]{2,1,0:T(8,128)(2,1)S(1)}, u32[]{:S(2)}, u32[]{:S(2)}) %all-to-all-start.7) | async-done | bytes 81952 | tf_op jit(solution)/shard_map/all_to_all | solution.py:39
  138.1 0.2 shard_map.148
  138.3 0.6 copy.28
  (19 shorter events, 0.1 us)
Async XLA Ops:
  0.6 74.2 %copy-start = (bf16[2560,32]{0,1:T(8,128)(2,1)S(1)}, bf16[2560,32]{0,1:T(8,128)(2,1)}, u32[]{:S(2)}) copy-start(bf16[2560,32]{0,1:T(8,128)(2,1)} %param.23) | copy-start | bytes 491524
  0.6 0.9 copy-start.4
  1.6 8.5 %copy-start.8 = (bf16[3,1280,128]{2,1,0:T(8,128)(2,1)S(1)}, bf16[3,1280,128]{2,1,0:T(8,128)(2,1)}, u32[]{:S(2)}) copy-start(bf16[3,1280,128]{2,1,0:T(8,128)(2,1)} %param.17) | copy-start | bytes 2949124
  2.5 8.2 %copy-start.11 = (f32[1280]{0:T(1024)S(1)}, f32[1280]{0:T(1024)}, u32[]{:S(2)}) copy-start(f32[1280]{0:T(1024)} %param.15) | copy-start | bytes 15364
  2.5 17.0 %all-to-all-start = ((bf16[8,160,256]{2,1,0:T(8,128)(2,1)}), bf16[8,160,256]{2,1,0:T(8,128)(2,1)S(1)}, u32[]{:S(2)}, u32[]{:S(2)}) async-start(bf16[8,160,256]{2,1,0:T(8,128)(2,1)} %shard_map.140), calls=%async_computation | async-start | bytes 1310720 | tf_op jit(solution)/shard_map/all_to_all | solution.py:39
  10.1 0.9 copy-start.12
  11.2 18.5 %copy-start.9 = (s32[16384]{0:T(1024)S(1)}, s32[16384]{0:T(1024)}, u32[]{:S(2)}) copy-start(s32[16384]{0:T(1024)} %param.14) | copy-start | bytes 196612
  20.4 19.2 %copy-start.13 = (f32[160]{0:T(256)S(1)}, f32[160]{0:T(256)}, u32[]{:S(2)}) copy-start(f32[160]{0:T(256)} %param.19) | copy-start | bytes 1924
  20.5 28.2 %copy-start.2 = (bf16[160,2560]{1,0:T(8,128)(2,1)S(1)}, bf16[160,2560]{1,0:T(8,128)(2,1)}, u32[]{:S(2)}) copy-start(bf16[160,2560]{1,0:T(8,128)(2,1)} %adapter_ref.1) | copy-start | bytes 2457604
  20.5 28.1 %copy-start.3 = (bf16[1024,160]{0,1:T(8,128)(2,1)S(1)}, bf16[1024,160]{0,1:T(8,128)(2,1)}, u32[]{:S(2)}) copy-start(bf16[1024,160]{0,1:T(8,128)(2,1)} %param.18) | copy-start | bytes 983044
  20.5 28.1 %copy-start.5 = (bf16[256,160]{0,1:T(8,128)(2,1)S(1)}, bf16[256,160]{0,1:T(8,128)(2,1)}, u32[]{:S(2)}) copy-start(bf16[256,160]{0,1:T(8,128)(2,1)} %param.13) | copy-start | bytes 245764
  20.5 9.3 %collective-permute-start = (bf16[256,256]{1,0:T(8,128)(2,1)S(1)}, bf16[256,256]{1,0:T(8,128)(2,1)S(1)}, u32[]{:S(2)}, u32[]{:S(2)}) collective-permute-start(bf16[256,256]{1,0:T(8,128)(2,1)S(1)} %get-tuple-element.11.own_ref), channel_id=1, source_target_pairs={{0,8},{8,16},{16,24},{24,32},{32,40},{40,48},{48,56},{56,64},{64,7... | collective-permute-start | bytes 393224 | tf_op jit(solution)/shard_map/ppermute | solution.py:289
  27.8 6.3 %collective-permute-start.1 = (bf16[256,256]{1,0:T(8,128)(2,1)S(1)}, bf16[256,256]{1,0:T(8,128)(2,1)S(1)}, u32[]{:S(2)}, u32[]{:S(2)}) collective-permute-start(bf16[256,256]{1,0:T(8,128)(2,1)S(1)} %get-tuple-element.11.own_ref), channel_id=1, source_target_pairs={{8,0},{16,8},{24,16},{32,24},{40,32},{48,40},{56,48},{64,56},{72,6... | collective-permute-start | bytes 393224 | tf_op jit(solution)/shard_map/ppermute | solution.py:290
  36.0 17.7 %copy-start.10 = (f32[2560]{0:T(1024)S(1)}, f32[2560]{0:T(1024)}, u32[]{:S(2)}) copy-start(f32[2560]{0:T(1024)} %param.21) | copy-start | bytes 30724
  36.0 12.6 %all-to-all-start.1 = ((bf16[8,128,256]{2,1,0:T(8,128)(2,1)}), bf16[8,128,256]{2,1,0:T(8,128)(2,1)S(1)}, u32[]{:S(2)}, u32[]{:S(2)}) async-start(bf16[8,128,256]{2,1,0:T(8,128)(2,1)} %shard_map.142), calls=%async_computation.1 | async-start | bytes 1048576 | tf_op jit(solution)/shard_map/all_to_all | solution.py:39
  50.1 34.8 %copy-start.1 = (bf16[2560,320]{0,1:T(8,128)(2,1)S(1)}, bf16[2560,320]{0,1:T(8,128)(2,1)}, u32[]{:S(2)}) copy-start(bf16[2560,320]{0,1:T(8,128)(2,1)} %param.22) | copy-start | bytes 4915204
  50.1 34.8 %copy-start.6 = (f32[64,5]{0,1:T(8,128)S(1)}, f32[64,5]{0,1:T(8,128)}, u32[]{:S(2)}) copy-start(f32[64,5]{0,1:T(8,128)} %param.24) | copy-start | bytes 3844
  50.1 34.9 %copy-start.7 = (f32[5]{0:T(128)S(1)}, f32[5]{0:T(128)}, u32[]{:S(2)}) copy-start(f32[5]{0:T(128)} %skip_ref.1) | copy-start | bytes 64
  50.1 12.6 %all-to-all-start.2 = ((bf16[8,8,2560]{2,1,0:T(8,128)(2,1)}), bf16[8,8,2560]{2,1,0:T(8,128)(2,1)S(1)}, u32[]{:S(2)}, u32[]{:S(2)}) async-start(bf16[8,8,2560]{2,1,0:T(8,128)(2,1)} %get-tuple-element.13), calls=%async_computation.2 | async-start | bytes 655360 | tf_op jit(solution)/shard_map/all_to_all | solution.py:39
  126.9 11.1 %all-to-all-start.7 = ((bf16[8,40,128]{2,1,0:T(8,128)(2,1)}), bf16[8,40,128]{2,1,0:T(8,128)(2,1)S(1)}, u32[]{:S(2)}, u32[]{:S(2)}) async-start(bf16[8,40,128]{2,1,0:T(8,128)(2,1)} %shard_map.147), calls=%async_computation.7 | async-start | bytes 163840 | tf_op jit(solution)/shard_map/all_to_all | solution.py:39

commit v4 on v3

--- a/solution.py
+++ b/solution.py
@@ -7,10 +7,10 @@
 from jax.experimental.pallas import tpu as pltpu
 from jax.sharding import PartitionSpec as P
 
+
 EHEAD_DIM = 64
 HDIM = 64
 NSTATE = 128
-WINDOW = 256
 GROUP = 8
 POOL = 4
 
@@ -21,10 +21,6 @@
 F32 = jnp.float32
 
 
-def shape(dims, kind):
-    return jax.ShapeDtypeStruct(dims, kind)
-
-
 def silu(v):
     return v / (1.0 + jnp.exp(-v))
 
@@ -37,6 +33,18 @@
 
 def swap(copies, axis, groups=None):
     return lax.all_to_all(copies, axis, 0, 0, tiled=True, axis_index_groups=groups)
+
+
+def trade(block, axis, pairs):
+    return lax.ppermute(block, axis, pairs + [(b, a) for a, b in pairs])
+
+
+def gather_halves(rows, hosts, count):
+    for bit in (4, 2, 1):
+        pairs = [(i, i ^ bit) for i in range(hosts) if not i & bit]
+        theirs = trade(rows, "head", pairs)
+        rows = jnp.concatenate([rows, theirs], axis=0)
+    return rows, trade(rows, "tm", [(i, i + 1) for i in range(0, count, 2)])
 
 
 def copy_kernel(x_ref, out_ref):
@@ -59,15 +67,15 @@
     kv_ref[...] = rounded[width:]
 
 
-def attend_kernel(place_ref, q_ref, own_ref, low_ref, high_ref, ids_ref, out_ref):
+def attend_kernel(q_ref, own_ref, chip_ref, core_ref, ids_ref, out_ref):
     width, frames = q_ref.shape
     blocks = ids_ref.shape[0]
-    place = place_ref[0]
-    pieces = (low_ref, own_ref, high_ref)
+    place = lax.axis_index("tm")
+    pieces = (chip_ref, own_ref, core_ref)
     mine = ids_ref[pl.ds(place, 1), :]
+    side = 1 - 2 * lax.rem(place, 2)
     allowed = []
-    for k in range(3):
-        at = place + (k - 1)
+    for at in (place - side, place, place + side):
         ids = ids_ref[pl.ds(jnp.clip(at, 0, blocks - 1), 1), :]
         ids = jnp.where((at >= 0) & (at < blocks), ids, -1.0)
         column = jnp.broadcast_to(ids, (8, frames)).T[:, 0:1]
@@ -134,15 +142,7 @@
     return dot(first, narrow, dims) + dot(second, narrow, dims)
 
 
-def state_kernel(
-    skip_ref, scaled_ref, weight_ref, coupler_ref, decay_ref, base_ref, grow_ref, c_ref, out_ref
-):
-    scaled = scaled_ref[...]
-    inputs = silu(dot(weight_ref[...], scaled, ((1,), (1,)))).astype(BF16)
-    couplers = jnp.concatenate([coupler_ref[k] for k in range(coupler_ref.shape[0])], axis=1)
-    b_in = couplers[:, :NSTATE]
-    c_in = couplers[:, NSTATE:]
-    c_ref[...] = c_in
+def decay_kernel(decay_ref, skip_ref, weight_ref, diagonal_ref, tail_ref, grow_ref, ends_ref):
     decay = decay_ref[...]
     heads, tokens = decay.shape
     log_decay = jnp.log(jnp.maximum(decay, SMALLEST))
@@ -153,25 +153,74 @@
     cumulative = dot(below, log_decay, ((1,), (1,)), precision=HIGHEST)
     across = dot(log_decay, below, ((1,), (1,)), precision=HIGHEST)
     grow_ref[...] = jnp.exp(cumulative)
-    affinity = dot(c_in, b_in, ((1,), (1,)))
     given = 1.0 - decay
     last = across[:, tokens - 1 : tokens]
-    tail = jnp.exp(last - across) * given
+    tail_ref[...] = jnp.exp(last - across) * given
+    for h in range(heads):
+        gap = jnp.where(causal, cumulative[:, h : h + 1] - across[h : h + 1, :], -1e30)
+        weight_ref[h] = jnp.exp(gap) * given[h : h + 1, :]
+        diagonal_ref[h] = jnp.where(late == early, skip_ref[:, h : h + 1], 0.0)
+    ends = jnp.concatenate([jnp.exp(last), jnp.zeros((8 - heads, 1), F32)], axis=0)
+    ends_ref[...] = split_rows(jnp.broadcast_to(ends, (8, NSTATE)))
+
+
+def fetch(sources, targets, sems):
+    moves = [
+        pltpu.make_async_copy(source, target, sems.at[k])
+        for k, (source, target) in enumerate(zip(sources, targets))
+    ]
+    for move in moves:
+        move.start()
+    return moves
+
+
+def state_kernel(
+    scaled_ref,
+    x_ref,
+    weight_ref,
+    diagonal_ref,
+    tail_ref,
+    ends_ref,
+    far_half_ref,
+    far_other_ref,
+    base_ref,
+    c_ref,
+    out_ref,
+    half_ref,
+    other_ref,
+    sems,
+):
+    moves = fetch((far_half_ref, far_other_ref), (half_ref, other_ref), sems)
+    scaled = scaled_ref[...]
+    inputs = silu(dot(x_ref[...], scaled, ((1,), (1,)))).astype(BF16)
+    for move in moves:
+        move.wait()
+    mine = silu(dot(scaled, half_ref[...], ((1,), (1,))))
+    other = silu(dot(scaled, other_ref[...], ((1,), (1,))))
+    odd_core = lax.rem(lax.axis_index("tm"), 2) == 1
+    flipped = lax.axis_index("head") >= lax.axis_size("head") // 2
+    first = jnp.where(odd_core, other, mine)
+    second = jnp.where(odd_core, mine, other)
+    step = NSTATE // 8
+    lane = lax.broadcasted_iota(jnp.int32, first.shape, 1)
+    even = lax.rem(lax.div(lane, step), 2) == 0
+    one = jnp.where(even, first, pltpu.roll(second, step, 1))
+    two = jnp.where(even, pltpu.roll(first, NSTATE - step, 1), second)
+    b_in = jnp.where(flipped, two, one).astype(BF16)
+    c_in = jnp.where(flipped, one, two).astype(BF16)
+    c_ref[...] = c_in
+    affinity = dot(c_in, b_in, ((1,), (1,)))
     states = []
-    for h in range(heads):
+    for h in range(weight_ref.shape[0]):
         cols = slice(h * HDIM, (h + 1) * HDIM)
-        gap = jnp.where(causal, cumulative[:, h : h + 1] - across[h : h + 1, :], -1e30)
-        weights = affinity * jnp.exp(gap) * given[h : h + 1, :]
-        weights = jnp.where(late == early, weights + skip_ref[h], weights)
+        weights = affinity * weight_ref[h] + diagonal_ref[h]
         base_ref[:, cols] = twice(weights, inputs[cols, :], ((1,), (1,)))
-        driven = inputs[cols, :].astype(F32) * tail[h : h + 1, :]
+        driven = inputs[cols, :].astype(F32) * tail_ref[h : h + 1, :]
         states.append(twice(driven, b_in))
-    ends = jnp.concatenate([jnp.exp(last), jnp.zeros((8 - heads, 1), F32)], axis=0)
-    ends = split_rows(jnp.broadcast_to(ends, (8, NSTATE)))
     state = jnp.concatenate(states, axis=0)
     share = state.shape[0] // GROUP
     for j in range(GROUP):
-        piece = jnp.concatenate([state[j * share : (j + 1) * share], ends], axis=0)
+        piece = jnp.concatenate([state[j * share : (j + 1) * share], ends_ref[...]], axis=0)
         out_ref[j] = piece.astype(BF16)
 
 
@@ -187,9 +236,9 @@
     return lax.shift_right_logical(rows, HDIM.bit_length() - 1)
 
 
-def near_kernel(place_ref, got_ref, out_ref, *, heads):
+def near_kernel(got_ref, out_ref, *, heads):
     share = got_ref.shape[1] - 8
-    lane = lax.rem(place_ref[0], GROUP)
+    lane = lax.rem(lax.axis_index("tm"), GROUP)
     row_head = row_heads(lane, share)
     state = jnp.zeros((share, NSTATE), F32)
     grown = jnp.ones((8, 1), F32)
@@ -205,10 +254,10 @@
         out_ref[j] = value
 
 
-def far_kernel(place_ref, got_ref, total_ref, out_ref, *, heads):
+def far_kernel(got_ref, total_ref, out_ref, *, heads):
     share = got_ref.shape[1] - 8
-    lane = lax.rem(place_ref[0], GROUP)
-    group = lax.div(place_ref[0], GROUP)
+    lane = lax.rem(lax.axis_index("tm"), GROUP)
+    group = lax.div(lax.axis_index("tm"), GROUP)
     row_head = row_heads(lane, share)
     before = jnp.zeros((share, NSTATE), F32)
     for k in range(total_ref.shape[0]):
@@ -232,21 +281,25 @@
         out_ref[:, cols] = value.astype(BF16)
 
 
-def call(kernel, outs, *operands, scalars=0):
-    placed = [
-        x if k < scalars else pltpu.with_memory_space_constraint(x, pltpu.VMEM)
-        for k, x in enumerate(operands)
-    ]
-    spaces = [pltpu.SMEM if k < scalars else pltpu.VMEM for k in range(len(operands))]
-    many = isinstance(outs[0][0], tuple)
+def call(kernel, outs, *operands, late=(), final=False):
+    vmem = pl.BlockSpec(memory_space=pltpu.VMEM)
+    scratch = [pltpu.VMEM(x.shape, x.dtype) for x in late]
+    if late:
+        scratch.append(pltpu.SemaphoreType.DMA((len(late),)))
     made = pl.pallas_call(
         kernel,
-        out_shape=tuple(pltpu.VMEM(dims, kind) for dims, kind in (outs if many else (outs,))),
-        in_specs=[pl.BlockSpec(memory_space=space) for space in spaces],
-        out_specs=tuple(pl.BlockSpec(memory_space=pltpu.VMEM) for _ in (outs if many else (outs,))),
-        compiler_params=pltpu.CompilerParams(vmem_limit_bytes=24 << 20),
-    )(*placed)
-    return made if many else made[0]
+        out_shape=tuple(
+            jax.ShapeDtypeStruct(dims, kind) if final else pltpu.VMEM(dims, kind)
+            for dims, kind in outs
+        ),
+        in_specs=[vmem for _ in operands] + [pl.BlockSpec(memory_space=pltpu.HBM) for _ in late],
+        out_specs=tuple(vmem for _ in outs),
+        scratch_shapes=scratch,
+        compiler_params=pltpu.CompilerParams(vmem_limit_bytes=16 << 20),
+    )(*[pltpu.with_memory_space_constraint(x, pltpu.VMEM) for x in operands],
+        *[pltpu.with_memory_space_constraint(x, pltpu.HBM) for x in late],
+    )
+    return made if len(outs) > 1 else made[0]
 
 
 def per_device(
@@ -273,84 +326,97 @@
     model = adapter.shape[1]
     tokens, heads = decay.shape
     per = tokens // hosts
-    where = place[None].astype(jnp.int32)
 
     across = frames.T
-    copies = call(copy_kernel, ((hosts, share, frame_count), BF16), across)
+    copies = call(copy_kernel, (((hosts, share, frame_count), BF16),), across)
     gathered = swap(copies, "head")
+    lanes = bc_weight.shape[1] // 2
+    half = lax.dynamic_slice_in_dim(bc_weight.T, lax.rem(place, 2) * lanes, lanes, 0)
+    half, other = gather_halves(half, hosts, count)
+    turned = jnp.transpose(qkv_weight, (0, 2, 1)).reshape(3 * head_width, features)
     queries, own = call(
         qkv_kernel,
         (((head_width, frame_count), BF16), ((2 * head_width, frame_count), BF16)),
         gathered,
         ln_gain[:, None],
         ln_bias[:, None],
-        jnp.transpose(qkv_weight, (0, 2, 1)).reshape(3 * head_width, features),
-    )
-    low = lax.ppermute(own, "tm", [(i, i + 1) for i in range(count - 1)])
-    high = lax.ppermute(own, "tm", [(i + 1, i) for i in range(count - 1)])
+        turned,
+    )
+    chip = trade(own, "tm", [(i, i + 1) for i in range(1, count - 1, 2)])
+    core = trade(own, "tm", [(i, i + 1) for i in range(0, count, 2)])
     attended = call(
         attend_kernel,
-        ((hosts, head_width, frame_count), BF16),
-        where,
+        (((hosts, head_width, frame_count), BF16),),
         queries,
         own,
-        low,
-        high,
+        chip,
+        core,
         segment_ids.astype(F32).reshape(count, frame_count),
-        scalars=1,
-    )
+    )
+    attended = swap(attended, "head")
     encoded, parts = call(
         encode_kernel,
         (((share, frame_count), BF16), ((hosts, per, model), BF16)),
-        swap(attended, "head"),
+        attended,
         out_weight.T,
         across,
         out_bias[:, None],
         adapter,
     )
-    scaled = call(
-        scale_kernel, ((hosts, per, model), BF16), swap(parts, "head"), rms_gain[None, :]
-    )
-    scaled = swap(scaled, "head").reshape(tokens, model)
-    coupler_part = jax.nn.silu(jnp.dot(scaled, bc_weight, preferred_element_type=F32)).astype(BF16)
-    couplers = swap(jnp.broadcast_to(coupler_part[None], (hosts,) + coupler_part.shape), "head")
-
+    parts = swap(parts, "head")
+    scaled = call(scale_kernel, (((hosts, per, model), BF16),), parts, rms_gain[None, :])
+    scaled = swap(scaled, "head")
+    scaled = scaled.reshape(tokens, model)
     rows = heads * HDIM // GROUP
-    base, grow, c_rows, ends = call(
+    weights, diagonal, tail, grow, ends = call(
+        decay_kernel,
+        (
+            ((heads, tokens, tokens), F32),
+            ((heads, tokens, tokens), F32),
+            ((heads, tokens), F32),
+            ((tokens, heads), F32),
+            ((8, NSTATE), F32),
+        ),
+        decay.T,
+        skip_gain[None, :],
+    )
+    base, c_rows, ends = call(
         state_kernel,
         (
             ((tokens, heads * HDIM), F32),
-            ((tokens, heads), F32),
             ((tokens, NSTATE), BF16),
             ((GROUP, rows + 8, NSTATE), BF16),
         ),
-        skip_gain,
         scaled,
         x_weight.T,
-        couplers,
-        decay.T,
-        scalars=1,
+        weights,
+        diagonal,
+        tail,
+        ends,
+        late=(half, other),
     )
     near = [[first + k for k in range(GROUP)] for first in range(0, count, GROUP)]
     far = [[lane + GROUP * k for k in range(count // GROUP)] for lane in range(GROUP)]
     got = swap(ends, "tm", near)
     totals = call(
         functools.partial(near_kernel, heads=heads),
-        ((count // GROUP, rows + 8, NSTATE), BF16),
-        where,
+        (((count // GROUP, rows + 8, NSTATE), BF16),),
         got,
-        scalars=1,
     )
     entering = call(
         functools.partial(far_kernel, heads=heads),
-        ((GROUP, rows, NSTATE), BF16),
-        where,
+        (((GROUP, rows, NSTATE), BF16),),
         got,
         swap(totals, "tm", far),
-        scalars=1,
     )
     mixed = call(
-        final_kernel, ((tokens, heads * HDIM), BF16), swap(entering, "tm", near), c_rows, base, grow
+        final_kernel,
+        (((tokens, heads * HDIM), BF16),),
+        swap(entering, "tm", near),
+        c_rows,
+        base,
+        grow,
+        final=True,
     )
     return (encoded.T, mixed)
 
@@ -371,6 +437,7 @@
         P("tm", "head"),
         P("head"),
     )
+
     return jax.shard_map(
         per_device,
         mesh=mesh,

time: 140 us -> 140 us (level)
  blocking collectives: 60.7 us -> 37.5 us
  starting transfers between devices: 29.9 us -> 49.9 us
  Pallas kernels: 8.33 us -> 11.9 us
  waiting for transfers between devices: 35 us -> 32.2 us
  other arithmetic: 0.01 us -> 1.8 us
    all_to_all x4 -> x2, blocking collectives: 60.7 us -> 37.5 us  [swap(): lax.all_to_all(copies, axis, 0, 0, tiled=True, axis_index_groups=groups)]
    ppermute x2 -> x6, starting transfers between devices: 9.19 us -> 26 us  [trade(): return lax.ppermute(block, axis, pairs + [(b, a) for a, b in pairs])]
    pallas_call x9 -> x10, Pallas kernels: 8.33 us -> 11.9 us  [call(): pl.pallas_call(kernel, out_shape=tuple((jax.ShapeDtypeStruct(dims, kind)...]
    all_to_all x4 -> x5, starting transfers between devices: 20.7 us -> 23.9 us  [swap(): lax.all_to_all(copies, axis, 0, 0, tiled=True, axis_index_groups=groups)]
    concatenate x0 -> x3, other arithmetic: none -> 1.79 us  [gather_halves(): rows = jnp.concatenate([rows, theirs], axis=0)]
    all_to_all x4 -> x5, waiting for transfers between devices: 30.7 us -> 29.1 us  [swap(): lax.all_to_all(copies, axis, 0, 0, tiled=True, axis_index_groups=groups)]
    ppermute x2 -> x6, waiting for transfers between devices: 4.29 us -> 3.08 us  [trade(): return lax.ppermute(block, axis, pairs + [(b, a) for a, b in pairs])]
  transfers between devices with their start and end apart: 6 -> 11, of which waited for: 5 -> 8; matrix products, arithmetic and copies ran while one was open for 1% -> 3% of each run, Pallas kernels for 0% -> 5%
where the time goes in v4:
time: 140 us; the launch traced here: 139 us
  starting transfers between devices  49.9 us (36%)
  blocking collectives  37.5 us (27%)
  waiting for transfers between devices  32.2 us (23%)
  Pallas kernels  11.9 us (8%)
  local copies, waits for them, and re-layouts  4.63 us (3%)
  other arithmetic  1.8 us (1%)
    all_to_all x2, blocking collectives, swap(): lax.all_to_all(copies, axis, 0, 0, tiled=True, axis_index_groups=groups)  37.5 us
    all_to_all x5, waiting for transfers between devices, swap(): lax.all_to_all(copies, axis, 0, 0, tiled=True, axis_index_groups=groups)  29.1 us
    ppermute x6, starting transfers between devices, trade(): return lax.ppermute(block, axis, pairs + [(b, a) for a, b in pairs])  26 us
    all_to_all x5, starting transfers between devices, swap(): lax.all_to_all(copies, axis, 0, 0, tiled=True, axis_index_groups=groups)  23.9 us
    pallas_call x10, Pallas kernels, call(): pl.pallas_call(kernel, out_shape=tuple((jax.ShapeDtypeStruct(dims, kind)...  11.9 us
    ppermute x6, waiting for transfers between devices, trade(): return lax.ppermute(block, axis, pairs + [(b, a) for a, b in pairs])  3.08 us
  transfers between devices with their start and end apart: 11, of which 8 were waited for; matrix products, arithmetic and copies ran while one was open for 3% of the time, Pallas kernels for 5%

profile of v4, /device:TPU:1, one launch (start us, length us, event | category | flops | bytes accessed | tf_op | source)
XLA Modules:
  0.0 138.8 jit_solution(18148128764382546966)
XLA Ops:
  0.6 0.0 copy-start
  0.7 0.9 copy-done
  1.6 5.5 %collective-permute-start.2 = (bf16[16,2560]{1,0:T(8,128)(2,1)S(1)}, bf16[16,2560]{1,0:T(8,128)(2,1)S(1)}, u32[]{:S(2)}, u32[]{:S(2)}) collective-permute-start(bf16[16,2560]{1,0:T(8,128)(2,1)S(1)} %dynamic-slice_bitcast_fusion), channel_id=1, source_target_pairs={{0,4},{1,5},{2,6},{3,7},{4,0},{5,1},{6,2},{7,3},{8,12},{9,13},{10,... | collective-permute-start | bytes 245768 | tf_op jit(solution)/shard_map/ppermute | solution.py:39
  7.0 1.8 %collective-permute-done.2 = bf16[16,2560]{1,0:T(8,128)(2,1)S(1)} collective-permute-done((bf16[16,2560]{1,0:T(8,128)(2,1)S(1)}, bf16[16,2560]{1,0:T(8,128)(2,1)S(1)}, u32[]{:S(2)}, u32[]{:S(2)}) %collective-permute-start.2) | collective-permute-done | bytes 81952 | tf_op jit(solution)/shard_map/ppermute | solution.py:39
  8.9 5.0 %collective-permute-start.3 = (bf16[32,2560]{1,0:T(8,128)(2,1)S(1)}, bf16[32,2560]{1,0:T(8,128)(2,1)S(1)}, u32[]{:S(2)}, u32[]{:S(2)}) collective-permute-start(bf16[32,2560]{1,0:T(8,128)(2,1)S(1)} %pad_maximum_fusion.2), channel_id=1, source_target_pairs={{0,2},{1,3},{4,6},{5,7},{2,0},{3,1},{6,4},{7,5},{8,10},{9,11},{12,... | collective-permute-start | bytes 491528 | tf_op jit(solution)/shard_map/ppermute | solution.py:39
  13.9 0.0 copy-start.4
  13.9 0.9 copy-done.4
  14.8 0.9 shard_map.140
  15.7 4.6 %all-to-all-start = ((bf16[8,160,256]{2,1,0:T(8,128)(2,1)}), bf16[8,160,256]{2,1,0:T(8,128)(2,1)S(1)}, u32[]{:S(2)}, u32[]{:S(2)}) async-start(bf16[8,160,256]{2,1,0:T(8,128)(2,1)} %shard_map.140), calls=%async_computation | async-start | bytes 1310720 | tf_op jit(solution)/shard_map/all_to_all | solution.py:35
  20.3 0.0 collective-permute-done.3
  20.3 0.0 copy-start.9
  20.3 0.8 pad_maximum_fusion.1
  21.1 3.4 %collective-permute-start.4 = (bf16[64,2560]{1,0:T(8,128)(2,1)}, bf16[64,2560]{1,0:T(8,128)(2,1)}, u32[]{:S(2)}, u32[]{:S(2)}) collective-permute-start(bf16[64,2560]{1,0:T(8,128)(2,1)} %pad_maximum_fusion.1), channel_id=1, source_target_pairs={{0,1},{2,3},{4,5},{6,7},{1,0},{3,2},{5,4},{7,6},{8,9},{10,11},{12,... | collective-permute-start | bytes 983048 | tf_op jit(solution)/shard_map/ppermute | solution.py:39
  24.5 0.2 broadcast_in_dim.20.gain_ref
  24.7 0.2 broadcast_in_dim.21.bias_ref
  24.9 1.6 %copy.16 = bf16[3,128,1280]{2,1,0:T(8,128)(2,1)S(1)} copy(bf16[3,128,1280]{1,2,0:T(8,128)(2,1)} %bitcast.21) | data formatting | bytes 1966080 | tf_op jit(solution)/shard_map/transpose | solution.py:336
  26.5 3.0 %all-to-all-done.x_ref = bf16[8,160,256]{2,1,0:T(8,128)(2,1)S(1)} async-done(((bf16[8,160,256]{2,1,0:T(8,128)(2,1)}), bf16[8,160,256]{2,1,0:T(8,128)(2,1)S(1)}, u32[]{:S(2)}, u32[]{:S(2)}) %all-to-all-start) | async-done | bytes 655392 | tf_op jit(solution)/shard_map/all_to_all | solution.py:35
  29.5 1.0 shard_map.141
  30.6 7.8 %collective-permute-start = (bf16[256,256]{1,0:T(8,128)(2,1)S(1)}, bf16[256,256]{1,0:T(8,128)(2,1)S(1)}, u32[]{:S(2)}, u32[]{:S(2)}) collective-permute-start(bf16[256,256]{1,0:T(8,128)(2,1)S(1)} %get-tuple-element.15.own_ref), channel_id=1, source_target_pairs={{8,16},{24,32},{40,48},{56,64},{72,80},{88,96},{104,112},{120,128}... | collective-permute-start | bytes 393224 | tf_op jit(solution)/shard_map/ppermute | solution.py:39
  38.4 1.9 %collective-permute-start.1 = (bf16[256,256]{1,0:T(8,128)(2,1)S(1)}, bf16[256,256]{1,0:T(8,128)(2,1)S(1)}, u32[]{:S(2)}, u32[]{:S(2)}) collective-permute-start(bf16[256,256]{1,0:T(8,128)(2,1)S(1)} %get-tuple-element.15.own_ref), channel_id=1, source_target_pairs={{0,8},{16,24},{32,40},{48,56},{64,72},{80,88},{96,104},{112,120},{... | collective-permute-start | bytes 393224 | tf_op jit(solution)/shard_map/ppermute | solution.py:39
  40.4 0.7 collective-permute-done.chip_ref
  41.0 0.6 collective-permute-done.1.core_ref
  41.6 2.0 %shard_map.142 = bf16[8,128,256]{2,1,0:T(8,128)(2,1)} custom-call(bf16[128,256]{1,0:T(8,128)(2,1)S(1)} %get-tuple-element.14.q_ref, bf16[256,256]{1,0:T(8,128)(2,1)S(1)} %get-tuple-element.15.own_ref, bf16[256,256]{1,0:T(8,128)(2,1)S(1)} %collective-permute-done.chip_ref, bf16[256,256]{1,0:T(8,128)(2,1)S(1)} %collective-permute-done.1.core_ref, ...), custom_call_target="tpu_custom_call" | custom-call | tf_op jit(solution)/shard_map/pallas_call | solution.py:289
  43.6 4.2 %all-to-all-start.1 = ((bf16[8,128,256]{2,1,0:T(8,128)(2,1)}), bf16[8,128,256]{2,1,0:T(8,128)(2,1)S(1)}, u32[]{:S(2)}, u32[]{:S(2)}) async-start(bf16[8,128,256]{2,1,0:T(8,128)(2,1)} %shard_map.142), calls=%async_computation.1 | async-start | bytes 1048576 | tf_op jit(solution)/shard_map/all_to_all | solution.py:35
  47.8 0.0 collective-permute-done.4
  47.8 1.0 pad_maximum_fusion.far_half_ref
  48.8 0.0 copy-start.12
  48.8 2.5 %collective-permute-start.5 = (bf16[128,2560]{1,0:T(8,128)(2,1)S(1)}, bf16[128,2560]{1,0:T(8,128)(2,1)}, u32[]{:S(2)}, u32[]{:S(2)}) collective-permute-start(bf16[128,2560]{1,0:T(8,128)(2,1)S(1)} %pad_maximum_fusion.far_half_ref), channel_id=1, source_target_pairs={{0,8},{16,24},{32,40},{48,56},{64,72},{80,88},{96,104},{112,120},{... | collective-permute-start | bytes 1966088 | tf_op jit(solution)/shard_map/ppermute | solution.py:39
  51.3 0.1 copy.19.bias_ref
  51.4 6.2 %all-to-all-done.1.att_ref = bf16[8,128,256]{2,1,0:T(8,128)(2,1)S(1)} async-done(((bf16[8,128,256]{2,1,0:T(8,128)(2,1)}), bf16[8,128,256]{2,1,0:T(8,128)(2,1)S(1)}, u32[]{:S(2)}, u32[]{:S(2)}) %all-to-all-start.1) | async-done | bytes 524320 | tf_op jit(solution)/shard_map/all_to_all | solution.py:35
  57.6 1.5 %shard_map.143 = (bf16[160,256]{1,0:T(8,128)(2,1)S(1)}, bf16[8,8,2560]{2,1,0:T(8,128)(2,1)}) custom-call(bf16[8,128,256]{2,1,0:T(8,128)(2,1)S(1)} %all-to-all-done.1.att_ref, bf16[160,1024]{1,0:T(8,128)(2,1)S(1)} %bitcast.16, bf16[160,256]{1,0:T(8,128)(2,1)S(1)} %bitcast.18, f32[160,1]{1,0:T(8,128)S(1)} %copy.19.bias_ref, bf16[160,2560]{1,0:T(8,128)(2,1)S(1)} %copy-done.2), custom_call_target="tpu_custom_call" | custom-call | tf_op jit(solution)/shard_map/pallas_call | solution.py:289
  59.1 4.8 %all-to-all-start.2 = ((bf16[8,8,2560]{2,1,0:T(8,128)(2,1)}), bf16[8,8,2560]{2,1,0:T(8,128)(2,1)S(1)}, u32[]{:S(2)}, u32[]{:S(2)}) async-start(bf16[8,8,2560]{2,1,0:T(8,128)(2,1)} %get-tuple-element.17), calls=%async_computation.2 | async-start | bytes 655360 | tf_op jit(solution)/shard_map/all_to_all | solution.py:35
  63.9 7.8 %all-to-all-done.2.part_ref = bf16[8,8,2560]{2,1,0:T(8,128)(2,1)S(1)} async-done(((bf16[8,8,2560]{2,1,0:T(8,128)(2,1)}), bf16[8,8,2560]{2,1,0:T(8,128)(2,1)S(1)}, u32[]{:S(2)}, u32[]{:S(2)}) %all-to-all-start.2) | async-done | bytes 327712 | tf_op jit(solution)/shard_map/all_to_all | solution.py:35
  71.7 0.9 shard_map.144
  72.6 4.3 %all-to-all-start.3 = ((bf16[8,8,2560]{2,1,0:T(8,128)(2,1)}), bf16[8,8,2560]{2,1,0:T(8,128)(2,1)S(1)}, u32[]{:S(2)}, u32[]{:S(2)}) async-start(bf16[8,8,2560]{2,1,0:T(8,128)(2,1)} %shard_map.144), calls=%async_computation.3 | async-start | bytes 655360 | tf_op jit(solution)/shard_map/all_to_all | solution.py:35
  76.9 0.0 copy-done.6
  77.0 0.3 shard_map.145
  77.3 0.0 collective-permute-done.5.far_other_ref
  77.3 7.5 %all-to-all-done.3 = bf16[8,8,2560]{2,1,0:T(8,128)(2,1)S(1)} async-done(((bf16[8,8,2560]{2,1,0:T(8,128)(2,1)}), bf16[8,8,2560]{2,1,0:T(8,128)(2,1)S(1)}, u32[]{:S(2)}, u32[]{:S(2)}) %all-to-all-start.3) | async-done | bytes 327712 | tf_op jit(solution)/shard_map/all_to_all | solution.py:35
  84.8 3.5 %shard_map.146 = (f32[64,320]{1,0:T(8,128)S(1)}, bf16[64,128]{1,0:T(8,128)(2,1)S(1)}, bf16[8,48,128]{2,1,0:T(8,128)(2,1)S(1)}) custom-call(bf16[64,2560]{1,0:T(8,128)(2,1)S(1)} %bitcast.15, bf16[320,2560]{1,0:T(8,128)(2,1)S(1)} %bitcast.14, f32[5,64,64]{2,1,0:T(8,128)S(1)} %get-tuple-element.18.weight_ref, f32[5,64,64]{2,1,0:T(8,128)S(1)} %get-tuple-element.19.diagonal_ref, ...), custom_call_target="tpu_custom_call" | custom-call | tf_op jit(solution)/shard_map/pallas_call | solution.py:289
  88.3 14.9 %all_to_all.35.got_ref = bf16[8,48,128]{2,1,0:T(8,128)(2,1)S(1)} all-to-all(bf16[8,48,128]{2,1,0:T(8,128)(2,1)S(1)} %get-tuple-element.22), channel_id=1, replica_groups={{0,8,16,24,32,40,48,56},{64,72,80,88,96,104,112,120},{128,136,144,152,1..., dimensions={0} | all-to-all | bytes 196608 | tf_op jit(solution)/shard_map/all_to_all | solution.py:35
  103.2 0.2 shard_map.147
  103.4 22.6 %all_to_all.36.total_ref = bf16[8,48,128]{2,1,0:T(8,128)(2,1)S(1)} all-to-all(bf16[8,48,128]{2,1,0:T(8,128)(2,1)S(1)} %shard_map.147), channel_id=1, replica_groups={{0,64,128,192,256,320,384,448},{8,72,136,200,264,328,392,456},{16,80,14..., dimensions={0} | all-to-all | bytes 196608 | tf_op jit(solution)/shard_map/all_to_all | solution.py:35
  126.0 0.9 shard_map.148
  126.9 6.0 %all-to-all-start.6 = ((bf16[8,40,128]{2,1,0:T(8,128)(2,1)}), bf16[8,40,128]{2,1,0:T(8,128)(2,1)S(1)}, u32[]{:S(2)}, u32[]{:S(2)}) async-start(bf16[8,40,128]{2,1,0:T(8,128)(2,1)} %shard_map.148), calls=%async_computation.6 | async-start | bytes 163840 | tf_op jit(solution)/shard_map/all_to_all | solution.py:35
  132.8 0.6 copy.20
  133.5 4.5 %all-to-all-done.6.state_ref = bf16[8,40,128]{2,1,0:T(8,128)(2,1)S(1)} async-done(((bf16[8,40,128]{2,1,0:T(8,128)(2,1)}), bf16[8,40,128]{2,1,0:T(8,128)(2,1)S(1)}, u32[]{:S(2)}, u32[]{:S(2)}) %all-to-all-start.6) | async-done | bytes 81952 | tf_op jit(solution)/shard_map/all_to_all | solution.py:35
  138.0 0.8 shard_map.149
  (30 shorter events, 0.1 us)
Async XLA Ops:
  0.6 0.9 copy-start
  1.6 7.3 %collective-permute-start.2 = (bf16[16,2560]{1,0:T(8,128)(2,1)S(1)}, bf16[16,2560]{1,0:T(8,128)(2,1)S(1)}, u32[]{:S(2)}, u32[]{:S(2)}) collective-permute-start(bf16[16,2560]{1,0:T(8,128)(2,1)S(1)} %dynamic-slice_bitcast_fusion), channel_id=1, source_target_pairs={{0,4},{1,5},{2,6},{3,7},{4,0},{5,1},{6,2},{7,3},{8,12},{9,13},{10,... | collective-permute-start | bytes 245768 | tf_op jit(solution)/shard_map/ppermute | solution.py:39
  8.9 11.5 %collective-permute-start.3 = (bf16[32,2560]{1,0:T(8,128)(2,1)S(1)}, bf16[32,2560]{1,0:T(8,128)(2,1)S(1)}, u32[]{:S(2)}, u32[]{:S(2)}) collective-permute-start(bf16[32,2560]{1,0:T(8,128)(2,1)S(1)} %pad_maximum_fusion.2), channel_id=1, source_target_pairs={{0,2},{1,3},{4,6},{5,7},{2,0},{3,1},{6,4},{7,5},{8,10},{9,11},{12,... | collective-permute-start | bytes 491528 | tf_op jit(solution)/shard_map/ppermute | solution.py:39
  13.9 0.9 copy-start.4
  14.8 9.7 %copy-start.13 = (f32[1280]{0:T(1024)S(1)}, f32[1280]{0:T(1024)}, u32[]{:S(2)}) copy-start(f32[1280]{0:T(1024)} %param.15) | copy-start | bytes 15364
  15.7 9.0 %copy-start.14 = (f32[1280]{0:T(1024)S(1)}, f32[1280]{0:T(1024)}, u32[]{:S(2)}) copy-start(f32[1280]{0:T(1024)} %param.16) | copy-start | bytes 15364
  15.7 13.9 %all-to-all-start = ((bf16[8,160,256]{2,1,0:T(8,128)(2,1)}), bf16[8,160,256]{2,1,0:T(8,128)(2,1)S(1)}, u32[]{:S(2)}, u32[]{:S(2)}) async-start(bf16[8,160,256]{2,1,0:T(8,128)(2,1)} %shard_map.140), calls=%async_computation | async-start | bytes 1310720 | tf_op jit(solution)/shard_map/all_to_all | solution.py:35
  20.3 6.2 %copy-start.9 = (bf16[32,2560]{1,0:T(8,128)(2,1)}, bf16[32,2560]{1,0:T(8,128)(2,1)S(1)}, u32[]{:S(2)}) copy-start(bf16[32,2560]{1,0:T(8,128)(2,1)S(1)} %collective-permute-done.3) | copy-start | bytes 491524
  21.1 26.7 %collective-permute-start.4 = (bf16[64,2560]{1,0:T(8,128)(2,1)}, bf16[64,2560]{1,0:T(8,128)(2,1)}, u32[]{:S(2)}, u32[]{:S(2)}) collective-permute-start(bf16[64,2560]{1,0:T(8,128)(2,1)} %pad_maximum_fusion.1), channel_id=1, source_target_pairs={{0,1},{2,3},{4,5},{6,7},{1,0},{3,2},{5,4},{7,6},{8,9},{10,11},{12,... | collective-permute-start | bytes 983048 | tf_op jit(solution)/shard_map/ppermute | solution.py:39
  29.5 10.8 %copy-start.11 = (s32[16384]{0:T(1024)S(1)}, s32[16384]{0:T(1024)}, u32[]{:S(2)}) copy-start(s32[16384]{0:T(1024)} %param.14) | copy-start | bytes 196612
  30.5 17.2 %copy-start.10 = (bf16[32,2560]{1,0:T(8,128)(2,1)S(1)}, bf16[32,2560]{1,0:T(8,128)(2,1)}, u32[]{:S(2)}) copy-start(bf16[32,2560]{1,0:T(8,128)(2,1)} %copy-done.9) | copy-start | bytes 491524
  30.6 10.4 %collective-permute-start = (bf16[256,256]{1,0:T(8,128)(2,1)S(1)}, bf16[256,256]{1,0:T(8,128)(2,1)S(1)}, u32[]{:S(2)}, u32[]{:S(2)}) collective-permute-start(bf16[256,256]{1,0:T(8,128)(2,1)S(1)} %get-tuple-element.15.own_ref), channel_id=1, source_target_pairs={{8,16},{24,32},{40,48},{56,64},{72,80},{88,96},{104,112},{120,128}... | collective-permute-start | bytes 393224 | tf_op jit(solution)/shard_map/ppermute | solution.py:39
  38.4 3.2 %collective-permute-start.1 = (bf16[256,256]{1,0:T(8,128)(2,1)S(1)}, bf16[256,256]{1,0:T(8,128)(2,1)S(1)}, u32[]{:S(2)}, u32[]{:S(2)}) collective-permute-start(bf16[256,256]{1,0:T(8,128)(2,1)S(1)} %get-tuple-element.15.own_ref), channel_id=1, source_target_pairs={{0,8},{16,24},{32,40},{48,56},{64,72},{80,88},{96,104},{112,120},{... | collective-permute-start | bytes 393224 | tf_op jit(solution)/shard_map/ppermute | solution.py:39
  43.6 7.7 %copy-start.15 = (f32[160]{0:T(256)S(1)}, f32[160]{0:T(256)}, u32[]{:S(2)}) copy-start(f32[160]{0:T(256)} %param.19) | copy-start | bytes 1924
  43.6 14.0 %copy-start.2 = (bf16[160,2560]{1,0:T(8,128)(2,1)S(1)}, bf16[160,2560]{1,0:T(8,128)(2,1)}, u32[]{:S(2)}) copy-start(bf16[160,2560]{1,0:T(8,128)(2,1)} %adapter_ref.1) | copy-start | bytes 2457604
  43.6 14.0 %copy-start.3 = (bf16[1024,160]{0,1:T(8,128)(2,1)S(1)}, bf16[1024,160]{0,1:T(8,128)(2,1)}, u32[]{:S(2)}) copy-start(bf16[1024,160]{0,1:T(8,128)(2,1)} %param.18) | copy-start | bytes 983044
  43.6 14.0 %copy-start.5 = (bf16[256,160]{0,1:T(8,128)(2,1)S(1)}, bf16[256,160]{0,1:T(8,128)(2,1)}, u32[]{:S(2)}) copy-start(bf16[256,160]{0,1:T(8,128)(2,1)} %param.13) | copy-start | bytes 245764
  43.6 14.0 %all-to-all-start.1 = ((bf16[8,128,256]{2,1,0:T(8,128)(2,1)}), bf16[8,128,256]{2,1,0:T(8,128)(2,1)S(1)}, u32[]{:S(2)}, u32[]{:S(2)}) async-start(bf16[8,128,256]{2,1,0:T(8,128)(2,1)} %shard_map.142), calls=%async_computation.1 | async-start | bytes 1048576 | tf_op jit(solution)/shard_map/all_to_all | solution.py:35
  48.8 23.8 %copy-start.8 = (bf16[128,2560]{1,0:T(8,128)(2,1)}, bf16[128,2560]{1,0:T(8,128)(2,1)S(1)}, u32[]{:S(2)}) copy-start(bf16[128,2560]{1,0:T(8,128)(2,1)S(1)} %pad_maximum_fusion.far_half_ref) | copy-start | bytes 1966084
  48.8 15.1 %copy-start.12 = (f32[2560]{0:T(1024)S(1)}, f32[2560]{0:T(1024)}, u32[]{:S(2)}) copy-start(f32[2560]{0:T(1024)} %param.21) | copy-start | bytes 30724
  48.8 28.5 %collective-permute-start.5 = (bf16[128,2560]{1,0:T(8,128)(2,1)S(1)}, bf16[128,2560]{1,0:T(8,128)(2,1)}, u32[]{:S(2)}, u32[]{:S(2)}) collective-permute-start(bf16[128,2560]{1,0:T(8,128)(2,1)S(1)} %pad_maximum_fusion.far_half_ref), channel_id=1, source_target_pairs={{0,8},{16,24},{32,40},{48,56},{64,72},{80,88},{96,104},{112,120},{... | collective-permute-start | bytes 1966088 | tf_op jit(solution)/shard_map/ppermute | solution.py:39
  59.1 17.9 %copy-start.6 = (f32[64,5]{0,1:T(8,128)S(1)}, f32[64,5]{0,1:T(8,128)}, u32[]{:S(2)}) copy-start(f32[64,5]{0,1:T(8,128)} %param.24) | copy-start | bytes 3844
  59.1 17.9 %copy-start.7 = (f32[5]{0:T(128)S(1)}, f32[5]{0:T(128)}, u32[]{:S(2)}) copy-start(f32[5]{0:T(128)} %param.25) | copy-start | bytes 64
  59.1 25.7 %copy-start.1 = (bf16[2560,320]{0,1:T(8,128)(2,1)S(1)}, bf16[2560,320]{0,1:T(8,128)(2,1)}, u32[]{:S(2)}) copy-start(bf16[2560,320]{0,1:T(8,128)(2,1)} %param.22) | copy-start | bytes 4915204
  59.1 12.6 %all-to-all-start.2 = ((bf16[8,8,2560]{2,1,0:T(8,128)(2,1)}), bf16[8,8,2560]{2,1,0:T(8,128)(2,1)S(1)}, u32[]{:S(2)}, u32[]{:S(2)}) async-start(bf16[8,8,2560]{2,1,0:T(8,128)(2,1)} %get-tuple-element.17), calls=%async_computation.2 | async-start | bytes 655360 | tf_op jit(solution)/shard_map/all_to_all | solution.py:35
  72.6 12.2 %all-to-all-start.3 = ((bf16[8,8,2560]{2,1,0:T(8,128)(2,1)}), bf16[8,8,2560]{2,1,0:T(8,128)(2,1)S(1)}, u32[]{:S(2)}, u32[]{:S(2)}) async-start(bf16[8,8,2560]{2,1,0:T(8,128)(2,1)} %shard_map.144), calls=%async_computation.3 | async-start | bytes 655360 | tf_op jit(solution)/shard_map/all_to_all | solution.py:35
  126.9 11.1 %all-to-all-start.6 = ((bf16[8,40,128]{2,1,0:T(8,128)(2,1)}), bf16[8,40,128]{2,1,0:T(8,128)(2,1)S(1)}, u32[]{:S(2)}, u32[]{:S(2)}) async-start(bf16[8,40,128]{2,1,0:T(8,128)(2,1)} %shard_map.148), calls=%async_computation.6 | async-start | bytes 163840 | tf_op jit(solution)/shard_map/all_to_all | solution.py:35

commit v5 on v4

--- a/solution.py
+++ b/solution.py
@@ -40,11 +40,19 @@
 
 
 def gather_halves(rows, hosts, count):
-    for bit in (4, 2, 1):
-        pairs = [(i, i ^ bit) for i in range(hosts) if not i & bit]
-        theirs = trade(rows, "head", pairs)
-        rows = jnp.concatenate([rows, theirs], axis=0)
-    return rows, trade(rows, "tm", [(i, i + 1) for i in range(0, count, 2)])
+    cores = [(i, i + 1) for i in range(0, count, 2)]
+
+    def across(block, bit):
+        return trade(block, "head", [(i, i ^ bit) for i in range(hosts) if not i & bit])
+
+    theirs = across(rows, 4)
+    rows = jnp.concatenate([rows, theirs], axis=0)
+    near = trade(rows, "tm", cores)
+    second = across(rows, 2)
+    rows = jnp.concatenate([rows, second], axis=0)
+    third = across(rows, 1)
+    later = jnp.concatenate([second, third], axis=0)
+    return rows, third, near, trade(later, "tm", cores)
 
 
 def copy_kernel(x_ref, out_ref):
@@ -116,10 +124,8 @@
     part_ref[...] = part.reshape(part_ref.shape).astype(BF16)
 
 
-def scale_kernel(part_ref, gain_ref, out_ref):
-    projected = jnp.sum(part_ref[...].astype(F32), axis=0)
-    spread = jnp.mean(jnp.square(projected), axis=-1, keepdims=True)
-    value = (projected * lax.rsqrt(spread + EPSILON) * gain_ref[...]).astype(BF16)
+def add_kernel(part_ref, out_ref):
+    value = jnp.sum(part_ref[...].astype(F32), axis=0).astype(BF16)
     for j in range(out_ref.shape[0]):
         out_ref[j] = value
 
@@ -136,13 +142,10 @@
     return parts[:, 0:1] + parts[:, 32:33] + parts[:, 64:65]
 
 
-def twice(wide, narrow, dims=((1,), (0,))):
-    first = wide.astype(BF16)
-    second = (wide - first.astype(F32)).astype(BF16)
-    return dot(first, narrow, dims) + dot(second, narrow, dims)
-
-
-def decay_kernel(decay_ref, skip_ref, weight_ref, diagonal_ref, tail_ref, grow_ref, ends_ref):
+def decay_kernel(
+    encoded_ref, decay_ref, skip_ref, written_ref, weight_ref, diagonal_ref, tail_ref, grow_ref, ends_ref
+):
+    written_ref[...] = encoded_ref[...]
     decay = decay_ref[...]
     heads, tokens = decay.shape
     log_decay = jnp.log(jnp.maximum(decay, SMALLEST))
@@ -175,14 +178,17 @@
 
 
 def state_kernel(
-    scaled_ref,
+    sums_ref,
+    gain_ref,
     x_ref,
     weight_ref,
     diagonal_ref,
     tail_ref,
     ends_ref,
-    far_half_ref,
-    far_other_ref,
+    rows_ref,
+    third_ref,
+    near_ref,
+    far_ref,
     base_ref,
     c_ref,
     out_ref,
@@ -190,34 +196,41 @@
     other_ref,
     sems,
 ):
-    moves = fetch((far_half_ref, far_other_ref), (half_ref, other_ref), sems)
-    scaled = scaled_ref[...]
+    targets = []
+    for ref, parts in ((half_ref, (rows_ref, third_ref)), (other_ref, (near_ref, far_ref))):
+        edge = parts[0].shape[0]
+        targets += [ref.at[pl.ds(0, edge)], ref.at[pl.ds(edge, parts[1].shape[0])]]
+    moves = fetch((rows_ref, third_ref, near_ref, far_ref), targets, sems)
+    count, per, model = sums_ref.shape
+    projected = sums_ref[: count // 2].astype(F32) + sums_ref[count // 2 :].astype(F32)
+    projected = projected.reshape(count // 2 * per, model)
+    spread = jnp.mean(jnp.square(projected), axis=-1, keepdims=True)
+    scaled = (projected * lax.rsqrt(spread + EPSILON) * gain_ref[...]).astype(BF16)
     inputs = silu(dot(x_ref[...], scaled, ((1,), (1,)))).astype(BF16)
     for move in moves:
         move.wait()
-    mine = silu(dot(scaled, half_ref[...], ((1,), (1,))))
-    other = silu(dot(scaled, other_ref[...], ((1,), (1,))))
+    mine = silu(dot(half_ref[...], scaled, ((1,), (1,))))
+    other = silu(dot(other_ref[...], scaled, ((1,), (1,))))
     odd_core = lax.rem(lax.axis_index("tm"), 2) == 1
     flipped = lax.axis_index("head") >= lax.axis_size("head") // 2
     first = jnp.where(odd_core, other, mine)
     second = jnp.where(odd_core, mine, other)
     step = NSTATE // 8
-    lane = lax.broadcasted_iota(jnp.int32, first.shape, 1)
-    even = lax.rem(lax.div(lane, step), 2) == 0
-    one = jnp.where(even, first, pltpu.roll(second, step, 1))
-    two = jnp.where(even, pltpu.roll(first, NSTATE - step, 1), second)
-    b_in = jnp.where(flipped, two, one).astype(BF16)
-    c_in = jnp.where(flipped, one, two).astype(BF16)
+    row = lax.broadcasted_iota(jnp.int32, first.shape, 0)
+    even = lax.rem(lax.div(row, step), 2) == 0
+    one = jnp.where(even, first, pltpu.roll(second, step, 0))
+    two = jnp.where(even, pltpu.roll(first, NSTATE - step, 0), second)
+    b_in = jnp.where(flipped, two, one).T.astype(BF16)
+    c_in = jnp.where(flipped, one, two).T.astype(BF16)
     c_ref[...] = c_in
     affinity = dot(c_in, b_in, ((1,), (1,)))
-    states = []
-    for h in range(weight_ref.shape[0]):
+    heads, tokens = tail_ref.shape
+    wide = inputs.astype(F32).reshape(heads, HDIM, tokens) * tail_ref[...].reshape(heads, 1, tokens)
+    state = dot(wide.reshape(heads * HDIM, tokens).astype(BF16), b_in)
+    for h in range(heads):
         cols = slice(h * HDIM, (h + 1) * HDIM)
-        weights = affinity * weight_ref[h] + diagonal_ref[h]
-        base_ref[:, cols] = twice(weights, inputs[cols, :], ((1,), (1,)))
-        driven = inputs[cols, :].astype(F32) * tail_ref[h : h + 1, :]
-        states.append(twice(driven, b_in))
-    state = jnp.concatenate(states, axis=0)
+        weights = (affinity * weight_ref[h] + diagonal_ref[h]).astype(BF16)
+        base_ref[:, cols] = dot(weights, inputs[cols, :], ((1,), (1,)))
     share = state.shape[0] // GROUP
     for j in range(GROUP):
         piece = jnp.concatenate([state[j * share : (j + 1) * share], ends_ref[...]], axis=0)
@@ -281,16 +294,16 @@
         out_ref[:, cols] = value.astype(BF16)
 
 
-def call(kernel, outs, *operands, late=(), final=False):
+def call(kernel, outs, *operands, late=(), scratch=(), final=0):
     vmem = pl.BlockSpec(memory_space=pltpu.VMEM)
-    scratch = [pltpu.VMEM(x.shape, x.dtype) for x in late]
+    scratch = [pltpu.VMEM(*buffer) for buffer in scratch]
     if late:
         scratch.append(pltpu.SemaphoreType.DMA((len(late),)))
     made = pl.pallas_call(
         kernel,
         out_shape=tuple(
-            jax.ShapeDtypeStruct(dims, kind) if final else pltpu.VMEM(dims, kind)
-            for dims, kind in outs
+            jax.ShapeDtypeStruct(dims, kind) if k < final else pltpu.VMEM(dims, kind)
+            for k, (dims, kind) in enumerate(outs)
         ),
         in_specs=[vmem for _ in operands] + [pl.BlockSpec(memory_space=pltpu.HBM) for _ in late],
         out_specs=tuple(vmem for _ in outs),
@@ -325,14 +338,15 @@
     head_width = qkv_weight.shape[2]
     model = adapter.shape[1]
     tokens, heads = decay.shape
-    per = tokens // hosts
+    near_hosts = hosts // 2
+    per = tokens // near_hosts
 
     across = frames.T
     copies = call(copy_kernel, (((hosts, share, frame_count), BF16),), across)
     gathered = swap(copies, "head")
     lanes = bc_weight.shape[1] // 2
     half = lax.dynamic_slice_in_dim(bc_weight.T, lax.rem(place, 2) * lanes, lanes, 0)
-    half, other = gather_halves(half, hosts, count)
+    coupler_rows = gather_halves(half, hosts, count)
     turned = jnp.transpose(qkv_weight, (0, 2, 1)).reshape(3 * head_width, features)
     queries, own = call(
         qkv_kernel,
@@ -356,29 +370,31 @@
     attended = swap(attended, "head")
     encoded, parts = call(
         encode_kernel,
-        (((share, frame_count), BF16), ((hosts, per, model), BF16)),
+        (((share, frame_count), BF16), ((near_hosts, per, model), BF16)),
         attended,
         out_weight.T,
         across,
         out_bias[:, None],
         adapter,
     )
-    parts = swap(parts, "head")
-    scaled = call(scale_kernel, (((hosts, per, model), BF16),), parts, rms_gain[None, :])
-    scaled = swap(scaled, "head")
-    scaled = scaled.reshape(tokens, model)
+    parts = swap(parts, "head", [list(range(i, i + near_hosts)) for i in range(0, hosts, near_hosts)])
+    sums = call(add_kernel, (((hosts, per, model), BF16),), parts)
+    sums = swap(sums, "head")
     rows = heads * HDIM // GROUP
-    weights, diagonal, tail, grow, ends = call(
+    written, weights, diagonal, tail, grow, ends = call(
         decay_kernel,
         (
+            ((share, frame_count), BF16),
             ((heads, tokens, tokens), F32),
             ((heads, tokens, tokens), F32),
             ((heads, tokens), F32),
             ((tokens, heads), F32),
             ((8, NSTATE), F32),
         ),
+        encoded,
         decay.T,
         skip_gain[None, :],
+        final=1,
     )
     base, c_rows, ends = call(
         state_kernel,
@@ -387,13 +403,15 @@
             ((tokens, NSTATE), BF16),
             ((GROUP, rows + 8, NSTATE), BF16),
         ),
-        scaled,
+        sums,
+        rms_gain[None, :],
         x_weight.T,
         weights,
         diagonal,
         tail,
         ends,
-        late=(half, other),
+        late=coupler_rows,
+        scratch=(((NSTATE, model), BF16),) * 2,
     )
     near = [[first + k for k in range(GROUP)] for first in range(0, count, GROUP)]
     far = [[lane + GROUP * k for k in range(count // GROUP)] for lane in range(GROUP)]
@@ -416,9 +434,9 @@
         c_rows,
         base,
         grow,
-        final=True,
-    )
-    return (encoded.T, mixed)
+        final=1,
+    )
+    return (written.T, mixed)
 
 
 def solution(mesh):

time: 140 us -> 133 us (0.950)
  blocking collectives: 37.5 us -> 58.4 us
  waiting for transfers between devices: 32.2 us -> 14.7 us
  starting transfers between devices: 49.9 us -> 42.9 us
    all_to_all x5 -> x3, waiting for transfers between devices: 29.1 us -> 7.82 us  [swap(): lax.all_to_all(copies, axis, 0, 0, tiled=True, axis_index_groups=groups)]
    all_to_all x2 -> x4, blocking collectives: 37.5 us -> 58.4 us  [swap(): lax.all_to_all(copies, axis, 0, 0, tiled=True, axis_index_groups=groups)]
    all_to_all x5 -> x3, starting transfers between devices: 23.9 us -> 15 us  [swap(): lax.all_to_all(copies, axis, 0, 0, tiled=True, axis_index_groups=groups)]
    ppermute x6 -> x7, waiting for transfers between devices: 3.08 us -> 6.9 us  [trade(): return lax.ppermute(block, axis, pairs + [(b, a) for a, b in pairs])]
    ppermute x6 -> x7, starting transfers between devices: 26 us -> 27.9 us  [trade(): return lax.ppermute(block, axis, pairs + [(b, a) for a, b in pairs])]
  transfers between devices with their start and end apart: 11 -> 10, of which waited for: 8 -> 6; matrix products, arithmetic and copies ran while one was open for 3% -> 2% of each run, Pallas kernels for 5% -> 4%
where the time goes in v5:
time: 133 us
  blocking collectives  58.4 us (44%)
  starting transfers between devices  42.9 us (32%)
  waiting for transfers between devices  14.7 us (11%)
  Pallas kernels  11.1 us (8%)
  local copies, waits for them, and re-layouts  3.82 us (3%)
    all_to_all x4, blocking collectives, swap(): lax.all_to_all(copies, axis, 0, 0, tiled=True, axis_index_groups=groups)  58.4 us
    ppermute x7, starting transfers between devices, trade(): return lax.ppermute(block, axis, pairs + [(b, a) for a, b in pairs])  27.9 us
    all_to_all x3, starting transfers between devices, swap(): lax.all_to_all(copies, axis, 0, 0, tiled=True, axis_index_groups=groups)  15 us
    pallas_call x10, Pallas kernels, call(): pl.pallas_call(kernel, out_shape=tuple((jax.ShapeDtypeStruct(dims, kind)...  11.1 us
    all_to_all x3, waiting for transfers between devices, swap(): lax.all_to_all(copies, axis, 0, 0, tiled=True, axis_index_groups=groups)  7.82 us
    ppermute x7, waiting for transfers between devices, trade(): return lax.ppermute(block, axis, pairs + [(b, a) for a, b in pairs])  6.9 us
  transfers between devices with their start and end apart: 10, of which 6 were waited for; matrix products, arithmetic and copies ran while one was open for 2% of the time, Pallas kernels for 4%

profile of v5, /device:TPU:1, one launch (start us, length us, event | category | flops | bytes accessed | tf_op | source)
XLA Modules:
  0.0 132.7 jit_solution(13561311734961066417)
XLA Ops:
  0.6 0.0 copy-start
  0.6 0.0 copy-start.4
  0.7 0.9 copy-done.4
  1.6 0.9 shard_map.140
  2.5 7.5 %all-to-all-start = ((bf16[8,160,256]{2,1,0:T(8,128)(2,1)}), bf16[8,160,256]{2,1,0:T(8,128)(2,1)S(1)}, u32[]{:S(2)}, u32[]{:S(2)}) async-start(bf16[8,160,256]{2,1,0:T(8,128)(2,1)} %shard_map.140), calls=%async_computation | async-start | bytes 1310720 | tf_op jit(solution)/shard_map/all_to_all | solution.py:35
  10.0 4.9 %collective-permute-start.2 = (bf16[16,2560]{1,0:T(8,128)(2,1)S(1)}, bf16[16,2560]{1,0:T(8,128)(2,1)S(1)}, u32[]{:S(2)}, u32[]{:S(2)}) collective-permute-start(bf16[16,2560]{1,0:T(8,128)(2,1)S(1)} %dynamic-slice_bitcast_fusion), channel_id=1, source_target_pairs={{0,4},{1,5},{2,6},{3,7},{4,0},{5,1},{6,2},{7,3},{8,12},{9,13},{10,... | collective-permute-start | bytes 245768 | tf_op jit(solution)/shard_map/ppermute | solution.py:39
  14.8 5.0 %collective-permute-done.2 = bf16[16,2560]{1,0:T(8,128)(2,1)S(1)} collective-permute-done((bf16[16,2560]{1,0:T(8,128)(2,1)S(1)}, bf16[16,2560]{1,0:T(8,128)(2,1)S(1)}, u32[]{:S(2)}, u32[]{:S(2)}) %collective-permute-start.2) | collective-permute-done | bytes 81952 | tf_op jit(solution)/shard_map/ppermute | solution.py:39
  19.8 0.7 pad_maximum_fusion.2
  20.5 4.6 %collective-permute-start.3 = (bf16[32,2560]{1,0:T(8,128)(2,1)}, bf16[32,2560]{1,0:T(8,128)(2,1)S(1)}, u32[]{:S(2)}, u32[]{:S(2)}) collective-permute-start(bf16[32,2560]{1,0:T(8,128)(2,1)} %pad_maximum_fusion.2), channel_id=1, source_target_pairs={{0,2},{1,3},{4,6},{5,7},{2,0},{3,1},{6,4},{7,5},{8,10},{9,11},{12,... | collective-permute-start | bytes 491528 | tf_op jit(solution)/shard_map/ppermute | solution.py:39
  25.1 0.2 broadcast_in_dim.20.gain_ref
  25.3 0.2 broadcast_in_dim.21.bias_ref
  25.6 1.6 %copy.16 = bf16[3,128,1280]{2,1,0:T(8,128)(2,1)S(1)} copy(bf16[3,128,1280]{1,2,0:T(8,128)(2,1)} %bitcast.18) | data formatting | bytes 1966080 | tf_op jit(solution)/shard_map/transpose | solution.py:350
  27.2 0.0 all-to-all-done.x_ref
  27.2 0.0 copy-start.14
  27.2 1.0 shard_map.141
  28.2 0.0 copy-start.12
  28.2 0.0 copy-start.18
  28.2 0.0 copy-start.2
  28.2 0.0 copy-start.3
  28.2 0.0 copy-start.5
  28.2 7.5 %collective-permute-start = (bf16[256,256]{1,0:T(8,128)(2,1)S(1)}, bf16[256,256]{1,0:T(8,128)(2,1)S(1)}, u32[]{:S(2)}, u32[]{:S(2)}) collective-permute-start(bf16[256,256]{1,0:T(8,128)(2,1)S(1)} %get-tuple-element.16.own_ref), channel_id=1, source_target_pairs={{8,16},{24,32},{40,48},{56,64},{72,80},{88,96},{104,112},{120,128}... | collective-permute-start | bytes 393224 | tf_op jit(solution)/shard_map/ppermute | solution.py:39
  35.8 1.9 %collective-permute-start.1 = (bf16[256,256]{1,0:T(8,128)(2,1)S(1)}, bf16[256,256]{1,0:T(8,128)(2,1)S(1)}, u32[]{:S(2)}, u32[]{:S(2)}) collective-permute-start(bf16[256,256]{1,0:T(8,128)(2,1)S(1)} %get-tuple-element.16.own_ref), channel_id=1, source_target_pairs={{0,8},{16,24},{32,40},{48,56},{64,72},{80,88},{96,104},{112,120},{... | collective-permute-start | bytes 393224 | tf_op jit(solution)/shard_map/ppermute | solution.py:39
  37.8 0.7 collective-permute-done.chip_ref
  38.4 0.6 collective-permute-done.1.core_ref
  39.0 1.9 %shard_map.142 = bf16[8,128,256]{2,1,0:T(8,128)(2,1)} custom-call(bf16[128,256]{1,0:T(8,128)(2,1)S(1)} %get-tuple-element.15.q_ref, bf16[256,256]{1,0:T(8,128)(2,1)S(1)} %get-tuple-element.16.own_ref, bf16[256,256]{1,0:T(8,128)(2,1)S(1)} %collective-permute-done.chip_ref, bf16[256,256]{1,0:T(8,128)(2,1)S(1)} %collective-permute-done.1.core_ref, ...), custom_call_target="tpu_custom_call" | custom-call | tf_op jit(solution)/shard_map/pallas_call | solution.py:302
  41.0 3.5 %all-to-all-start.1 = ((bf16[8,128,256]{2,1,0:T(8,128)(2,1)}), bf16[8,128,256]{2,1,0:T(8,128)(2,1)S(1)}, u32[]{:S(2)}, u32[]{:S(2)}) async-start(bf16[8,128,256]{2,1,0:T(8,128)(2,1)} %shard_map.142), calls=%async_computation.1 | async-start | bytes 1048576 | tf_op jit(solution)/shard_map/all_to_all | solution.py:35
  44.5 0.0 collective-permute-done.3
  44.5 3.3 %collective-permute-start.4 = (bf16[64,2560]{1,0:T(8,128)(2,1)S(1)}, bf16[64,2560]{1,0:T(8,128)(2,1)S(1)}, u32[]{:S(2)}, u32[]{:S(2)}) collective-permute-start(bf16[64,2560]{1,0:T(8,128)(2,1)S(1)} %pad_maximum_fusion.1.rows_ref), channel_id=1, source_target_pairs={{0,1},{2,3},{4,5},{6,7},{1,0},{3,2},{5,4},{7,6},{8,9},{10,11},{12,... | collective-permute-start | bytes 983048 | tf_op jit(solution)/shard_map/ppermute | solution.py:39
  47.8 0.1 copy.19.bias_ref
  47.9 6.6 %all-to-all-done.1.att_ref = bf16[8,128,256]{2,1,0:T(8,128)(2,1)S(1)} async-done(((bf16[8,128,256]{2,1,0:T(8,128)(2,1)}), bf16[8,128,256]{2,1,0:T(8,128)(2,1)S(1)}, u32[]{:S(2)}, u32[]{:S(2)}) %all-to-all-start.1) | async-done | bytes 524320 | tf_op jit(solution)/shard_map/all_to_all | solution.py:35
  54.5 0.7 shard_map.143
  55.3 8.9 %all_to_all.35.part_ref = bf16[4,16,2560]{2,1,0:T(8,128)(2,1)S(1)} all-to-all(bf16[4,16,2560]{2,1,0:T(8,128)(2,1)S(1)} %get-tuple-element.19), channel_id=1, replica_groups={{0,1,2,3},{4,5,6,7},{8,9,10,11},{12,13,14,15},{16,17,18,19},{20,21,22,2..., dimensions={0} | all-to-all | bytes 655360 | tf_op jit(solution)/shard_map/all_to_all | solution.py:35
  64.2 0.9 shard_map.145
  65.1 4.1 %all-to-all-start.3 = ((bf16[8,16,2560]{2,1,0:T(8,128)(2,1)}), bf16[8,16,2560]{2,1,0:T(8,128)(2,1)S(1)}, u32[]{:S(2)}, u32[]{:S(2)}) async-start(bf16[8,16,2560]{2,1,0:T(8,128)(2,1)} %shard_map.145), calls=%async_computation.3 | async-start | bytes 1310720 | tf_op jit(solution)/shard_map/all_to_all | solution.py:35
  69.2 0.0 collective-permute-done.4.third_ref
  69.3 3.8 %collective-permute-start.6 = (bf16[96,2560]{1,0:T(8,128)(2,1)S(1)}, bf16[96,2560]{1,0:T(8,128)(2,1)S(1)}, u32[]{:S(2)}, u32[]{:S(2)}) collective-permute-start(bf16[96,2560]{1,0:T(8,128)(2,1)S(1)} %pad_maximum_fusion), channel_id=1, source_target_pairs={{0,8},{16,24},{32,40},{48,56},{64,72},{80,88},{96,104},{112,120},{... | collective-permute-start | bytes 1474568 | tf_op jit(solution)/shard_map/ppermute | solution.py:39
  73.1 1.9 %collective-permute-start.5 = (bf16[32,2560]{1,0:T(8,128)(2,1)}, bf16[32,2560]{1,0:T(8,128)(2,1)S(1)}, u32[]{:S(2)}, u32[]{:S(2)}) collective-permute-start(bf16[32,2560]{1,0:T(8,128)(2,1)} %pad_maximum_fusion.2), channel_id=1, source_target_pairs={{0,8},{16,24},{32,40},{48,56},{64,72},{80,88},{96,104},{112,120},{... | collective-permute-start | bytes 491528 | tf_op jit(solution)/shard_map/ppermute | solution.py:39
  75.1 0.9 shard_map.144
  76.0 0.6 collective-permute-done.5.near_ref
  76.6 0.7 copy-done.13
  77.3 1.2 all-to-all-done.3.sums_ref
  78.5 3.6 %shard_map.146 = (f32[64,320]{1,0:T(8,128)S(1)}, bf16[64,128]{1,0:T(8,128)(2,1)S(1)}, bf16[8,48,128]{2,1,0:T(8,128)(2,1)S(1)}) custom-call(bf16[8,16,2560]{2,1,0:T(8,128)(2,1)S(1)} %all-to-all-done.3.sums_ref, f32[1,2560]{1,0:T(1,128)S(1)} %broadcast_in_dim.19.gain_ref, bf16[320,2560]{1,0:T(8,128)(2,1)S(1)} %bitcast.12, ...), custom_call_target="tpu_custom_call" | custom-call | tf_op jit(solution)/shard_map/pallas_call | solution.py:302
  82.1 16.4 %all_to_all.36.got_ref = bf16[8,48,128]{2,1,0:T(8,128)(2,1)S(1)} all-to-all(bf16[8,48,128]{2,1,0:T(8,128)(2,1)S(1)} %get-tuple-element.24), channel_id=1, replica_groups={{0,8,16,24,32,40,48,56},{64,72,80,88,96,104,112,120},{128,136,144,152,1..., dimensions={0} | all-to-all | bytes 196608 | tf_op jit(solution)/shard_map/all_to_all | solution.py:35
  98.4 0.2 shard_map.147
  98.6 22.2 %all_to_all.37.total_ref = bf16[8,48,128]{2,1,0:T(8,128)(2,1)S(1)} all-to-all(bf16[8,48,128]{2,1,0:T(8,128)(2,1)S(1)} %shard_map.147), channel_id=1, replica_groups={{0,64,128,192,256,320,384,448},{8,72,136,200,264,328,392,456},{16,80,14..., dimensions={0} | all-to-all | bytes 196608 | tf_op jit(solution)/shard_map/all_to_all | solution.py:35
  120.8 0.2 shard_map.148
  121.0 10.9 %all_to_all.38.state_ref = bf16[8,40,128]{2,1,0:T(8,128)(2,1)S(1)} all-to-all(bf16[8,40,128]{2,1,0:T(8,128)(2,1)S(1)} %shard_map.148), channel_id=1, replica_groups={{0,8,16,24,32,40,48,56},{64,72,80,88,96,104,112,120},{128,136,144,152,1..., dimensions={0} | all-to-all | bytes 163840 | tf_op jit(solution)/shard_map/all_to_all | solution.py:35
  132.0 0.8 shard_map.149
  (35 shorter events, 0.2 us)
Async XLA Ops:
  0.6 9.3 %copy-start = (bf16[2560,32]{0,1:T(8,128)(2,1)S(1)}, bf16[2560,32]{0,1:T(8,128)(2,1)}, u32[]{:S(2)}) copy-start(bf16[2560,32]{0,1:T(8,128)(2,1)} %param.23) | copy-start | bytes 491524
  0.6 0.9 copy-start.4
  1.6 23.5 %copy-start.16 = (f32[1280]{0:T(1024)S(1)}, f32[1280]{0:T(1024)}, u32[]{:S(2)}) copy-start(f32[1280]{0:T(1024)} %param.15) | copy-start | bytes 15364
  1.6 23.8 %copy-start.17 = (f32[1280]{0:T(1024)S(1)}, f32[1280]{0:T(1024)}, u32[]{:S(2)}) copy-start(f32[1280]{0:T(1024)} %param.16) | copy-start | bytes 15364
  2.5 24.7 %all-to-all-start = ((bf16[8,160,256]{2,1,0:T(8,128)(2,1)}), bf16[8,160,256]{2,1,0:T(8,128)(2,1)S(1)}, u32[]{:S(2)}, u32[]{:S(2)}) async-start(bf16[8,160,256]{2,1,0:T(8,128)(2,1)} %shard_map.140), calls=%async_computation | async-start | bytes 1310720 | tf_op jit(solution)/shard_map/all_to_all | solution.py:35
  10.0 9.9 %collective-permute-start.2 = (bf16[16,2560]{1,0:T(8,128)(2,1)S(1)}, bf16[16,2560]{1,0:T(8,128)(2,1)S(1)}, u32[]{:S(2)}, u32[]{:S(2)}) collective-permute-start(bf16[16,2560]{1,0:T(8,128)(2,1)S(1)} %dynamic-slice_bitcast_fusion), channel_id=1, source_target_pairs={{0,4},{1,5},{2,6},{3,7},{4,0},{5,1},{6,2},{7,3},{8,12},{9,13},{10,... | collective-permute-start | bytes 245768 | tf_op jit(solution)/shard_map/ppermute | solution.py:39
  19.8 5.7 %copy-start.11 = (bf16[16,2560]{1,0:T(8,128)(2,1)}, bf16[16,2560]{1,0:T(8,128)(2,1)S(1)}, u32[]{:S(2)}) copy-start(bf16[16,2560]{1,0:T(8,128)(2,1)S(1)} %collective-permute-done.2) | copy-start | bytes 245764
  20.5 23.9 %collective-permute-start.3 = (bf16[32,2560]{1,0:T(8,128)(2,1)}, bf16[32,2560]{1,0:T(8,128)(2,1)S(1)}, u32[]{:S(2)}, u32[]{:S(2)}) collective-permute-start(bf16[32,2560]{1,0:T(8,128)(2,1)} %pad_maximum_fusion.2), channel_id=1, source_target_pairs={{0,2},{1,3},{4,6},{5,7},{2,0},{3,1},{6,4},{7,5},{8,10},{9,11},{12,... | collective-permute-start | bytes 491528 | tf_op jit(solution)/shard_map/ppermute | solution.py:39
  27.2 10.6 %copy-start.14 = (s32[16384]{0:T(1024)S(1)}, s32[16384]{0:T(1024)}, u32[]{:S(2)}) copy-start(s32[16384]{0:T(1024)} %param.14) | copy-start | bytes 196612
  28.2 16.3 %copy-start.12 = (bf16[16,2560]{1,0:T(8,128)(2,1)S(1)}, bf16[16,2560]{1,0:T(8,128)(2,1)}, u32[]{:S(2)}) copy-start(bf16[16,2560]{1,0:T(8,128)(2,1)} %copy-done.11) | copy-start | bytes 245764
  28.2 19.6 %copy-start.18 = (f32[160]{0:T(256)S(1)}, f32[160]{0:T(256)}, u32[]{:S(2)}) copy-start(f32[160]{0:T(256)} %param.19) | copy-start | bytes 1924
  28.2 26.3 %copy-start.2 = (bf16[160,2560]{1,0:T(8,128)(2,1)S(1)}, bf16[160,2560]{1,0:T(8,128)(2,1)}, u32[]{:S(2)}) copy-start(bf16[160,2560]{1,0:T(8,128)(2,1)} %adapter_ref.1) | copy-start | bytes 2457604
  28.2 26.3 %copy-start.3 = (bf16[1024,160]{0,1:T(8,128)(2,1)S(1)}, bf16[1024,160]{0,1:T(8,128)(2,1)}, u32[]{:S(2)}) copy-start(bf16[1024,160]{0,1:T(8,128)(2,1)} %param.18) | copy-start | bytes 983044
  28.2 26.3 %copy-start.5 = (bf16[256,160]{0,1:T(8,128)(2,1)S(1)}, bf16[256,160]{0,1:T(8,128)(2,1)}, u32[]{:S(2)}) copy-start(bf16[256,160]{0,1:T(8,128)(2,1)} %param.13) | copy-start | bytes 245764
  28.2 10.2 %collective-permute-start = (bf16[256,256]{1,0:T(8,128)(2,1)S(1)}, bf16[256,256]{1,0:T(8,128)(2,1)S(1)}, u32[]{:S(2)}, u32[]{:S(2)}) collective-permute-start(bf16[256,256]{1,0:T(8,128)(2,1)S(1)} %get-tuple-element.16.own_ref), channel_id=1, source_target_pairs={{8,16},{24,32},{40,48},{56,64},{72,80},{88,96},{104,112},{120,128}... | collective-permute-start | bytes 393224 | tf_op jit(solution)/shard_map/ppermute | solution.py:39
  35.8 3.2 %collective-permute-start.1 = (bf16[256,256]{1,0:T(8,128)(2,1)S(1)}, bf16[256,256]{1,0:T(8,128)(2,1)S(1)}, u32[]{:S(2)}, u32[]{:S(2)}) collective-permute-start(bf16[256,256]{1,0:T(8,128)(2,1)S(1)} %get-tuple-element.16.own_ref), channel_id=1, source_target_pairs={{0,8},{16,24},{32,40},{48,56},{64,72},{80,88},{96,104},{112,120},{... | collective-permute-start | bytes 393224 | tf_op jit(solution)/shard_map/ppermute | solution.py:39
  41.0 13.6 %all-to-all-start.1 = ((bf16[8,128,256]{2,1,0:T(8,128)(2,1)}), bf16[8,128,256]{2,1,0:T(8,128)(2,1)S(1)}, u32[]{:S(2)}, u32[]{:S(2)}) async-start(bf16[8,128,256]{2,1,0:T(8,128)(2,1)} %shard_map.142), calls=%async_computation.1 | async-start | bytes 1048576 | tf_op jit(solution)/shard_map/all_to_all | solution.py:35
  44.5 20.6 %copy-start.8 = (bf16[64,2560]{1,0:T(8,128)(2,1)}, bf16[64,2560]{1,0:T(8,128)(2,1)S(1)}, u32[]{:S(2)}) copy-start(bf16[64,2560]{1,0:T(8,128)(2,1)S(1)} %pad_maximum_fusion.1.rows_ref) | copy-start | bytes 983044
  44.5 24.7 %collective-permute-start.4 = (bf16[64,2560]{1,0:T(8,128)(2,1)S(1)}, bf16[64,2560]{1,0:T(8,128)(2,1)S(1)}, u32[]{:S(2)}, u32[]{:S(2)}) collective-permute-start(bf16[64,2560]{1,0:T(8,128)(2,1)S(1)} %pad_maximum_fusion.1.rows_ref), channel_id=1, source_target_pairs={{0,1},{2,3},{4,5},{6,7},{1,0},{3,2},{5,4},{7,6},{8,9},{10,11},{12,... | collective-permute-start | bytes 983048 | tf_op jit(solution)/shard_map/ppermute | solution.py:39
  64.2 10.8 %copy-start.15 = (f32[2560]{0:T(1024)S(1)}, f32[2560]{0:T(1024)}, u32[]{:S(2)}) copy-start(f32[2560]{0:T(1024)} %param.21) | copy-start | bytes 30724
  64.2 10.8 %copy-start.6 = (f32[64,5]{0,1:T(8,128)S(1)}, f32[64,5]{0,1:T(8,128)}, u32[]{:S(2)}) copy-start(f32[64,5]{0,1:T(8,128)} %param.24) | copy-start | bytes 3844
  64.2 10.9 %copy-start.7 = (f32[5]{0:T(128)S(1)}, f32[5]{0:T(128)}, u32[]{:S(2)}) copy-start(f32[5]{0:T(128)} %param.25) | copy-start | bytes 64
  64.2 14.3 %copy-start.1 = (bf16[2560,320]{0,1:T(8,128)(2,1)S(1)}, bf16[2560,320]{0,1:T(8,128)(2,1)}, u32[]{:S(2)}) copy-start(bf16[2560,320]{0,1:T(8,128)(2,1)} %param.22) | copy-start | bytes 4915204
  65.1 13.4 %all-to-all-start.3 = ((bf16[8,16,2560]{2,1,0:T(8,128)(2,1)}), bf16[8,16,2560]{2,1,0:T(8,128)(2,1)S(1)}, u32[]{:S(2)}, u32[]{:S(2)}) async-start(bf16[8,16,2560]{2,1,0:T(8,128)(2,1)} %shard_map.145), calls=%async_computation.3 | async-start | bytes 1310720 | tf_op jit(solution)/shard_map/all_to_all | solution.py:35
  69.2 5.8 %copy-start.9 = (bf16[64,2560]{1,0:T(8,128)(2,1)}, bf16[64,2560]{1,0:T(8,128)(2,1)S(1)}, u32[]{:S(2)}) copy-start(bf16[64,2560]{1,0:T(8,128)(2,1)S(1)} %collective-permute-done.4.third_ref) | copy-start | bytes 983044
  69.3 8.0 %collective-permute-start.6 = (bf16[96,2560]{1,0:T(8,128)(2,1)S(1)}, bf16[96,2560]{1,0:T(8,128)(2,1)S(1)}, u32[]{:S(2)}, u32[]{:S(2)}) collective-permute-start(bf16[96,2560]{1,0:T(8,128)(2,1)S(1)} %pad_maximum_fusion), channel_id=1, source_target_pairs={{0,8},{16,24},{32,40},{48,56},{64,72},{80,88},{96,104},{112,120},{... | collective-permute-start | bytes 1474568 | tf_op jit(solution)/shard_map/ppermute | solution.py:39
  73.1 3.5 %collective-permute-start.5 = (bf16[32,2560]{1,0:T(8,128)(2,1)}, bf16[32,2560]{1,0:T(8,128)(2,1)S(1)}, u32[]{:S(2)}, u32[]{:S(2)}) collective-permute-start(bf16[32,2560]{1,0:T(8,128)(2,1)} %pad_maximum_fusion.2), channel_id=1, source_target_pairs={{0,8},{16,24},{32,40},{48,56},{64,72},{80,88},{96,104},{112,120},{... | collective-permute-start | bytes 491528 | tf_op jit(solution)/shard_map/ppermute | solution.py:39
  76.6 0.7 copy-start.13
  77.2 1.2 copy-start.10
